TPU v7x, 32 devices: a whole 2x2x4 slice. The times are simulated.
32 devices in a mesh: ctx: 16 (over z, y, core), head: 2 (over x).
Axes of the slice: x: 2, y: 2, z: 4, core: 2. Of those that a mesh axis runs over, the one named last changes fastest.
Arguments:
- queries: bfloat16 [8192, 8, 4, 128], P('ctx', None, 'head'), may hold values from -6 to 6
- key_heads: bfloat16 [8192, 8, 128], P('ctx'), may hold values from -6 to 6
- value_heads: bfloat16 [8192, 8, 128], P('ctx'), may hold values from -6 to 6
- out_grad: bfloat16 [8192, 8, 4, 128], P('ctx', None, 'head'), may hold values from -6 to 6
- doc_ids: int32 [8192], P('ctx'), may hold values from 0 to 31, never falling along the last dimension, each value on 1 to 2048 neighbouring positions
Outputs:
- query_grad: bfloat16 [8192, 8, 4, 128], P('ctx', None, 'head')
- key_grad: bfloat16 [8192, 8, 128], P('ctx', 'head')
- value_grad: bfloat16 [8192, 8, 128], P('ctx', 'head')
Inputs may be any that keep to these rules, and one draw needn't show every extreme that they name: `doc_ids`: ids never fall along the sequence; a document has at most 2048 tokens.
All inputs are finite; a program needn't handle non-finite values.
Results may differ from a plain program's by a relative error of at most 0.012.
Values may be sent and summed in bfloat16 or wider, within the bound.
No kernel may reach another device: no remote copies, remote signals or barrier semaphores. Data moves between devices by JAX's collectives and lax.ppermute only.
A program may use at most 64 MiB of HBM per device.

v0:
```python
import jax
import jax.numpy as jnp
from jax import lax
from jax.sharding import PartitionSpec as P

WINDOW = 256


def from_behind(block, axis, distance):
    devices = range(lax.axis_size(axis))
    route = [(i - distance, i) for i in devices if i - distance in devices]
    return lax.ppermute(block, axis, route)


def head_grads(query_n, key_n, value_n, grad_n, visible):
    scaling = 1.0 / query_n.shape[-1] ** 0.5
    scores = jnp.einsum("lgd,md->glm", query_n, key_n, preferred_element_type=jnp.float32) * scaling
    scores = jnp.where(visible[None], scores, -jnp.inf)
    top_score = jnp.max(scores, axis=-1, keepdims=True)
    weights = jnp.exp(scores - top_score)
    attn_prob = weights / jnp.sum(weights, axis=-1, keepdims=True)
    prob_low = attn_prob.astype(jnp.bfloat16)
    attended = jnp.einsum("glm,md->lgd", prob_low, value_n, preferred_element_type=jnp.float32)
    row_delta = jnp.sum(grad_n.astype(jnp.float32) * attended, axis=-1)
    grad_prob = jnp.einsum("lgd,md->glm", grad_n, value_n, preferred_element_type=jnp.float32)
    grad_low = (attn_prob * (grad_prob - jnp.transpose(row_delta)[:, :, None])).astype(jnp.bfloat16)
    query_part = (
        jnp.einsum("glm,md->lgd", grad_low, key_n, preferred_element_type=jnp.float32) * scaling
    ).astype(jnp.bfloat16)
    key_part = (
        jnp.einsum("glm,lgd->md", grad_low, query_n, preferred_element_type=jnp.float32) * scaling
    )
    value_part = jnp.einsum("glm,lgd->md", prob_low, grad_n, preferred_element_type=jnp.float32)
    return (query_part, key_part, value_part)


def visibility(doc_ids, prev_docs, block_rows, reach):
    anchor = lax.axis_index("ctx") * block_rows
    doc_key = jnp.concatenate([prev_docs, doc_ids], 0)
    pos_query = anchor + jnp.arange(block_rows, dtype=jnp.int32)
    pos_key = anchor - reach + jnp.arange(block_rows + reach, dtype=jnp.int32)
    lag_rows = pos_query[:, None] - pos_key[None, :]
    return (
        (lag_rows >= 0)
        & (lag_rows < reach)
        & (doc_ids[:, None] == doc_key[None, :])
        & (pos_key[None, :] >= 0)
    )


def run_heads(queries, out_grad, key_win, value_win, visible):
    window_rows = key_win.shape[0]
    kv_count = key_win.shape[1]
    head_size = key_win.shape[2]

    def head_step(kv_head, loop_state):
        query_acc, key_acc, value_acc = loop_state
        query_n = lax.dynamic_index_in_dim(queries, kv_head, 1, keepdims=False)
        grad_n = lax.dynamic_index_in_dim(out_grad, kv_head, 1, keepdims=False)
        key_n = lax.dynamic_index_in_dim(key_win, kv_head, 1, keepdims=False)
        value_n = lax.dynamic_index_in_dim(value_win, kv_head, 1, keepdims=False)
        query_part, key_part, value_part = head_grads(query_n, key_n, value_n, grad_n, visible)
        query_acc = lax.dynamic_update_index_in_dim(query_acc, query_part, kv_head, 1)
        key_acc = lax.dynamic_update_index_in_dim(key_acc, key_part, kv_head, 1)
        value_acc = lax.dynamic_update_index_in_dim(value_acc, value_part, kv_head, 1)
        return (query_acc, key_acc, value_acc)

    initial = (
        jnp.zeros_like(queries),
        jnp.zeros((window_rows, kv_count, head_size), jnp.float32),
        jnp.zeros((window_rows, kv_count, head_size), jnp.float32),
    )
    return lax.fori_loop(0, kv_count, head_step, initial)


def on_device(queries, key_heads, value_heads, out_grad, doc_ids):
    block_rows = queries.shape[0]
    kv_count = key_heads.shape[1]
    reach = WINDOW
    tail_docs = doc_ids[block_rows - reach :]
    half_heads = kv_count // lax.axis_size("head")
    first_head = lax.axis_index("head") * half_heads
    group_queries, group_grads = (
        lax.all_to_all(queries, "head", split_axis=1, concat_axis=2, tiled=True),
        lax.all_to_all(out_grad, "head", split_axis=1, concat_axis=2, tiled=True),
    )
    own_keys = lax.dynamic_slice_in_dim(key_heads, first_head, half_heads, 1)
    own_values = lax.dynamic_slice_in_dim(value_heads, first_head, half_heads, 1)
    prev_keys, prev_values, prev_docs = from_behind(
        (own_keys[block_rows - reach :], own_values[block_rows - reach :], tail_docs), "ctx", 1
    )
    key_win = jnp.concatenate([prev_keys, own_keys], 0)
    value_win = jnp.concatenate([prev_values, own_values], 0)
    visible = visibility(doc_ids, prev_docs, block_rows, reach)
    group_qgrad, key_acc, value_acc = run_heads(
        group_queries, group_grads, key_win, value_win, visible
    )
    back_keys, back_values = from_behind((key_acc[:reach], value_acc[:reach]), "ctx", -1)
    key_grad = key_acc[reach:].at[block_rows - reach :].add(back_keys)
    value_grad = value_acc[reach:].at[block_rows - reach :].add(back_values)
    query_grad = lax.all_to_all(group_qgrad, "head", split_axis=2, concat_axis=1, tiled=True)
    return (query_grad, key_grad.astype(jnp.bfloat16), value_grad.astype(jnp.bfloat16))


def solution(mesh):
    in_specs = (
        P("ctx", None, "head", None),
        P("ctx", None, None),
        P("ctx", None, None),
        P("ctx", None, "head", None),
        P("ctx"),
    )
    out_specs = (P("ctx", None, "head", None), P("ctx", "head", None), P("ctx", "head", None))
    return jax.shard_map(
        on_device, mesh=mesh, in_specs=in_specs, out_specs=out_specs, check_vma=False
    )
```

profile of v0, /device:TPU:1, one launch (start us, length us, event | category | flops | bytes accessed | tf_op | source)
XLA Modules:
  0.0 273.9 jit_solution(13850583160561415136)
XLA Ops:
  0.6 4.3 %copy.30 = bf16[512,8,2,128]{3,2,0,1:T(2,128)(2,1)} copy(bf16[512,8,2,128]{3,2,1,0:T(2,128)(2,1)} %param.11) | data formatting | bytes 4194304 | tf_op args[0]
  5.0 3.8 %all-to-all-start = ((bf16[512,8,2,128]{3,2,0,1:T(2,128)(2,1)}), bf16[512,8,2,128]{3,2,0,1:T(2,128)(2,1)S(1)}, u32[]{:S(2)}, u32[]{:S(2)}) async-start(bf16[512,8,2,128]{3,2,0,1:T(2,128)(2,1)} %copy.30), calls=%async_computation | async-start | bytes 4194304 | tf_op jit(solution)/shard_map/all_to_all | solution.py:84
  8.8 4.4 %copy.33 = bf16[512,8,2,128]{3,2,0,1:T(2,128)(2,1)} copy(bf16[512,8,2,128]{3,2,1,0:T(2,128)(2,1)} %param.14) | data formatting | bytes 4194304 | tf_op args[3]
  13.1 20.7 %all-to-all-done = bf16[512,8,2,128]{3,2,0,1:T(2,128)(2,1)S(1)} async-done(((bf16[512,8,2,128]{3,2,0,1:T(2,128)(2,1)}), bf16[512,8,2,128]{3,2,0,1:T(2,128)(2,1)S(1)}, u32[]{:S(2)}, u32[]{:S(2)}) %all-to-all-start) | async-done | bytes 2097184 | tf_op jit(solution)/shard_map/all_to_all | solution.py:84
  33.8 4.8 %all-to-all-start.1 = ((bf16[512,8,2,128]{3,2,0,1:T(2,128)(2,1)}), bf16[512,8,2,128]{3,2,0,1:T(2,128)(2,1)}, u32[]{:S(2)}, u32[]{:S(2)}) async-start(bf16[512,8,2,128]{3,2,0,1:T(2,128)(2,1)} %copy.33), calls=%async_computation.1 | async-start | bytes 4194304 | tf_op jit(solution)/shard_map/all_to_all | solution.py:85
  38.7 4.5 %collective-permute-start.1 = (s32[256]{0:T(256)S(1)}, s32[256]{0:T(256)S(1)}, u32[]{:S(2)}, u32[]{:S(2)}) collective-permute-start(s32[256]{0:T(256)S(1)} %slice.72), channel_id=1, source_target_pairs={{0,2},{2,4},{4,6},{6,8},{8,10},{10,12},{12,14},{14,16},{16,18},{18... | collective-permute-start | bytes 3080 | tf_op jit(solution)/shard_map/ppermute | solution.py:12
  43.2 1.8 constant_dynamic-slice_fusion
  45.1 1.9 collective-permute-start.2
  47.8 3.7 %collective-permute-start = (bf16[256,4,128]{2,0,1:T(8,128)(2,1)}, bf16[256,4,128]{2,0,1:T(8,128)(2,1)}, u32[]{:S(2)}, u32[]{:S(2)}) collective-permute-start(bf16[256,4,128]{2,0,1:T(8,128)(2,1)} %slice.80), channel_id=1, source_target_pairs={{0,2},{2,4},{4,6},{6,8},{8,10},{10,12},{12,14},{14,16},{16,18},{18... | collective-permute-start | bytes 786440 | tf_op jit(solution)/shard_map/ppermute | solution.py:12
  51.7 1.9 pad_maximum_fusion.1
  53.5 1.4 collective-permute-done
  55.0 1.9 pad_maximum_fusion
  56.9 1.8 copy.31
  58.7 3.7 %all-to-all-done.1 = bf16[512,8,2,128]{3,2,0,1:T(2,128)(2,1)} async-done(((bf16[512,8,2,128]{3,2,0,1:T(2,128)(2,1)}), bf16[512,8,2,128]{3,2,0,1:T(2,128)(2,1)}, u32[]{:S(2)}, u32[]{:S(2)}) %all-to-all-start.1) | async-done | bytes 2097184 | tf_op jit(solution)/shard_map/all_to_all | solution.py:85
  62.4 2.0 copy.34
  64.4 171.7 %while.20 = (s32[]{:T(128)}, bf16[512,4,4,128]{0,3,1,2:T(8,128)(2,1)}, f32[768,4,128]{2,1,0:T(4,128)}, f32[768,4,128]{2,1,0:T(4,128)}, bf16[768,4,128]{2,0,1:T(8...) while((s32[]{:T(128)}, ...), condition=%wide.region_4.5_spmd.clone, body=%wide.region_0.4_spmd.clone.sunk | while | flops 2435808000 | bytes 70048704 | solution.py:73
  64.4 0.8 fusion.109
  65.3 6.2 %fusion.110 = (f32[4,512]{1,0:T(4,128)S(1)}, f32[4,512,768]{1,2,0:T(8,128)}) fusion(pred[512,768]{0,1:T(8,128)(4,1)S(1)} %fusion.109, bf16[512,4,4,128]{3,0,2,1:T(8,128)(2,1)} %get-tuple-element.367, s32[]{:T(128)S(6)} %copy.65, bf16[768,4,128]{2,0,1:T(8,128)(2,1)} %get-tuple-element.366), kind=kOutput, calls=%fused_computation.69.clone.1 | convolution fusion | flops 408945408 | bytes 7414784 | tf_op jit(solution)/shard_map/while/body/eval_jaxpr/sub | solution.py:20
  71.4 3.7 %fusion.111 = bf16[4,512,768]{1,2,0:T(8,128)(2,1)S(1)} fusion(f32[4,512,768]{1,2,0:T(8,128)} %get-tuple-element.330, f32[4,512]{1,0:T(4,128)S(1)} %get-tuple-element.331), kind=kLoop, calls=%fused_computation.12.clone.1 | loop fusion | flops 3145728 | bytes 9445376 | tf_op jit(solution)/shard_map/while/body/eval_jaxpr/convert_element_type | solution.py:22
  75.1 2.7 fusion.112
  77.8 1.0 fusion.116
  78.8 1.9 fusion.113
  80.8 2.0 fusion.115
  82.8 2.3 fusion.114
  85.1 11.1 %dynamic_update_slice.31 = f32[768,4,128]{2,1,0:T(4,128)} dynamic-update-slice(f32[768,4,128]{2,1,0:T(4,128)} %get-tuple-element.349, f32[768,1,128]{2,1,0:T(1,128)S(1)} %bitcast.147, s32[]{:T(128)} %constant.126.clone.1..sunk, s32[]{:T(128)S(6)} %copy.65, s32[]{:T(128)} %constant.126.clone.1..sunk) | dynamic-update-slice | bytes 786436 | tf_op jit(solution)/shard_map/while/body/eval_jaxpr/jit(dynamic_update_index_in_dim)/dynamic_update_slice | solution.py:64
  96.3 11.1 %dynamic_update_slice.32 = f32[768,4,128]{2,1,0:T(4,128)} dynamic-update-slice(f32[768,4,128]{2,1,0:T(4,128)} %get-tuple-element.350, f32[768,1,128]{2,1,0:T(1,128)S(1)} %bitcast.146, s32[]{:T(128)} %constant.126.clone.1..sunk, s32[]{:T(128)S(6)} %copy.65, s32[]{:T(128)} %constant.126.clone.1..sunk) | dynamic-update-slice | bytes 786436 | tf_op jit(solution)/shard_map/while/body/eval_jaxpr/jit(dynamic_update_index_in_dim)/dynamic_update_slice | solution.py:65
  107.4 0.8 fusion.109
  108.2 6.1 %fusion.110 = (f32[4,512]{1,0:T(4,128)S(1)}, f32[4,512,768]{1,2,0:T(8,128)}) fusion(pred[512,768]{0,1:T(8,128)(4,1)S(1)} %fusion.109, bf16[512,4,4,128]{3,0,2,1:T(8,128)(2,1)} %get-tuple-element.367, s32[]{:T(128)S(6)} %copy.65, bf16[768,4,128]{2,0,1:T(8,128)(2,1)} %get-tuple-element.366), kind=kOutput, calls=%fused_computation.69.clone.1 | convolution fusion | flops 408945408 | bytes 7414784 | tf_op jit(solution)/shard_map/while/body/eval_jaxpr/sub | solution.py:20
  114.3 3.7 %fusion.111 = bf16[4,512,768]{1,2,0:T(8,128)(2,1)S(1)} fusion(f32[4,512,768]{1,2,0:T(8,128)} %get-tuple-element.330, f32[4,512]{1,0:T(4,128)S(1)} %get-tuple-element.331), kind=kLoop, calls=%fused_computation.12.clone.1 | loop fusion | flops 3145728 | bytes 9445376 | tf_op jit(solution)/shard_map/while/body/eval_jaxpr/convert_element_type | solution.py:22
  118.0 2.7 fusion.112
  120.7 1.0 fusion.116
  121.7 1.9 fusion.113
  123.7 2.0 fusion.115
  125.7 2.3 fusion.114
  128.0 11.1 %dynamic_update_slice.31 = f32[768,4,128]{2,1,0:T(4,128)} dynamic-update-slice(f32[768,4,128]{2,1,0:T(4,128)} %get-tuple-element.349, f32[768,1,128]{2,1,0:T(1,128)S(1)} %bitcast.147, s32[]{:T(128)} %constant.126.clone.1..sunk, s32[]{:T(128)S(6)} %copy.65, s32[]{:T(128)} %constant.126.clone.1..sunk) | dynamic-update-slice | bytes 786436 | tf_op jit(solution)/shard_map/while/body/eval_jaxpr/jit(dynamic_update_index_in_dim)/dynamic_update_slice | solution.py:64
  139.2 11.1 %dynamic_update_slice.32 = f32[768,4,128]{2,1,0:T(4,128)} dynamic-update-slice(f32[768,4,128]{2,1,0:T(4,128)} %get-tuple-element.350, f32[768,1,128]{2,1,0:T(1,128)S(1)} %bitcast.146, s32[]{:T(128)} %constant.126.clone.1..sunk, s32[]{:T(128)S(6)} %copy.65, s32[]{:T(128)} %constant.126.clone.1..sunk) | dynamic-update-slice | bytes 786436 | tf_op jit(solution)/shard_map/while/body/eval_jaxpr/jit(dynamic_update_index_in_dim)/dynamic_update_slice | solution.py:65
  151.1 6.2 %fusion.110 = (f32[4,512]{1,0:T(4,128)S(1)}, f32[4,512,768]{1,2,0:T(8,128)}) fusion(pred[512,768]{0,1:T(8,128)(4,1)S(1)} %fusion.109, bf16[512,4,4,128]{3,0,2,1:T(8,128)(2,1)} %get-tuple-element.367, s32[]{:T(128)S(6)} %copy.65, bf16[768,4,128]{2,0,1:T(8,128)(2,1)} %get-tuple-element.366), kind=kOutput, calls=%fused_computation.69.clone.1 | convolution fusion | flops 408945408 | bytes 7414784 | tf_op jit(solution)/shard_map/while/body/eval_jaxpr/sub | solution.py:20
  157.2 3.7 %fusion.111 = bf16[4,512,768]{1,2,0:T(8,128)(2,1)S(1)} fusion(f32[4,512,768]{1,2,0:T(8,128)} %get-tuple-element.330, f32[4,512]{1,0:T(4,128)S(1)} %get-tuple-element.331), kind=kLoop, calls=%fused_computation.12.clone.1 | loop fusion | flops 3145728 | bytes 9445376 | tf_op jit(solution)/shard_map/while/body/eval_jaxpr/convert_element_type | solution.py:22
  160.9 2.7 fusion.112
  163.6 1.0 fusion.116
  164.6 1.9 fusion.113
  166.6 2.0 fusion.115
  168.6 2.3 fusion.114
  170.9 11.1 %dynamic_update_slice.31 = f32[768,4,128]{2,1,0:T(4,128)} dynamic-update-slice(f32[768,4,128]{2,1,0:T(4,128)} %get-tuple-element.349, f32[768,1,128]{2,1,0:T(1,128)S(1)} %bitcast.147, s32[]{:T(128)} %constant.126.clone.1..sunk, s32[]{:T(128)S(6)} %copy.65, s32[]{:T(128)} %constant.126.clone.1..sunk) | dynamic-update-slice | bytes 786436 | tf_op jit(solution)/shard_map/while/body/eval_jaxpr/jit(dynamic_update_index_in_dim)/dynamic_update_slice | solution.py:64
  182.1 11.1 %dynamic_update_slice.32 = f32[768,4,128]{2,1,0:T(4,128)} dynamic-update-slice(f32[768,4,128]{2,1,0:T(4,128)} %get-tuple-element.350, f32[768,1,128]{2,1,0:T(1,128)S(1)} %bitcast.146, s32[]{:T(128)} %constant.126.clone.1..sunk, s32[]{:T(128)S(6)} %copy.65, s32[]{:T(128)} %constant.126.clone.1..sunk) | dynamic-update-slice | bytes 786436 | tf_op jit(solution)/shard_map/while/body/eval_jaxpr/jit(dynamic_update_index_in_dim)/dynamic_update_slice | solution.py:65
  194.0 6.1 %fusion.110 = (f32[4,512]{1,0:T(4,128)S(1)}, f32[4,512,768]{1,2,0:T(8,128)}) fusion(pred[512,768]{0,1:T(8,128)(4,1)S(1)} %fusion.109, bf16[512,4,4,128]{3,0,2,1:T(8,128)(2,1)} %get-tuple-element.367, s32[]{:T(128)S(6)} %copy.65, bf16[768,4,128]{2,0,1:T(8,128)(2,1)} %get-tuple-element.366), kind=kOutput, calls=%fused_computation.69.clone.1 | convolution fusion | flops 408945408 | bytes 7414784 | tf_op jit(solution)/shard_map/while/body/eval_jaxpr/sub | solution.py:20
  200.1 3.7 %fusion.111 = bf16[4,512,768]{1,2,0:T(8,128)(2,1)S(1)} fusion(f32[4,512,768]{1,2,0:T(8,128)} %get-tuple-element.330, f32[4,512]{1,0:T(4,128)S(1)} %get-tuple-element.331), kind=kLoop, calls=%fused_computation.12.clone.1 | loop fusion | flops 3145728 | bytes 9445376 | tf_op jit(solution)/shard_map/while/body/eval_jaxpr/convert_element_type | solution.py:22
  203.8 2.7 fusion.112
  206.5 1.0 fusion.116
  207.5 1.9 fusion.113
  209.5 2.0 fusion.115
  211.5 2.3 fusion.114
  213.8 11.1 %dynamic_update_slice.31 = f32[768,4,128]{2,1,0:T(4,128)} dynamic-update-slice(f32[768,4,128]{2,1,0:T(4,128)} %get-tuple-element.349, f32[768,1,128]{2,1,0:T(1,128)S(1)} %bitcast.147, s32[]{:T(128)} %constant.126.clone.1..sunk, s32[]{:T(128)S(6)} %copy.65, s32[]{:T(128)} %constant.126.clone.1..sunk) | dynamic-update-slice | bytes 786436 | tf_op jit(solution)/shard_map/while/body/eval_jaxpr/jit(dynamic_update_index_in_dim)/dynamic_update_slice | solution.py:64
  225.0 11.1 %dynamic_update_slice.32 = f32[768,4,128]{2,1,0:T(4,128)} dynamic-update-slice(f32[768,4,128]{2,1,0:T(4,128)} %get-tuple-element.350, f32[768,1,128]{2,1,0:T(1,128)S(1)} %bitcast.146, s32[]{:T(128)} %constant.126.clone.1..sunk, s32[]{:T(128)S(6)} %copy.65, s32[]{:T(128)} %constant.126.clone.1..sunk) | dynamic-update-slice | bytes 786436 | tf_op jit(solution)/shard_map/while/body/eval_jaxpr/jit(dynamic_update_index_in_dim)/dynamic_update_slice | solution.py:65
  236.1 1.1 slice.76
  237.2 4.0 %collective-permute-start.3 = (f32[256,4,128]{2,1,0:T(4,128)S(1)}, f32[256,4,128]{2,1,0:T(4,128)S(1)}, u32[]{:S(2)}, u32[]{:S(2)}) collective-permute-start(f32[256,4,128]{2,1,0:T(4,128)S(1)} %slice.76), channel_id=1, source_target_pairs={{2,0},{4,2},{6,4},{8,6},{10,8},{12,10},{14,12},{16,14},{18,16},{20... | collective-permute-start | bytes 1572872 | tf_op jit(solution)/shard_map/ppermute | solution.py:12
  241.2 3.8 %all-to-all-start.2 = ((bf16[512,4,4,128]{0,3,1,2:T(8,128)(2,1)}), bf16[512,4,4,128]{0,3,1,2:T(8,128)(2,1)S(1)}, u32[]{:S(2)}, u32[]{:S(2)}) async-start(bf16[512,4,4,128]{0,3,1,2:T(8,128)(2,1)} %get-tuple-element.183), calls=%async_computation.2 | async-start | bytes 4194304 | tf_op jit(solution)/shard_map/all_to_all | solution.py:101
  245.0 1.2 slice.79
  246.2 1.9 collective-permute-start.4
  248.1 2.2 slice.77
  250.7 6.3 %collective-permute-done.4 = f32[256,4,128]{2,1,0:T(4,128)S(1)} collective-permute-done((f32[256,4,128]{2,1,0:T(4,128)S(1)}, f32[256,4,128]{2,1,0:T(4,128)S(1)}, u32[]{:S(2)}, u32[]{:S(2)}) %collective-permute-start.4) | collective-permute-done | bytes 524320 | tf_op jit(solution)/shard_map/ppermute | solution.py:12
  257.0 1.9 add_dynamic-update-slice_fusion
  258.8 11.2 %all-to-all-done.2 = bf16[512,4,4,128]{0,3,1,2:T(8,128)(2,1)S(1)} async-done(((bf16[512,4,4,128]{0,3,1,2:T(8,128)(2,1)}), bf16[512,4,4,128]{0,3,1,2:T(8,128)(2,1)S(1)}, u32[]{:S(2)}, u32[]{:S(2)}) %all-to-all-start.2) | async-done | bytes 2097184 | tf_op jit(solution)/shard_map/all_to_all | solution.py:101
  270.0 3.9 %copy.36 = bf16[512,2,4,2,128]{4,3,2,1,0:T(2,128)(2,1)} copy(bf16[512,2,4,2,128]{0,4,2,3,1:T(8,128)(2,1)S(1)} %bitcast.151) | data formatting | bytes 4194304 | tf_op jit(solution)/shard_map/all_to_all | solution.py:101
  (35 shorter events, 2.9 us)
Async XLA Ops:
  5.0 28.9 %all-to-all-start = ((bf16[512,8,2,128]{3,2,0,1:T(2,128)(2,1)}), bf16[512,8,2,128]{3,2,0,1:T(2,128)(2,1)S(1)}, u32[]{:S(2)}, u32[]{:S(2)}) async-start(bf16[512,8,2,128]{3,2,0,1:T(2,128)(2,1)} %copy.30), calls=%async_computation | async-start | bytes 4194304 | tf_op jit(solution)/shard_map/all_to_all | solution.py:84
  13.1 25.5 %copy-start.4 = (s32[512]{0:T(512)S(1)}, s32[512]{0:T(512)}, u32[]{:S(2)}) copy-start(s32[512]{0:T(512)} %param.15) | copy-start | bytes 6148
  13.1 30.1 %copy-start.3 = (bf16[512,8,128]{2,1,0:T(8,128)(2,1)S(1)}, bf16[512,8,128]{2,1,0:T(8,128)(2,1)}, u32[]{:S(2)}) copy-start(bf16[512,8,128]{2,1,0:T(8,128)(2,1)} %param.13) | copy-start | bytes 3145732
  33.8 28.6 %all-to-all-start.1 = ((bf16[512,8,2,128]{3,2,0,1:T(2,128)(2,1)}), bf16[512,8,2,128]{3,2,0,1:T(2,128)(2,1)}, u32[]{:S(2)}, u32[]{:S(2)}) async-start(bf16[512,8,2,128]{3,2,0,1:T(2,128)(2,1)} %copy.33), calls=%async_computation.1 | async-start | bytes 4194304 | tf_op jit(solution)/shard_map/all_to_all | solution.py:85
  38.7 12.9 %collective-permute-start.1 = (s32[256]{0:T(256)S(1)}, s32[256]{0:T(256)S(1)}, u32[]{:S(2)}, u32[]{:S(2)}) collective-permute-start(s32[256]{0:T(256)S(1)} %slice.72), channel_id=1, source_target_pairs={{0,2},{2,4},{4,6},{6,8},{8,10},{10,12},{12,14},{14,16},{16,18},{18... | collective-permute-start | bytes 3080 | tf_op jit(solution)/shard_map/ppermute | solution.py:12
  45.1 6.5 %collective-permute-start.2 = (bf16[256,4,128]{2,0,1:T(8,128)(2,1)S(1)}, bf16[256,4,128]{2,0,1:T(8,128)(2,1)}, u32[]{:S(2)}, u32[]{:S(2)}) collective-permute-start(bf16[256,4,128]{2,0,1:T(8,128)(2,1)S(1)} %slice.81), channel_id=1, source_target_pairs={{0,2},{2,4},{4,6},{6,8},{8,10},{10,12},{12,14},{14,16},{16,18},{18... | collective-permute-start | bytes 786440 | tf_op jit(solution)/shard_map/ppermute | solution.py:12
  47.8 7.1 %collective-permute-start = (bf16[256,4,128]{2,0,1:T(8,128)(2,1)}, bf16[256,4,128]{2,0,1:T(8,128)(2,1)}, u32[]{:S(2)}, u32[]{:S(2)}) collective-permute-start(bf16[256,4,128]{2,0,1:T(8,128)(2,1)} %slice.80), channel_id=1, source_target_pairs={{0,2},{2,4},{4,6},{6,8},{8,10},{10,12},{12,14},{14,16},{16,18},{18... | collective-permute-start | bytes 786440 | tf_op jit(solution)/shard_map/ppermute | solution.py:12
  75.1 3.7 %copy-start = (f32[4,512,768]{1,2,0:T(8,128)S(1)}, f32[4,512,768]{1,2,0:T(8,128)}, u32[]{:S(2)}) copy-start(f32[4,512,768]{1,2,0:T(8,128)} %get-tuple-element.330) | copy-start | bytes 18874372 | tf_op jit(solution)/shard_map/while
  118.0 3.7 %copy-start = (f32[4,512,768]{1,2,0:T(8,128)S(1)}, f32[4,512,768]{1,2,0:T(8,128)}, u32[]{:S(2)}) copy-start(f32[4,512,768]{1,2,0:T(8,128)} %get-tuple-element.330) | copy-start | bytes 18874372 | tf_op jit(solution)/shard_map/while
  160.9 3.7 %copy-start = (f32[4,512,768]{1,2,0:T(8,128)S(1)}, f32[4,512,768]{1,2,0:T(8,128)}, u32[]{:S(2)}) copy-start(f32[4,512,768]{1,2,0:T(8,128)} %get-tuple-element.330) | copy-start | bytes 18874372 | tf_op jit(solution)/shard_map/while
  203.8 3.7 %copy-start = (f32[4,512,768]{1,2,0:T(8,128)S(1)}, f32[4,512,768]{1,2,0:T(8,128)}, u32[]{:S(2)}) copy-start(f32[4,512,768]{1,2,0:T(8,128)} %get-tuple-element.330) | copy-start | bytes 18874372 | tf_op jit(solution)/shard_map/while
  237.2 13.3 %collective-permute-start.3 = (f32[256,4,128]{2,1,0:T(4,128)S(1)}, f32[256,4,128]{2,1,0:T(4,128)S(1)}, u32[]{:S(2)}, u32[]{:S(2)}) collective-permute-start(f32[256,4,128]{2,1,0:T(4,128)S(1)} %slice.76), channel_id=1, source_target_pairs={{2,0},{4,2},{6,4},{8,6},{10,8},{12,10},{14,12},{16,14},{18,16},{20... | collective-permute-start | bytes 1572872 | tf_op jit(solution)/shard_map/ppermute | solution.py:12
  241.2 28.8 %all-to-all-start.2 = ((bf16[512,4,4,128]{0,3,1,2:T(8,128)(2,1)}), bf16[512,4,4,128]{0,3,1,2:T(8,128)(2,1)S(1)}, u32[]{:S(2)}, u32[]{:S(2)}) async-start(bf16[512,4,4,128]{0,3,1,2:T(8,128)(2,1)} %get-tuple-element.183), calls=%async_computation.2 | async-start | bytes 4194304 | tf_op jit(solution)/shard_map/all_to_all | solution.py:101
  245.0 5.3 %copy-start.1 = (f32[768,4,128]{2,1,0:T(4,128)S(1)}, f32[768,4,128]{2,1,0:T(4,128)}, u32[]{:S(2)}) copy-start(f32[768,4,128]{2,1,0:T(4,128)} %get-tuple-element.184) | copy-start | bytes 4718596
  246.2 10.8 %collective-permute-start.4 = (f32[256,4,128]{2,1,0:T(4,128)S(1)}, f32[256,4,128]{2,1,0:T(4,128)S(1)}, u32[]{:S(2)}, u32[]{:S(2)}) collective-permute-start(f32[256,4,128]{2,1,0:T(4,128)S(1)} %slice.79), channel_id=1, source_target_pairs={{2,0},{4,2},{6,4},{8,6},{10,8},{12,10},{14,12},{16,14},{18,16},{20... | collective-permute-start | bytes 1572872 | tf_op jit(solution)/shard_map/ppermute | solution.py:12
  250.7 6.3 %copy-start.2 = (bf16[512,4,128]{2,1,0:T(4,128)(2,1)}, bf16[512,4,128]{2,1,0:T(4,128)(2,1)S(1)}, u32[]{:S(2)}) copy-start(bf16[512,4,128]{2,1,0:T(4,128)(2,1)S(1)} %add_dynamic-update-slice_fusion.1) | copy-start | bytes 1572868
where the time goes:
time: 278 us; the launch traced here: 274 us
  local copies, waits for them, and re-layouts  113 us (41%)
  matrix products  64.5 us (23%)
  waiting for transfers between devices  43.4 us (16%)
  starting transfers between devices  28.4 us (10%)
  other arithmetic  23.8 us (9%)
    dynamic_update_slice x4, local copies, waits for them, and re-layouts, head_step(): key_acc = lax.dynamic_update_index_in_dim(key_acc, key_part, kv_head, 1)  44.5 us
    dynamic_update_slice x4, local copies, waits for them, and re-layouts, head_step(): lax.dynamic_update_index_in_dim(value_acc, value_part, kv_head, 1)  44.5 us
    sub x4, matrix products, head_grads(): weights = jnp.exp(scores - top_score)  24.6 us
    all_to_all x1, waiting for transfers between devices, on_device(): lax.all_to_all(queries, 'head', split_axis=1, concat_axis=2, tiled=True)  20.7 us
    ppermute x5, starting transfers between devices, from_behind(): return lax.ppermute(block, axis, route)  16.1 us
    convert_element_type x4, other arithmetic, head_grads(): prob_low = attn_prob.astype(jnp.bfloat16)  14.7 us
    all_to_all x1, waiting for transfers between devices, on_device(): lax.all_to_all(group_qgrad, 'head', split_axis=2, concat_axis=1, tiled=True)  11.2 us
    dot_general x4, matrix products, head_grads(): jnp.einsum('glm,md->lgd', prob_low, value_n, preferred_element_type=jnp.f...  10.9 us
  transfers between devices with their start and end apart: 8, of which 5 were waited for; matrix products, arithmetic and copies ran while one was open for 7% of the time, Pallas kernels for 0%

commit v1 on v0

v1 whole, which is shorter than its diff:
```python
import functools

import jax
import jax.numpy as jnp
from jax import lax
from jax.experimental import pallas as pl
from jax.experimental.pallas import tpu as pltpu
from jax.sharding import PartitionSpec as P

WINDOW = 256
CHUNK = 128
LOG2E = 1.4426950408889634
F32 = jnp.float32
BF16 = jnp.bfloat16


def dot(a, b, contract):
    return lax.dot_general(a, b, ((contract[0], contract[1]), ((), ())), preferred_element_type=F32)


def chunk_grads(q, do, k, v, kt, low):
    cols = q.shape[0]
    group = cols // CHUNK
    scale = 1.0 / q.shape[1] ** 0.5
    rows = lax.broadcasted_iota(jnp.int32, (k.shape[0], cols), 0)
    last = lax.div(lax.broadcasted_iota(jnp.int32, (1, cols), 1), jnp.int32(group)) + WINDOW
    scores = dot(k, q, ((1,), (1,)))
    grad_prob = dot(v, do, ((1,), (1,)))
    scores = jnp.where((rows >= low) & (rows <= last), scores, -1e30)
    top = jnp.max(scores, axis=0, keepdims=True)
    weights = jnp.exp2((scores - top) * (scale * LOG2E))
    total = jnp.sum(weights, axis=0, keepdims=True)
    prob = weights * (1.0 / total)
    delta = jnp.sum(prob * grad_prob, axis=0, keepdims=True)
    prob_low = prob.astype(BF16)
    grad_low = (prob * (grad_prob - delta)).astype(BF16)
    query_grad = dot(kt, grad_low, ((1,), (0,))) * scale
    return (
        query_grad.T.astype(BF16),
        dot(grad_low, q, ((1,), (0,))),
        dot(prob_low, do, ((1,), (0,))),
    )


def kernel(head_ref, *refs, chunks, first, halo, carry, emit, aliased):
    it = iter(refs)
    low_ref, q_ref, do_ref, kv_ref = next(it), next(it), next(it), next(it)
    halo_ref = next(it) if halo else None
    carry_ref = next(it) if carry else None
    if aliased:
        next(it)
    dq_ref = next(it)
    own_ref = next(it)
    back_ref = next(it) if halo else None
    acc = next(it)
    win = next(it) if halo else None
    head_size = q_ref.shape[-1]
    group = q_ref.shape[-2]
    cols = CHUNK * group
    scale = 1.0 / head_size**0.5
    span = kv_ref.shape[1]
    if halo:
        win[:, :WINDOW] = halo_ref[...]
        win[:, WINDOW:] = kv_ref[...]
        src = win
    else:
        src = kv_ref
    acc[...] = jnp.zeros_like(acc)
    kt = src[0].T
    for slot, chunk in enumerate(chunks):
        start = chunk * CHUNK - WINDOW - first
        keys = slice(start, start + WINDOW + CHUNK)
        own = slice(slot * CHUNK, (slot + 1) * CHUNK)
        q = q_ref[own].reshape(cols, head_size)
        do = do_ref[own].reshape(cols, head_size)
        low = low_ref[slot : slot + 1, :]
        dq, dk, dv = chunk_grads(q, do, src[0, keys], src[1, keys], kt[:, keys], low)
        dq_ref[own] = dq.reshape(CHUNK, group, head_size)
        acc[0, keys] += dk
        acc[1, keys] += dv
    off = 0
    if halo:
        back_ref[0] = (acc[0, :WINDOW] * scale).astype(BF16)
        back_ref[1] = acc[1, :WINDOW].astype(BF16)
        off = WINDOW
    for i, factor in ((0, scale), (1, 1.0)):
        value = acc[i, off:] * factor
        if carry:
            value = value + carry_ref[i]
        own_ref[i] = value.astype(own_ref.dtype)


def attend(head, low, queries, out_grad, kv, halo, carry, query_grad, chunks, heads, emit):
    tokens, kv_count, group, head_size = queries.shape
    rows = len(chunks) * CHUNK
    row_block = chunks[0] * CHUNK // rows
    has_halo = halo is not None
    first = -WINDOW if has_halo else 0
    top = (chunks[-1] + 1) * CHUNK
    span = top
    q_spec = pl.BlockSpec((rows, None, group, head_size), lambda n, h: (row_block, n + h[0], 0, 0))
    part = lambda r, block=0: pl.BlockSpec((2, None, r, head_size), lambda n, h: (0, n, block, 0))
    in_specs = [
        pl.BlockSpec(low.shape, lambda n, h: (0, 0)),
        q_spec,
        q_spec,
        pl.BlockSpec((2, None, span, head_size), lambda n, h: (0, n + h[0], 0, 0)),
    ]
    operands = [low, queries, out_grad, kv]
    if has_halo:
        in_specs.append(part(WINDOW))
        operands.append(halo)
    if carry is not None:
        in_specs.append(part(span))
        operands.append(carry)
    aliases = {}
    if query_grad is not None:
        aliases = {1 + len(operands): 0}
        in_specs.append(pl.BlockSpec(memory_space=pl.ANY))
        operands.append(query_grad)
    out_specs = [q_spec, part(span)]
    out_shape = [
        jax.ShapeDtypeStruct(queries.shape, BF16),
        jax.ShapeDtypeStruct((2, heads, span, head_size), emit),
    ]
    window = span + (WINDOW if has_halo else 0)
    scratch = [pltpu.VMEM((2, window, head_size), F32)]
    if has_halo:
        out_specs.append(part(WINDOW))
        out_shape.append(jax.ShapeDtypeStruct((2, heads, WINDOW, head_size), BF16))
        scratch.append(pltpu.VMEM((2, window, head_size), BF16))
    flops = heads * len(chunks) * 5 * 2 * CHUNK * group * (WINDOW + CHUNK) * head_size
    return pl.pallas_call(
        functools.partial(
            kernel,
            chunks=chunks,
            first=first,
            halo=has_halo,
            carry=carry is not None,
            emit=emit,
            aliased=query_grad is not None,
        ),
        grid_spec=pltpu.PrefetchScalarGridSpec(
            num_scalar_prefetch=1,
            grid=(heads,),
            in_specs=in_specs,
            out_specs=out_specs,
            scratch_shapes=scratch,
        ),
        out_shape=out_shape,
        input_output_aliases=aliases,
        compiler_params=pltpu.CompilerParams(vmem_limit_bytes=32 * 1024 * 1024),
        cost_estimate=pl.CostEstimate(
            flops=flops, bytes_accessed=heads * rows * group * head_size * 8, transcendentals=0
        ),
    )(head, *operands)


def shift(block, axis, distance):
    devices = range(lax.axis_size(axis))
    return lax.ppermute(block, axis, [(i - distance, i) for i in devices if i - distance in devices])


def swap(block):
    return lax.ppermute(block, "head", [(0, 1), (1, 0)])


def on_device(queries, key_heads, value_heads, out_grad, doc_ids):
    tokens, kv_count, group, _ = queries.shape
    half = kv_count // 2
    mine = lax.axis_index("head") * half
    other = half - mine
    chunk_count = tokens // CHUNK
    split = WINDOW // CHUNK
    kv = jnp.stack([key_heads.transpose(1, 0, 2), value_heads.transpose(1, 0, 2)])
    tail = kv[:, :, tokens - WINDOW :]
    halo_other = shift(lax.dynamic_slice_in_dim(tail, other, half, 1), "ctx", 1)
    prev_docs = shift(doc_ids[tokens - WINDOW :], "ctx", 1)
    halo_mine = shift(lax.dynamic_slice_in_dim(tail, mine, half, 1), "ctx", 1)

    token = jnp.arange(tokens, dtype=jnp.int32)
    lower = jnp.sum((doc_ids[None, :] < doc_ids[:, None]).astype(jnp.int32), axis=1)
    prev_docs = jnp.where(lax.axis_index("ctx") == 0, -1, prev_docs)
    before = jnp.sum((prev_docs[None, :] < doc_ids[:WINDOW, None]).astype(jnp.int32), axis=1)

    def columns(low):
        low = jnp.repeat(low, group).reshape(-1, CHUNK * group)
        base = jnp.arange(low.shape[0], dtype=jnp.int32)[:, None] * CHUNK
        return low - base

    low_late = columns(jnp.maximum(token + 1, lower + WINDOW)[WINDOW:] - WINDOW)
    low_early = columns(jnp.maximum(token[:WINDOW] + 1, lower[:WINDOW] + before))

    head_other = jnp.reshape(other, (1,))
    head_mine = jnp.reshape(mine, (1,))
    late = tuple(range(split, chunk_count))
    early = tuple(range(split))
    query_grad, part_other = attend(
        head_other, low_late, queries, out_grad, kv, None, None, None, late, half, F32
    )
    query_grad, first_other, back_other = attend(
        head_other, low_early, queries, out_grad, kv, halo_other, part_other, query_grad, early, half, BF16
    )
    back_other = shift(back_other, "ctx", -1)
    first_other = swap(first_other)
    query_grad, part_mine, back_mine = attend(
        head_mine,
        jnp.concatenate([low_early, low_late - 0]),
        queries,
        out_grad,
        kv,
        halo_mine,
        None,
        query_grad,
        early + late,
        half,
        F32,
    )
    last_other = part_other[:, :, WINDOW:]
    last_other = last_other.at[:, :, tokens - 2 * WINDOW :].add(back_other.astype(F32))
    last_other = swap(last_other.astype(BF16))
    back_mine = shift(back_mine, "ctx", -1)
    total = part_mine + jnp.concatenate([first_other, last_other], 2).astype(F32)
    total = total.at[:, :, tokens - WINDOW :].add(back_mine.astype(F32))
    total = total.astype(BF16).transpose(0, 2, 1, 3)
    return query_grad, total[0], total[1]


def solution(mesh):
    in_specs = (
        P("ctx", None, "head", None),
        P("ctx", None, None),
        P("ctx", None, None),
        P("ctx", None, "head", None),
        P("ctx"),
    )
    out_specs = (P("ctx", None, "head", None), P("ctx", "head", None), P("ctx", "head", None))
    return jax.shard_map(on_device, mesh=mesh, in_specs=in_specs, out_specs=out_specs, check_vma=False)
```

time: 278 us -> 75 us (0.27); the launches traced: 274 us -> 74.7 us
  local copies, waits for them, and re-layouts: 113 us -> 8.95 us
  matrix products: 64.5 us -> 0 us
  Pallas kernels: 0 us -> 25.3 us
  waiting for transfers between devices: 43.4 us -> 20.9 us
  other arithmetic: 23.8 us -> 1.52 us
  starting transfers between devices: 28.4 us -> 17.2 us
    dynamic_update_slice x8 -> x0, local copies, waits for them, and re-layouts: 89 us -> none  [the longest x4 44.5 us: head_step(): key_acc = lax.dynamic_update_index_in_dim(key_acc, key_part, kv_head, 1)]
    dot_general x20 -> x0, matrix products: 39.9 us -> none  [the longest x4 10.9 us: head_grads(): jnp.einsum('glm,md->lgd', prob_low, value_n, preferred_element_type=jnp.f...]
    all_to_all x3 -> x0, waiting for transfers between devices: 35.6 us -> none  [the longest x1 20.7 us: on_device(): lax.all_to_all(queries, 'head', split_axis=1, concat_axis=2, tiled=True)]
    pallas_call x0 -> x3, Pallas kernels: none -> 25.3 us  [attend(): pl.pallas_call(functools.partial(kernel, chunks=chunks, first=first, halo...]
    sub x4 -> x0, matrix products: 24.6 us -> none  [head_grads(): weights = jnp.exp(scores - top_score)]
    convert_element_type x4 -> x1, other arithmetic: 14.7 us -> 0.11 us  [on_device(): last_other = swap(last_other.astype(BF16))]
    ppermute x5 -> x7, waiting for transfers between devices: 7.73 us -> 20.9 us  [the longest x5 20.9 us: shift(): lax.ppermute(block, axis, [(i - distance, i) for i in devices if i - dist...]
    all_to_all x3 -> x0, starting transfers between devices: 12.3 us -> none  [the longest x1 4.81 us: on_device(): lax.all_to_all(out_grad, 'head', split_axis=1, concat_axis=2, tiled=True)]
  transfers between devices with their start and end apart: 8 -> 7, of which waited for: 5 -> 4; matrix products, arithmetic and copies ran while one was open for 7% -> 2% of each run, Pallas kernels for 0% -> 25%
where the time goes in v1:
time: 75 us; the launch traced here: 74.7 us
  Pallas kernels  25.3 us (34%)
  waiting for transfers between devices  20.9 us (28%)
  starting transfers between devices  17.2 us (23%)
  local copies, waits for them, and re-layouts  8.95 us (12%)
  other arithmetic  1.52 us (2%)
  between operations  0.84 us (1%)
    pallas_call x3, Pallas kernels, attend(): pl.pallas_call(functools.partial(kernel, chunks=chunks, first=first, halo...  25.3 us
    ppermute x5, waiting for transfers between devices, shift(): lax.ppermute(block, axis, [(i - distance, i) for i in devices if i - dist...  20.9 us
    ppermute x5, starting transfers between devices, shift(): lax.ppermute(block, axis, [(i - distance, i) for i in devices if i - dist...  14.6 us
    unnamed x10, local copies, waits for them, and re-layouts  5.6 us
    ppermute x2, starting transfers between devices, swap(): return lax.ppermute(block, 'head', [(0, 1), (1, 0)])  2.58 us
    another operation x1, local copies, waits for them, and re-layouts, on_device(): jnp.stack([key_heads.transpose(1, 0, 2), value_heads.transpose(1, 0, 2)])  1.92 us
  transfers between devices with their start and end apart: 7, of which 4 were waited for; matrix products, arithmetic and copies ran while one was open for 2% of the time, Pallas kernels for 25%

profile of v1, /device:TPU:1, one launch (start us, length us, event | category | flops | bytes accessed | tf_op | source)
XLA Modules:
  0.0 74.7 jit_solution(14975164291528286051)
XLA Ops:
  0.6 1.9 %copy_bitcast_fusion = (bf16[1,8,512,128]{3,2,1,0:T(8,128)(2,1)S(1)}, bf16[1,8,512,128]{3,2,1,0:T(8,128)(2,1)S(1)}) fusion(bf16[512,8,128]{2,1,0:T(8,128)(2,1)} %param.13, bf16[512,8,128]{2,1,0:T(8,128)(2,1)} %param.12), kind=kLoop, calls=%fused_computation.7 | loop fusion | bytes 4194304 | tf_op jit(solution)/shard_map/stack | solution.py:175
  2.6 0.0 copy-start.3
  2.6 0.1 fusion
  2.7 0.9 %constant_dynamic-slice_fusion = (bf16[2,4,256,128]{3,2,1,0:T(8,128)(2,1)}, bf16[2,4,256,128]{3,2,1,0:T(8,128)(2,1)S(1)}) fusion(bf16[2,8,256,128]{3,2,1,0:T(8,128)(2,1)S(1)} %fusion, s32[]{:T(128)S(6)} %select_n.17, s32[]{:T(128)S(6)} %select_n.16), kind=kLoop, calls=%fused_computation.23 | loop fusion | bytes 2097160 | tf_op jit(solution)/shard_map/dynamic_slice | solution.py:177
  3.6 4.5 %collective-permute-start.2 = (bf16[2,4,256,128]{3,2,1,0:T(8,128)(2,1)}, bf16[2,4,256,128]{3,2,1,0:T(8,128)(2,1)S(1)}, u32[]{:S(2)}, u32[]{:S(2)}) collective-permute-start(bf16[2,4,256,128]{3,2,1,0:T(8,128)(2,1)} %get-tuple-element.62), channel_id=1, source_target_pairs={{0,2},{2,4},{4,6},{6,8},{8,10},{10,12},{12,14},{14,16},{16,18},{18... | collective-permute-start | bytes 1572872 | tf_op jit(solution)/shard_map/ppermute | solution.py:161
  8.1 0.0 copy-done.3
  8.1 1.9 %collective-permute-start = (s32[256]{0:T(256)S(1)}, s32[256]{0:T(256)S(1)}, u32[]{:S(2)}, u32[]{:S(2)}) collective-permute-start(s32[256]{0:T(256)S(1)} %get-tuple-element.65), channel_id=1, source_target_pairs={{0,2},{2,4},{4,6},{6,8},{8,10},{10,12},{12,14},{14,16},{16,18},{18... | collective-permute-start | bytes 3080 | tf_op jit(solution)/shard_map/ppermute | solution.py:161
  10.0 0.2 convert_reduce_fusion
  10.3 0.2 pad_maximum_fusion.refs_3_
  10.5 0.1 broadcast_in_dim.23
  10.6 0.1 broadcast_in_dim.24
  10.8 3.7 %collective-permute-done = s32[256]{0:T(256)S(1)} collective-permute-done((s32[256]{0:T(256)S(1)}, s32[256]{0:T(256)S(1)}, u32[]{:S(2)}, u32[]{:S(2)}) %collective-permute-start) | collective-permute-done | bytes 1056 | tf_op jit(solution)/shard_map/ppermute | solution.py:161
  14.5 0.2 convert_reduce_fusion.1
  14.7 0.1 broadcast_in_dim.21
  14.8 0.1 broadcast_in_dim.22
  15.0 0.1 broadcast_subtract_fusion.1
  15.0 0.0 copy-start
  15.0 1.6 %copy-done = bf16[512,8,2,128]{3,2,1,0:T(2,128)(2,1)S(1)} copy-done((bf16[512,8,2,128]{3,2,1,0:T(2,128)(2,1)S(1)}, bf16[512,8,2,128]{3,2,1,0:T(2,128)(2,1)}, u32[]{:S(2)}) %copy-start) | copy-done | bytes 2097176
  16.6 0.0 copy-start.2
  16.6 1.6 %copy-done.2 = bf16[512,8,2,128]{3,2,1,0:T(2,128)(2,1)S(1)} copy-done((bf16[512,8,2,128]{3,2,1,0:T(2,128)(2,1)S(1)}, bf16[512,8,2,128]{3,2,1,0:T(2,128)(2,1)}, u32[]{:S(2)}) %copy-start.2) | copy-done | bytes 2097176
  18.2 0.0 copy-start.1
  18.2 6.8 %shard_map.81 = (bf16[512,8,2,128]{3,2,1,0:T(2,128)(2,1)}, f32[2,4,512,128]{3,2,1,0:T(8,128)S(1)}) custom-call(s32[1]{0:T(128)} %bitcast.7.head_ref, s32[2,256]{1,0:T(2,128)S(1)} %get-tuple-element.67.refs_0_, bf16[512,8,2,128]{3,2,1,0:T(2,128)(2,1)S(1)} %copy-done, bf16[512,8,2,128]{3,2,1,0:T(2,128)(2,1)S(1)} %copy-done.2, ...), custom_call_target="tpu_custom_call" | custom-call | flops 1006632960 | bytes 2097152 | tf_op jit(solution)/shard_map/pallas_call | solution.py:133
  25.0 0.0 collective-permute-done.2.refs_4_
  25.0 0.0 copy-done.1
  25.0 6.9 %shard_map.82 = (bf16[512,8,2,128]{3,2,1,0:T(2,128)(2,1)}, bf16[2,4,256,128]{3,2,1,0:T(8,128)(2,1)S(1)}, bf16[2,4,256,128]{3,2,1,0:T(8,128)(2,1)S(1)}) custom-call(s32[1]{0:T(128)} %bitcast.7.head_ref, s32[2,256]{1,0:T(2,128)S(1)} %get-tuple-element.66.refs_0_, bf16[512,8,2,128]{3,2,1,0:T(2,128)(2,1)S(1)} %copy-done.1, ...), custom_call_target="tpu_custom_call", output_to_operand_aliasing={{0}: (7, {})} | custom-call | flops 1006632960 | bytes 2097152 | tf_op jit(solution)/shard_map/pallas_call | solution.py:133
  31.9 1.9 %collective-permute-start.4 = (bf16[2,4,256,128]{3,2,1,0:T(8,128)(2,1)S(1)}, bf16[2,4,256,128]{3,2,1,0:T(8,128)(2,1)S(1)}, u32[]{:S(2)}, u32[]{:S(2)}) collective-permute-start(bf16[2,4,256,128]{3,2,1,0:T(8,128)(2,1)S(1)} %get-tuple-element.49), channel_id=1, source_target_pairs={{2,0},{4,2},{6,4},{8,6},{10,8},{12,10},{14,12},{16,14},{18,16},{20... | collective-permute-start | bytes 1572872 | tf_op jit(solution)/shard_map/ppermute | solution.py:161
  33.8 4.3 %collective-permute-start.1 = (bf16[2,4,256,128]{3,2,1,0:T(8,128)(2,1)S(1)}, bf16[2,4,256,128]{3,2,1,0:T(8,128)(2,1)S(1)}, u32[]{:S(2)}, u32[]{:S(2)}) collective-permute-start(bf16[2,4,256,128]{3,2,1,0:T(8,128)(2,1)S(1)} %get-tuple-element.63), channel_id=1, source_target_pairs={{0,2},{2,4},{4,6},{6,8},{8,10},{10,12},{12,14},{14,16},{16,18},{18... | collective-permute-start | bytes 1572872 | tf_op jit(solution)/shard_map/ppermute | solution.py:161
  38.1 1.3 %collective-permute-start.3 = (bf16[2,4,256,128]{3,2,1,0:T(8,128)(2,1)S(1)}, bf16[2,4,256,128]{3,2,1,0:T(8,128)(2,1)S(1)}, u32[]{:S(2)}, u32[]{:S(2)}) collective-permute-start(bf16[2,4,256,128]{3,2,1,0:T(8,128)(2,1)S(1)} %get-tuple-element.48), channel_id=1, source_target_pairs={{0,1},{1,0},{2,3},{3,2},{4,5},{5,4},{6,7},{7,6},{8,9},{9,8},{10,11... | collective-permute-start | bytes 1572872 | tf_op jit(solution)/shard_map/ppermute | solution.py:165
  39.4 3.9 %collective-permute-done.4 = bf16[2,4,256,128]{3,2,1,0:T(8,128)(2,1)S(1)} collective-permute-done((bf16[2,4,256,128]{3,2,1,0:T(8,128)(2,1)S(1)}, bf16[2,4,256,128]{3,2,1,0:T(8,128)(2,1)S(1)}, u32[]{:S(2)}, u32[]{:S(2)}) %collective-permute-start.4) | collective-permute-done | bytes 524320 | tf_op jit(solution)/shard_map/ppermute | solution.py:161
  43.3 0.1 add_convert_fusion
  43.4 1.3 %collective-permute-start.5 = (bf16[2,4,256,128]{3,2,1,0:T(8,128)(2,1)S(1)}, bf16[2,4,256,128]{3,2,1,0:T(8,128)(2,1)S(1)}, u32[]{:S(2)}, u32[]{:S(2)}) collective-permute-start(bf16[2,4,256,128]{3,2,1,0:T(8,128)(2,1)S(1)} %add_convert_fusion), channel_id=1, source_target_pairs={{0,1},{1,0},{2,3},{3,2},{4,5},{5,4},{6,7},{7,6},{8,9},{9,8},{10,11... | collective-permute-start | bytes 1572872 | tf_op jit(solution)/shard_map/ppermute | solution.py:165
  44.7 4.1 %collective-permute-done.1.refs_4_ = bf16[2,4,256,128]{3,2,1,0:T(8,128)(2,1)S(1)} collective-permute-done((bf16[2,4,256,128]{3,2,1,0:T(8,128)(2,1)S(1)}, bf16[2,4,256,128]{3,2,1,0:T(8,128)(2,1)S(1)}, u32[]{:S(2)}, u32[]{:S(2)}) %collective-permute-start.1) | collective-permute-done | bytes 524320 | tf_op jit(solution)/shard_map/ppermute | solution.py:161
  48.9 11.7 %shard_map.83 = (bf16[512,8,2,128]{3,2,1,0:T(2,128)(2,1)}, f32[2,4,512,128]{3,2,1,0:T(8,128)S(1)}, bf16[2,4,256,128]{3,2,1,0:T(8,128)(2,1)S(1)}) custom-call(s32[1]{0:T(128)} %bitcast.head_ref, s32[4,256]{1,0:T(4,128)S(1)} %pad_add_fusion.refs_0_, bf16[512,8,2,128]{3,2,1,0:T(2,128)(2,1)S(1)} %copy-done.1, ...), custom_call_target="tpu_custom_call", output_to_operand_aliasing={{0}: (6, {})} | custom-call | flops 2013265920 | bytes 4194304 | tf_op jit(solution)/shard_map/pallas_call | solution.py:133
  60.5 1.9 %collective-permute-start.6 = (bf16[2,4,256,128]{3,2,1,0:T(8,128)(2,1)S(1)}, bf16[2,4,256,128]{3,2,1,0:T(8,128)(2,1)S(1)}, u32[]{:S(2)}, u32[]{:S(2)}) collective-permute-start(bf16[2,4,256,128]{3,2,1,0:T(8,128)(2,1)S(1)} %get-tuple-element.50), channel_id=1, source_target_pairs={{2,0},{4,2},{6,4},{8,6},{10,8},{12,10},{14,12},{16,14},{18,16},{20... | collective-permute-start | bytes 1572872 | tf_op jit(solution)/shard_map/ppermute | solution.py:161
  62.5 0.0 collective-permute-done.3
  62.5 0.0 collective-permute-done.5
  62.5 0.2 convert_add_fusion
  62.7 9.1 %collective-permute-done.6 = bf16[2,4,256,128]{3,2,1,0:T(8,128)(2,1)S(1)} collective-permute-done((bf16[2,4,256,128]{3,2,1,0:T(8,128)(2,1)S(1)}, bf16[2,4,256,128]{3,2,1,0:T(8,128)(2,1)S(1)}, u32[]{:S(2)}, u32[]{:S(2)}) %collective-permute-start.6) | collective-permute-done | bytes 524320 | tf_op jit(solution)/shard_map/ppermute | solution.py:161
  71.8 0.2 fusion.1
  72.0 0.2 convert_bitcast_fusion
  72.2 0.1 slice_bitcast_fusion
  72.3 1.2 %copy.20 = bf16[512,4,128]{2,1,0:T(4,128)(2,1)} copy(bf16[512,4,128]{2,0,1:T(8,128)(2,1)S(1)} %get-tuple-element.61) | data formatting | bytes 1048576
  73.5 1.2 %copy.21 = bf16[512,4,128]{2,1,0:T(4,128)(2,1)} copy(bf16[512,4,128]{2,0,1:T(8,128)(2,1)S(1)} %get-tuple-element.60) | data formatting | bytes 1048576
  (8 shorter events, 0.0 us)
Async XLA Ops:
  2.6 5.5 %copy-start.3 = (s32[512]{0:T(512)S(1)}, s32[512]{0:T(512)}, u32[]{:S(2)}) copy-start(s32[512]{0:T(512)} %param.15) | copy-start | bytes 6148
  3.6 21.4 %collective-permute-start.2 = (bf16[2,4,256,128]{3,2,1,0:T(8,128)(2,1)}, bf16[2,4,256,128]{3,2,1,0:T(8,128)(2,1)S(1)}, u32[]{:S(2)}, u32[]{:S(2)}) collective-permute-start(bf16[2,4,256,128]{3,2,1,0:T(8,128)(2,1)} %get-tuple-element.62), channel_id=1, source_target_pairs={{0,2},{2,4},{4,6},{6,8},{8,10},{10,12},{12,14},{14,16},{16,18},{18... | collective-permute-start | bytes 1572872 | tf_op jit(solution)/shard_map/ppermute | solution.py:161
  8.1 6.4 %collective-permute-start = (s32[256]{0:T(256)S(1)}, s32[256]{0:T(256)S(1)}, u32[]{:S(2)}, u32[]{:S(2)}) collective-permute-start(s32[256]{0:T(256)S(1)} %get-tuple-element.65), channel_id=1, source_target_pairs={{0,2},{2,4},{4,6},{6,8},{8,10},{10,12},{12,14},{14,16},{16,18},{18... | collective-permute-start | bytes 3080 | tf_op jit(solution)/shard_map/ppermute | solution.py:161
  15.0 1.6 %copy-start = (bf16[512,8,2,128]{3,2,1,0:T(2,128)(2,1)S(1)}, bf16[512,8,2,128]{3,2,1,0:T(2,128)(2,1)}, u32[]{:S(2)}) copy-start(bf16[512,8,2,128]{3,2,1,0:T(2,128)(2,1)} %refs_1_.5) | copy-start | bytes 6291460
  16.6 1.6 %copy-start.2 = (bf16[512,8,2,128]{3,2,1,0:T(2,128)(2,1)S(1)}, bf16[512,8,2,128]{3,2,1,0:T(2,128)(2,1)}, u32[]{:S(2)}) copy-start(bf16[512,8,2,128]{3,2,1,0:T(2,128)(2,1)} %refs_2_.5) | copy-start | bytes 6291460
  18.2 6.8 %copy-start.1 = (bf16[512,8,2,128]{3,2,1,0:T(2,128)(2,1)S(1)}, bf16[512,8,2,128]{3,2,1,0:T(2,128)(2,1)}, u32[]{:S(2)}) copy-start(bf16[512,8,2,128]{3,2,1,0:T(2,128)(2,1)} %refs_1_.5) | copy-start | bytes 6291460
  31.9 11.5 %collective-permute-start.4 = (bf16[2,4,256,128]{3,2,1,0:T(8,128)(2,1)S(1)}, bf16[2,4,256,128]{3,2,1,0:T(8,128)(2,1)S(1)}, u32[]{:S(2)}, u32[]{:S(2)}) collective-permute-start(bf16[2,4,256,128]{3,2,1,0:T(8,128)(2,1)S(1)} %get-tuple-element.49), channel_id=1, source_target_pairs={{2,0},{4,2},{6,4},{8,6},{10,8},{12,10},{14,12},{16,14},{18,16},{20... | collective-permute-start | bytes 1572872 | tf_op jit(solution)/shard_map/ppermute | solution.py:161
  33.8 15.1 %collective-permute-start.1 = (bf16[2,4,256,128]{3,2,1,0:T(8,128)(2,1)S(1)}, bf16[2,4,256,128]{3,2,1,0:T(8,128)(2,1)S(1)}, u32[]{:S(2)}, u32[]{:S(2)}) collective-permute-start(bf16[2,4,256,128]{3,2,1,0:T(8,128)(2,1)S(1)} %get-tuple-element.63), channel_id=1, source_target_pairs={{0,2},{2,4},{4,6},{6,8},{8,10},{10,12},{12,14},{14,16},{16,18},{18... | collective-permute-start | bytes 1572872 | tf_op jit(solution)/shard_map/ppermute | solution.py:161
  38.1 24.4 %collective-permute-start.3 = (bf16[2,4,256,128]{3,2,1,0:T(8,128)(2,1)S(1)}, bf16[2,4,256,128]{3,2,1,0:T(8,128)(2,1)S(1)}, u32[]{:S(2)}, u32[]{:S(2)}) collective-permute-start(bf16[2,4,256,128]{3,2,1,0:T(8,128)(2,1)S(1)} %get-tuple-element.48), channel_id=1, source_target_pairs={{0,1},{1,0},{2,3},{3,2},{4,5},{5,4},{6,7},{7,6},{8,9},{9,8},{10,11... | collective-permute-start | bytes 1572872 | tf_op jit(solution)/shard_map/ppermute | solution.py:165
  43.4 19.0 %collective-permute-start.5 = (bf16[2,4,256,128]{3,2,1,0:T(8,128)(2,1)S(1)}, bf16[2,4,256,128]{3,2,1,0:T(8,128)(2,1)S(1)}, u32[]{:S(2)}, u32[]{:S(2)}) collective-permute-start(bf16[2,4,256,128]{3,2,1,0:T(8,128)(2,1)S(1)} %add_convert_fusion), channel_id=1, source_target_pairs={{0,1},{1,0},{2,3},{3,2},{4,5},{5,4},{6,7},{7,6},{8,9},{9,8},{10,11... | collective-permute-start | bytes 1572872 | tf_op jit(solution)/shard_map/ppermute | solution.py:165
  60.5 11.2 %collective-permute-start.6 = (bf16[2,4,256,128]{3,2,1,0:T(8,128)(2,1)S(1)}, bf16[2,4,256,128]{3,2,1,0:T(8,128)(2,1)S(1)}, u32[]{:S(2)}, u32[]{:S(2)}) collective-permute-start(bf16[2,4,256,128]{3,2,1,0:T(8,128)(2,1)S(1)} %get-tuple-element.50), channel_id=1, source_target_pairs={{2,0},{4,2},{6,4},{8,6},{10,8},{12,10},{14,12},{16,14},{18,16},{20... | collective-permute-start | bytes 1572872 | tf_op jit(solution)/shard_map/ppermute | solution.py:161

commit v2 on v0

v2 whole, which is shorter than its diff:
```python
import functools

import jax
import jax.numpy as jnp
from jax import lax
from jax.experimental import pallas as pl
from jax.experimental.pallas import tpu as pltpu
from jax.sharding import PartitionSpec as P

WINDOW = 256
CHUNK = WINDOW // 2
PAD = 8
LOG2E = 1.4426950408889634
F32 = jnp.float32
BF16 = jnp.bfloat16
VMEM = pl.BlockSpec(memory_space=pltpu.VMEM)
SMEM = pl.BlockSpec(memory_space=pltpu.SMEM)
ANY = pl.BlockSpec(memory_space=pl.ANY)
MIB = 1024 * 1024


def dot(a, b, contract):
    return lax.dot_general(a, b, (((contract[0],), (contract[1],)), ((), ())), preferred_element_type=F32)


def params(limit):
    return pltpu.CompilerParams(vmem_limit_bytes=limit * MIB)


def count_smaller(column, row):
    return jnp.sum((column < row).astype(F32), axis=0, keepdims=True)


def prepare_kernel(sel_ref, key_ref, value_ref, docs_ref, kv_ref, other_ref, mine_ref):
    half = other_ref.shape[1]
    tokens = key_ref.shape[0]
    kv_ref[0] = jnp.transpose(key_ref[...], (1, 0, 2))
    kv_ref[1] = jnp.transpose(value_ref[...], (1, 0, 2))
    tail = docs_ref[...].astype(BF16)
    for part, out in ((0, other_ref), (1, mine_ref)):
        first = sel_ref[part] * half
        for i in range(2):
            for h in range(half):
                out[i, h, :WINDOW] = kv_ref[i, first + h, tokens - WINDOW :]
                out[i, h, WINDOW:] = tail


def half_grads(chunks, get_q, get_do, get_keys, get_low, scale, group, put_dq, put_block):
    cols = CHUNK * group
    row = lax.broadcasted_iota(jnp.int32, (CHUNK, cols), 0)
    token = lax.broadcasted_iota(jnp.int32, (CHUNK, cols), 1) & (CHUNK - 1)
    old = row > token
    old_low = old.astype(F32).astype(BF16)
    new_low = 1 - old_low
    position = jnp.where(old, row, row + 2 * CHUNK)
    middle = row + CHUNK
    qs, dos, dqs = {}, {}, {}
    heads = None
    sums = {}
    state = {}

    def fetch(c):
        qs[c], dos[c] = get_q(c), get_do(c)

    fetch(0)
    heads = qs[0].shape[0] // group
    items = [(c, h) for c in range(len(chunks)) for h in range(heads)]

    def scores(item):
        c, h = item
        if c not in qs:
            fetch(c)
        q = qs[c][h * group : (h + 1) * group].reshape(cols, -1)
        do = dos[c][h * group : (h + 1) * group].reshape(cols, -1)
        k, v = get_keys(h, c)
        state[item] = (q, do, k, dot(k, q, (1, 1)), dot(v, do, (1, 1)))

    def soft(item):
        c, h = item
        q, do, k, s, dp = state[item]
        low = get_low(c)
        s = [
            jnp.where(position >= low, jnp.where(old, s[:CHUNK], s[2 * CHUNK :]), -1e30),
            jnp.where(middle >= low, s[CHUNK : 2 * CHUNK], -1e30),
        ]
        dp = [jnp.where(old, dp[:CHUNK], dp[2 * CHUNK :]), dp[CHUNK : 2 * CHUNK]]
        top = functools.reduce(jnp.maximum, [jnp.max(x, axis=0, keepdims=True) for x in s])
        w = [jnp.exp2((x - top) * (scale * LOG2E)) for x in s]
        total = sum(jnp.sum(x, axis=0, keepdims=True) for x in w)
        inverse = 1.0 / total
        p = [x * inverse for x in w]
        delta = sum(jnp.sum(x * y, axis=0, keepdims=True) for x, y in zip(p, dp))
        ds = [(x * (y - delta)).astype(BF16) for x, y in zip(p, dp)]
        p = [x.astype(BF16) for x in p]
        p = jnp.concatenate([p[0] * old_low, p[1], p[0] * new_low], 0)
        ds = jnp.concatenate([ds[0] * old_low, ds[1], ds[0] * new_low], 0)
        state[item] = (q, do, k, p, ds)

    def grads(item):
        c, h = item
        q, do, k, p, ds = state.pop(item)
        dv = dot(p, do, (1, 0))
        dk = dot(ds, q, (1, 0))
        for b in range(3):
            rows = slice(b * CHUNK, (b + 1) * CHUNK)
            key = (h, c + b)
            new = (dk[rows], dv[rows])
            if key in sums:
                new = (sums[key][0] + new[0], sums[key][1] + new[1])
            sums[key] = new
            if b == 0 or c == len(chunks) - 1:
                put_block(h, c + b, *sums.pop(key))
        dqs[item] = (dot(k.T, ds, (1, 0)) * scale).T.astype(BF16).reshape(group, CHUNK, -1)
        if h == heads - 1:
            full = jnp.concatenate([dqs.pop((c, i)) for i in range(heads)], 0)
            put_dq(c, jnp.transpose(full, (1, 0, 2)))

    scores(items[0])
    for n, item in enumerate(items):
        if n + 1 < len(items):
            scores(items[n + 1])
        if n:
            grads(items[n - 1])
        soft(item)
    grads(items[-1])


def store_rows(buf, sem, slot, dq_ref, rows, where):
    return pltpu.make_async_copy(buf.at[slot], dq_ref.at[rows, where, :], sem.at[slot])


def late_kernel(sel_ref, low_ref, q_ref, do_ref, kv_ref, dq_ref, part_ref, buf, sem, *, chunks, group):
    half = part_ref.shape[2]
    rows = half * group
    scale = 1.0 / q_ref.shape[-1] ** 0.5

    def one(n, carry):
        sel = sel_ref[n]
        where = pl.ds(pl.multiple_of(sel * rows, rows), rows)

        def tokens(c):
            return slice(chunks[c] * CHUNK, (chunks[c] + 1) * CHUNK)

        def put_dq(c, value):
            slot = n * len(chunks) + c
            buf[slot] = value
            store_rows(buf, sem, slot, dq_ref, tokens(c), where).start()

        def get_keys(h, c):
            keys = slice((chunks[c] - 2) * CHUNK, (chunks[c] + 1) * CHUNK)
            return kv_ref[0, sel * half + h, keys], kv_ref[1, sel * half + h, keys]

        def put_block(h, b, dk, dv):
            block = slice((chunks[0] - 2 + b) * CHUNK, (chunks[0] - 1 + b) * CHUNK)
            part_ref[n, 0, h, block] = dk * scale
            part_ref[n, 1, h, block] = dv

        half_grads(
            chunks,
            lambda c: jnp.transpose(q_ref[tokens(c), where, :], (1, 0, 2)),
            lambda c: jnp.transpose(do_ref[tokens(c), where, :], (1, 0, 2)),
            get_keys,
            lambda c: low_ref[chunks[c] : chunks[c] + 1, :],
            scale,
            group,
            put_dq,
            put_block,
        )
        return carry

    lax.fori_loop(0, 2, one, 0)
    for n in range(2):
        for c, chunk in enumerate(chunks):
            rows_of = slice(chunk * CHUNK, (chunk + 1) * CHUNK)
            store_rows(buf, sem, n * len(chunks) + c, dq_ref, rows_of, slice(0, rows)).wait()


def early_kernel(
    sel_ref, docs_ref, low_ref, q_ref, do_ref, kv_ref, halo_ref, part_ref, dq_in, dq_ref, own_ref, back_ref, buf, sem, *, group, n
):
    half = own_ref.shape[1]
    rows = half * group
    scale = 1.0 / q_ref.shape[-1] ** 0.5
    sel = sel_ref[n]
    where = pl.ds(pl.multiple_of(sel * rows, rows), rows)
    before = jnp.where(sel_ref[2] == 0, -1.0, halo_ref[0, 0, WINDOW:].astype(F32)).T
    lows = []
    for c in range(2):
        docs = docs_ref[c : c + 1, :]
        count = count_smaller(before[:, :1], docs) + count_smaller(before[:, 1:2], docs)
        count = jnp.concatenate([count] * group, 1)
        lows.append(low_ref[c : c + 1, :] - WINDOW + count.astype(jnp.int32))

    def tokens(c):
        return slice(c * CHUNK, (c + 1) * CHUNK)

    def put_dq(c, value):
        buf[c] = value
        store_rows(buf, sem, c, dq_ref, tokens(c), where).start()

    def get_keys(h, c):
        return tuple(
            jnp.concatenate(
                [halo_ref[i, h, c * CHUNK : WINDOW], kv_ref[i, sel * half + h, : (c + 1) * CHUNK]], 0
            )
            for i in range(2)
        )

    def put_block(h, b, dk, dv):
        dk = dk * scale
        if b < 2:
            block = slice(b * CHUNK, (b + 1) * CHUNK)
            back_ref[0, h, block] = dk.astype(BF16)
            back_ref[1, h, block] = dv.astype(BF16)
        else:
            block = slice((b - 2) * CHUNK, (b - 1) * CHUNK)
            own_ref[0, h, block] = (dk + part_ref[n, 0, h, block]).astype(own_ref.dtype)
            own_ref[1, h, block] = (dv + part_ref[n, 1, h, block]).astype(own_ref.dtype)

    half_grads(
        (0, 1),
        lambda c: jnp.transpose(q_ref[tokens(c), where, :], (1, 0, 2)),
        lambda c: jnp.transpose(do_ref[tokens(c), where, :], (1, 0, 2)),
        get_keys,
        lambda c: lows[c],
        scale,
        group,
        put_dq,
        put_block,
    )
    for c in range(2):
        store_rows(buf, sem, c, dq_ref, tokens(c), where).wait()


def finish_kernel(first_ref, first_in, part_ref, last_in, back_in, dk_ref, dv_ref, *, n):
    tokens = dk_ref.shape[0]
    for i, out in ((0, dk_ref), (1, dv_ref)):
        value = first_ref[i] + first_in[i].astype(F32)
        out[:WINDOW] = jnp.transpose(value.astype(BF16), (1, 0, 2))
        late = part_ref[n, i, :, WINDOW:] + last_in[i].astype(F32)
        value = late[:, tokens - 2 * WINDOW :] + back_in[i].astype(F32)
        if tokens > 2 * WINDOW:
            value = jnp.concatenate([late[:, : tokens - 2 * WINDOW], value], 1)
        out[WINDOW:] = jnp.transpose(value.astype(BF16), (1, 0, 2))


def shift(block, axis, distance):
    devices = range(lax.axis_size(axis))
    return lax.ppermute(block, axis, [(i - distance, i) for i in devices if i - distance in devices])


def swap(block):
    return lax.ppermute(block, "head", [(0, 1), (1, 0)])


def on_device(queries, key_heads, value_heads, out_grad, doc_ids):
    tokens, kv_count, group, size = queries.shape
    half = kv_count // 2
    chunks = tokens // CHUNK
    shape = jax.ShapeDtypeStruct
    head = lax.axis_index("head")
    sel = jnp.stack([1 - head, head, lax.axis_index("ctx")]).astype(jnp.int32)
    rows = queries.reshape(tokens, kv_count * group, size)
    grads = out_grad.reshape(tokens, kv_count * group, size)
    docs = doc_ids.reshape(chunks, CHUNK).astype(F32)
    tail = jnp.pad(docs[chunks - 2 :], ((0, PAD - 2), (0, 0)))
    halo_shape = shape((2, half, WINDOW + PAD, size), BF16)
    kv, halo_other, halo_mine = pl.pallas_call(
        prepare_kernel,
        in_specs=[SMEM, VMEM, VMEM, VMEM],
        out_specs=[VMEM] * 3,
        out_shape=[shape((2, kv_count, tokens, size), BF16), halo_shape, halo_shape],
        compiler_params=params(16),
        name="prepare",
    )(sel, key_heads, value_heads, tail)
    halo_other = shift(halo_other, "ctx", 1)
    halo_mine = shift(halo_mine, "ctx", 1)

    smaller = jnp.sum((doc_ids[:, None] < doc_ids[None, :]).astype(jnp.int32), axis=0)
    low = smaller.reshape(chunks, CHUNK) + (WINDOW - CHUNK * jnp.arange(chunks, dtype=jnp.int32)[:, None])
    low = jnp.concatenate([low] * group, 1)

    def cost(n):
        work = n * 10 * CHUNK * group * (WINDOW + CHUNK) * size
        return pl.CostEstimate(flops=work * 10, bytes_accessed=n * CHUNK * group * size * 8, transcendentals=0)

    def staging(n):
        return [pltpu.VMEM((n, CHUNK, half * group, size), BF16), pltpu.SemaphoreType.DMA((n,))]

    late = tuple(range(2, chunks))
    query_grad, part = pl.pallas_call(
        functools.partial(late_kernel, chunks=late, group=group),
        in_specs=[SMEM] + [VMEM] * 4,
        out_specs=[ANY, VMEM],
        out_shape=[shape(rows.shape, BF16), shape((2, 2, half, tokens, size), F32)],
        scratch_shapes=staging(2 * len(late)),
        compiler_params=params(24),
        cost_estimate=cost(kv_count * len(late)),
        name="late",
    )(sel, low, rows, grads, kv)

    def early(n, halo, query_grad, emit):
        return pl.pallas_call(
            functools.partial(early_kernel, group=group, n=n),
            in_specs=[SMEM] + [VMEM] * 7 + [ANY],
            out_specs=[ANY, VMEM, VMEM],
            scratch_shapes=staging(2),
            out_shape=[
                shape(rows.shape, BF16),
                shape((2, half, WINDOW, size), emit),
                shape((2, half, WINDOW, size), BF16),
            ],
            input_output_aliases={8: 0},
            compiler_params=params(24),
            cost_estimate=cost(half * 2),
            name="early",
        )(sel, docs, low, rows, grads, kv, halo, part, query_grad)

    query_grad, first_other, back_other = early(0, halo_other, query_grad, BF16)
    first_other = swap(first_other)
    back_other = shift(back_other, "ctx", -1)
    query_grad, first_mine, back_mine = early(1, halo_mine, query_grad, F32)
    back_mine = shift(back_mine, "ctx", -1)
    back_other, _ = lax.optimization_barrier((back_other, first_mine))
    last_other = part[0, :, :, WINDOW:]
    last_other = last_other.at[:, :, tokens - 2 * WINDOW :].add(back_other.astype(F32))
    last_other = swap(last_other.astype(BF16))
    out = shape((tokens, half, size), BF16)
    key_grad, value_grad = pl.pallas_call(
        functools.partial(finish_kernel, n=1),
        in_specs=[VMEM] * 5,
        out_specs=[VMEM] * 2,
        out_shape=[out, out],
        compiler_params=params(16),
        name="finish",
    )(first_mine, first_other, part, last_other, back_mine)
    return query_grad.reshape(queries.shape), key_grad, value_grad


def solution(mesh):
    in_specs = (
        P("ctx", None, "head", None),
        P("ctx", None, None),
        P("ctx", None, None),
        P("ctx", None, "head", None),
        P("ctx"),
    )
    out_specs = (P("ctx", None, "head", None), P("ctx", "head", None), P("ctx", "head", None))
    return jax.shard_map(on_device, mesh=mesh, in_specs=in_specs, out_specs=out_specs, check_vma=False)
```

time: 278 us -> 62.3 us (0.22)
  the two profiles are of different devices: /device:TPU:1 before, /device:TPU:16 now
where the time goes in v2:
time: 62.3 us; the launch traced here: 61.9 us
  waiting for transfers between devices  25.7 us (41%)
  Pallas kernels  18.2 us (29%)
  starting transfers between devices  12 us (19%)
  local copies, waits for them, and re-layouts  4.07 us (7%)
  other arithmetic  1.19 us (2%)
  between operations  0.74 us (1%)
    ppermute x2, waiting for transfers between devices, swap(): return lax.ppermute(block, 'head', [(0, 1), (1, 0)])  18.4 us
    ppermute x4, starting transfers between devices, shift(): lax.ppermute(block, axis, [(i - distance, i) for i in devices if i - dist...  9.86 us
    pallas_call x2, Pallas kernels, early(): pl.pallas_call(functools.partial(early_kernel, group=group, n=n), in_spec...  8.57 us
    ppermute x4, waiting for transfers between devices, shift(): lax.ppermute(block, axis, [(i - distance, i) for i in devices if i - dist...  7.35 us
    pallas_call x1, Pallas kernels, on_device(): pl.pallas_call(functools.partial(late_kernel, chunks=late, group=group),...  7.07 us
    unnamed x10, local copies, waits for them, and re-layouts  4.05 us
    ppermute x2, starting transfers between devices, swap(): return lax.ppermute(block, 'head', [(0, 1), (1, 0)])  2.16 us
    pallas_call x1, Pallas kernels, on_device(): pl.pallas_call(functools.partial(finish_kernel, n=1), in_specs=[VMEM] * 5...  1.42 us
  transfers between devices with their start and end apart: 6, of which 4 were waited for; matrix products, arithmetic and copies ran while one was open for 1% of the time, Pallas kernels for 25%

profile of v2, /device:TPU:16, one launch (start us, length us, event | category | flops | bytes accessed | tf_op | source)
XLA Modules:
  0.0 61.9 jit_solution(15209598763121679149)
XLA Ops:
  0.6 0.0 copy-start.4
  0.6 0.7 %fusion.1 = (f32[512]{0:T(512)S(1)}, f32[4,128]{1,0:T(4,128)S(1)}) fusion(s32[512]{0:T(512)} %param.13), kind=kLoop, calls=%fused_computation.9 | loop fusion | flops 512 | bytes 6144 | tf_op jit(solution)/shard_map/convert_element_type | solution.py:265
  1.4 0.1 pad_add_fusion.1.sel_ref
  1.5 0.0 copy-start
  1.5 1.2 %copy-done = bf16[512,8,128]{2,1,0:T(8,128)(2,1)S(1)} copy-done((bf16[512,8,128]{2,1,0:T(8,128)(2,1)S(1)}, bf16[512,8,128]{2,1,0:T(8,128)(2,1)}, u32[]{:S(2)}) %copy-start) | copy-done | bytes 1048600
  2.7 0.0 copy-start.1
  2.7 1.2 %copy-done.1 = bf16[512,8,128]{2,1,0:T(8,128)(2,1)S(1)} copy-done((bf16[512,8,128]{2,1,0:T(8,128)(2,1)S(1)}, bf16[512,8,128]{2,1,0:T(8,128)(2,1)}, u32[]{:S(2)}) %copy-start.1) | copy-done | bytes 1048600
  3.9 0.0 copy-start.2
  3.9 1.1 %prepare.1 = (bf16[2,8,512,128]{3,2,1,0:T(8,128)(2,1)S(1)}, bf16[2,4,264,128]{3,2,1,0:T(8,128)(2,1)S(1)}, bf16[2,4,264,128]{3,2,1,0:T(8,128)(2,1)S(1)}) custom-call(s32[3]{0:T(128)S(1)} %pad_add_fusion.1.sel_ref, bf16[512,8,128]{2,1,0:T(8,128)(2,1)S(1)} %copy-done, bf16[512,8,128]{2,1,0:T(8,128)(2,1)S(1)} %copy-done.1, f32[8,128]{1,0:T(8,128)S(1)} %pad.7.docs_ref), custom_call_target="tpu_custom_call" | custom-call | tf_op jit(solution)/shard_map/prepare/pallas_call | solution.py:268
  5.1 1.9 %collective-permute-start = (bf16[2,4,264,128]{3,2,1,0:T(8,128)(2,1)S(1)}, bf16[2,4,264,128]{3,2,1,0:T(8,128)(2,1)S(1)}, u32[]{:S(2)}, u32[]{:S(2)}) collective-permute-start(bf16[2,4,264,128]{3,2,1,0:T(8,128)(2,1)S(1)} %get-tuple-element.38), channel_id=1, source_target_pairs={{0,2},{2,4},{4,6},{6,8},{8,10},{10,12},{12,14},{14,16},{16,18},{18... | collective-permute-start | bytes 1622024 | tf_op jit(solution)/shard_map/ppermute | solution.py:249
  7.0 3.5 %collective-permute-start.1 = (bf16[2,4,264,128]{3,2,1,0:T(8,128)(2,1)S(1)}, bf16[2,4,264,128]{3,2,1,0:T(8,128)(2,1)S(1)}, u32[]{:S(2)}, u32[]{:S(2)}) collective-permute-start(bf16[2,4,264,128]{3,2,1,0:T(8,128)(2,1)S(1)} %get-tuple-element.40), channel_id=1, source_target_pairs={{0,2},{2,4},{4,6},{6,8},{8,10},{10,12},{12,14},{14,16},{16,18},{18... | collective-permute-start | bytes 1622024 | tf_op jit(solution)/shard_map/ppermute | solution.py:249
  10.6 0.0 copy-done.4
  10.6 0.2 convert_reduce_fusion
  10.7 0.1 bitcast_add_fusion.1
  10.8 0.0 copy-done.2
  10.8 0.0 copy-start.3
  10.8 1.6 %copy-done.3 = bf16[512,8,2,128]{3,2,1,0:T(2,128)(2,1)S(1)} copy-done((bf16[512,8,2,128]{3,2,1,0:T(2,128)(2,1)S(1)}, bf16[512,8,2,128]{3,2,1,0:T(2,128)(2,1)}, u32[]{:S(2)}) %copy-start.3) | copy-done | bytes 2097176
  12.4 7.1 %late.1 = (bf16[512,16,128]{2,1,0:T(8,128)(2,1)}, f32[2,2,4,512,128]{4,3,2,1,0:T(8,128)S(1)}) custom-call(s32[3]{0:T(128)S(1)} %pad_add_fusion.1.sel_ref, s32[4,256]{1,0:T(4,128)S(1)} %pad_add_fusion.low_ref, bf16[512,16,128]{2,1,0:T(8,128)(2,1)S(1)} %bitcast.16, bf16[512,16,128]{2,1,0:T(8,128)(2,1)S(1)} %bitcast.19, ...), custom_call_target="tpu_custom_call" | custom-call | flops 20132659200 | bytes 4194304 | tf_op jit(solution)/shard_map/late/pallas_call | solution.py:291
  19.5 2.9 %collective-permute-done.1.halo_ref = bf16[2,4,264,128]{3,2,1,0:T(8,128)(2,1)S(1)} collective-permute-done((bf16[2,4,264,128]{3,2,1,0:T(8,128)(2,1)S(1)}, bf16[2,4,264,128]{3,2,1,0:T(8,128)(2,1)S(1)}, u32[]{:S(2)}, u32[]{:S(2)}) %collective-permute-start.1) | collective-permute-done | bytes 540704 | tf_op jit(solution)/shard_map/ppermute | solution.py:249
  22.4 4.3 %early.2 = (bf16[512,16,128]{2,1,0:T(8,128)(2,1)}, bf16[2,4,256,128]{3,2,1,0:T(8,128)(2,1)S(1)}, bf16[2,4,256,128]{3,2,1,0:T(8,128)(2,1)S(1)}) custom-call(s32[3]{0:T(128)S(1)} %pad_add_fusion.1.sel_ref, f32[4,128]{1,0:T(4,128)S(1)} %get-tuple-element.52.docs_ref, s32[4,256]{1,0:T(4,128)S(1)} %pad_add_fusion.low_ref, ...), custom_call_target="tpu_custom_call", output_to_operand_aliasing={{0}: (8, {})} | custom-call | flops 10066329600 | bytes 2097152 | tf_op jit(solution)/shard_map/early/pallas_call | solution.py:303
  26.7 1.9 %collective-permute-start.3 = (bf16[2,4,256,128]{3,2,1,0:T(8,128)(2,1)S(1)}, bf16[2,4,256,128]{3,2,1,0:T(8,128)(2,1)S(1)}, u32[]{:S(2)}, u32[]{:S(2)}) collective-permute-start(bf16[2,4,256,128]{3,2,1,0:T(8,128)(2,1)S(1)} %get-tuple-element.46), channel_id=1, source_target_pairs={{2,0},{4,2},{6,4},{8,6},{10,8},{12,10},{14,12},{16,14},{18,16},{20... | collective-permute-start | bytes 1572872 | tf_op jit(solution)/shard_map/ppermute | solution.py:249
  28.7 0.0 collective-permute-done.halo_ref
  28.7 4.3 %early.3 = (bf16[512,16,128]{2,1,0:T(8,128)(2,1)}, f32[2,4,256,128]{3,2,1,0:T(8,128)S(1)}, bf16[2,4,256,128]{3,2,1,0:T(8,128)(2,1)S(1)}) custom-call(s32[3]{0:T(128)S(1)} %pad_add_fusion.1.sel_ref, f32[4,128]{1,0:T(4,128)S(1)} %get-tuple-element.52.docs_ref, s32[4,256]{1,0:T(4,128)S(1)} %pad_add_fusion.low_ref, ...), custom_call_target="tpu_custom_call", output_to_operand_aliasing={{0}: (8, {})} | custom-call | flops 10066329600 | bytes 2097152 | tf_op jit(solution)/shard_map/early/pallas_call | solution.py:303
  33.0 2.5 %collective-permute-start.5 = (bf16[2,4,256,128]{3,2,1,0:T(8,128)(2,1)S(1)}, bf16[2,4,256,128]{3,2,1,0:T(8,128)(2,1)S(1)}, u32[]{:S(2)}, u32[]{:S(2)}) collective-permute-start(bf16[2,4,256,128]{3,2,1,0:T(8,128)(2,1)S(1)} %get-tuple-element.48), channel_id=1, source_target_pairs={{2,0},{4,2},{6,4},{8,6},{10,8},{12,10},{14,12},{16,14},{18,16},{20... | collective-permute-start | bytes 1572872 | tf_op jit(solution)/shard_map/ppermute | solution.py:249
  35.5 1.6 %collective-permute-start.2 = (bf16[2,4,256,128]{3,2,1,0:T(8,128)(2,1)S(1)}, bf16[2,4,256,128]{3,2,1,0:T(8,128)(2,1)S(1)}, u32[]{:S(2)}, u32[]{:S(2)}) collective-permute-start(bf16[2,4,256,128]{3,2,1,0:T(8,128)(2,1)S(1)} %get-tuple-element.45), channel_id=1, source_target_pairs={{0,1},{1,0},{2,3},{3,2},{4,5},{5,4},{6,7},{7,6},{8,9},{9,8},{10,11... | collective-permute-start | bytes 1572872 | tf_op jit(solution)/shard_map/ppermute | solution.py:253
  37.0 0.0 collective-permute-done.3
  37.0 0.1 fusion
  37.1 0.6 collective-permute-start.4
  37.7 4.4 %collective-permute-done.5.back_in = bf16[2,4,256,128]{3,2,1,0:T(8,128)(2,1)S(1)} collective-permute-done((bf16[2,4,256,128]{3,2,1,0:T(8,128)(2,1)S(1)}, bf16[2,4,256,128]{3,2,1,0:T(8,128)(2,1)S(1)}, u32[]{:S(2)}, u32[]{:S(2)}) %collective-permute-start.5) | collective-permute-done | bytes 524320 | tf_op jit(solution)/shard_map/ppermute | solution.py:249
  42.1 8.2 %collective-permute-done.2.first_in = bf16[2,4,256,128]{3,2,1,0:T(8,128)(2,1)S(1)} collective-permute-done((bf16[2,4,256,128]{3,2,1,0:T(8,128)(2,1)S(1)}, bf16[2,4,256,128]{3,2,1,0:T(8,128)(2,1)S(1)}, u32[]{:S(2)}, u32[]{:S(2)}) %collective-permute-start.2) | collective-permute-done | bytes 524320 | tf_op jit(solution)/shard_map/ppermute | solution.py:253
  50.3 10.2 %collective-permute-done.4.last_in = bf16[2,4,256,128]{3,2,1,0:T(8,128)(2,1)S(1)} collective-permute-done((bf16[2,4,256,128]{3,2,1,0:T(8,128)(2,1)S(1)}, bf16[2,4,256,128]{3,2,1,0:T(8,128)(2,1)S(1)}, u32[]{:S(2)}, u32[]{:S(2)}) %collective-permute-start.4) | collective-permute-done | bytes 524320 | tf_op jit(solution)/shard_map/ppermute | solution.py:253
  60.5 1.4 %finish.1 = (bf16[512,4,128]{2,1,0:T(4,128)(2,1)}, bf16[512,4,128]{2,1,0:T(4,128)(2,1)}) custom-call(f32[2,4,256,128]{3,2,1,0:T(8,128)S(1)} %get-tuple-element.44.first_ref, bf16[2,4,256,128]{3,2,1,0:T(8,128)(2,1)S(1)} %collective-permute-done.2.first_in, f32[2,2,4,512,128]{4,3,2,1,0:T(8,128)S(1)} %get-tuple-element.39.part_ref, ...), custom_call_target="tpu_custom_call" | custom-call | tf_op jit(solution)/shard_map/finish/pallas_call | solution.py:329
  (4 shorter events, 0.0 us)
Async XLA Ops:
  0.6 9.9 %copy-start.4 = (s32[512]{0:T(512)S(1)}, s32[512]{0:T(512)}, u32[]{:S(2)}) copy-start(s32[512]{0:T(512)} %param.13) | copy-start | bytes 6148
  1.5 1.2 %copy-start = (bf16[512,8,128]{2,1,0:T(8,128)(2,1)S(1)}, bf16[512,8,128]{2,1,0:T(8,128)(2,1)}, u32[]{:S(2)}) copy-start(bf16[512,8,128]{2,1,0:T(8,128)(2,1)} %key_ref.1) | copy-start | bytes 3145732
  2.7 1.2 %copy-start.1 = (bf16[512,8,128]{2,1,0:T(8,128)(2,1)S(1)}, bf16[512,8,128]{2,1,0:T(8,128)(2,1)}, u32[]{:S(2)}) copy-start(bf16[512,8,128]{2,1,0:T(8,128)(2,1)} %value_ref.1) | copy-start | bytes 3145732
  3.9 6.9 %copy-start.2 = (bf16[512,8,2,128]{3,2,1,0:T(2,128)(2,1)S(1)}, bf16[512,8,2,128]{3,2,1,0:T(2,128)(2,1)}, u32[]{:S(2)}) copy-start(bf16[512,8,2,128]{3,2,1,0:T(2,128)(2,1)} %param.9) | copy-start | bytes 6291460
  5.1 23.6 %collective-permute-start = (bf16[2,4,264,128]{3,2,1,0:T(8,128)(2,1)S(1)}, bf16[2,4,264,128]{3,2,1,0:T(8,128)(2,1)S(1)}, u32[]{:S(2)}, u32[]{:S(2)}) collective-permute-start(bf16[2,4,264,128]{3,2,1,0:T(8,128)(2,1)S(1)} %get-tuple-element.38), channel_id=1, source_target_pairs={{0,2},{2,4},{4,6},{6,8},{8,10},{10,12},{12,14},{14,16},{16,18},{18... | collective-permute-start | bytes 1622024 | tf_op jit(solution)/shard_map/ppermute | solution.py:249
  7.0 15.4 %collective-permute-start.1 = (bf16[2,4,264,128]{3,2,1,0:T(8,128)(2,1)S(1)}, bf16[2,4,264,128]{3,2,1,0:T(8,128)(2,1)S(1)}, u32[]{:S(2)}, u32[]{:S(2)}) collective-permute-start(bf16[2,4,264,128]{3,2,1,0:T(8,128)(2,1)S(1)} %get-tuple-element.40), channel_id=1, source_target_pairs={{0,2},{2,4},{4,6},{6,8},{8,10},{10,12},{12,14},{14,16},{16,18},{18... | collective-permute-start | bytes 1622024 | tf_op jit(solution)/shard_map/ppermute | solution.py:249
  10.8 1.6 %copy-start.3 = (bf16[512,8,2,128]{3,2,1,0:T(2,128)(2,1)S(1)}, bf16[512,8,2,128]{3,2,1,0:T(2,128)(2,1)}, u32[]{:S(2)}) copy-start(bf16[512,8,2,128]{3,2,1,0:T(2,128)(2,1)} %param.12) | copy-start | bytes 6291460
  26.7 10.3 %collective-permute-start.3 = (bf16[2,4,256,128]{3,2,1,0:T(8,128)(2,1)S(1)}, bf16[2,4,256,128]{3,2,1,0:T(8,128)(2,1)S(1)}, u32[]{:S(2)}, u32[]{:S(2)}) collective-permute-start(bf16[2,4,256,128]{3,2,1,0:T(8,128)(2,1)S(1)} %get-tuple-element.46), channel_id=1, source_target_pairs={{2,0},{4,2},{6,4},{8,6},{10,8},{12,10},{14,12},{16,14},{18,16},{20... | collective-permute-start | bytes 1572872 | tf_op jit(solution)/shard_map/ppermute | solution.py:249
  33.0 9.2 %collective-permute-start.5 = (bf16[2,4,256,128]{3,2,1,0:T(8,128)(2,1)S(1)}, bf16[2,4,256,128]{3,2,1,0:T(8,128)(2,1)S(1)}, u32[]{:S(2)}, u32[]{:S(2)}) collective-permute-start(bf16[2,4,256,128]{3,2,1,0:T(8,128)(2,1)S(1)} %get-tuple-element.48), channel_id=1, source_target_pairs={{2,0},{4,2},{6,4},{8,6},{10,8},{12,10},{14,12},{16,14},{18,16},{20... | collective-permute-start | bytes 1572872 | tf_op jit(solution)/shard_map/ppermute | solution.py:249
  35.5 14.9 %collective-permute-start.2 = (bf16[2,4,256,128]{3,2,1,0:T(8,128)(2,1)S(1)}, bf16[2,4,256,128]{3,2,1,0:T(8,128)(2,1)S(1)}, u32[]{:S(2)}, u32[]{:S(2)}) collective-permute-start(bf16[2,4,256,128]{3,2,1,0:T(8,128)(2,1)S(1)} %get-tuple-element.45), channel_id=1, source_target_pairs={{0,1},{1,0},{2,3},{3,2},{4,5},{5,4},{6,7},{7,6},{8,9},{9,8},{10,11... | collective-permute-start | bytes 1572872 | tf_op jit(solution)/shard_map/ppermute | solution.py:253
  37.1 23.4 %collective-permute-start.4 = (bf16[2,4,256,128]{3,2,1,0:T(8,128)(2,1)S(1)}, bf16[2,4,256,128]{3,2,1,0:T(8,128)(2,1)S(1)}, u32[]{:S(2)}, u32[]{:S(2)}) collective-permute-start(bf16[2,4,256,128]{3,2,1,0:T(8,128)(2,1)S(1)} %fusion), channel_id=1, source_target_pairs={{0,1},{1,0},{2,3},{3,2},{4,5},{5,4},{6,7},{7,6},{8,9},{9,8},{10,11... | collective-permute-start | bytes 1572872 | tf_op jit(solution)/shard_map/ppermute | solution.py:253

commit v3 on v2

v3 whole, which is shorter than its diff:
```python
import functools

import jax
import jax.numpy as jnp
from jax import lax
from jax.experimental import pallas as pl
from jax.experimental.pallas import tpu as pltpu
from jax.sharding import PartitionSpec as P


WINDOW = 256
CHUNK = WINDOW // 2
PAD = 8
LOG2E = 1.4426950408889634
F32 = jnp.float32
BF16 = jnp.bfloat16
VMEM = pl.BlockSpec(memory_space=pltpu.VMEM)
SMEM = pl.BlockSpec(memory_space=pltpu.SMEM)
ANY = pl.BlockSpec(memory_space=pl.ANY)
HBM = pl.BlockSpec(memory_space=pltpu.HBM)
MIB = 1024 * 1024


def dot(a, b, contract):
    return lax.dot_general(a, b, (((contract[0],), (contract[1],)), ((), ())), preferred_element_type=F32)


def params(limit):
    return pltpu.CompilerParams(vmem_limit_bytes=limit * MIB)


def count_smaller(column, row):
    return jnp.sum((column < row).astype(F32), axis=0, keepdims=True)


def tail_kernel(sel_ref, key_ref, value_ref, docs_ref, kv_ref, halo_ref, buf, sem):
    half = halo_ref.shape[1]
    chunks = docs_ref.shape[0]
    first = key_ref.shape[0] - WINDOW
    copies = [
        pltpu.make_async_copy(ref.at[pl.ds(first, WINDOW)], buf.at[i], sem.at[i])
        for i, ref in enumerate((key_ref, value_ref))
    ]
    for copy in copies:
        copy.start()
    pad = jnp.zeros((PAD - 2, CHUNK), BF16)
    tail = jnp.concatenate([docs_ref[chunks - 2 :].astype(F32).astype(BF16), pad], 0)
    for i in range(2):
        copies[i].wait()
        kv_ref[i] = jnp.transpose(buf[i], (1, 0, 2))
        for h in range(half):
            halo_ref[i, h, :WINDOW] = kv_ref[i, sel_ref[0] * half + h]
            halo_ref[i, h, WINDOW:] = tail


def rest_kernel(sel_ref, key_ref, value_ref, docs_ref, tail_ref, kv_ref, halo_ref, low_ref, buf, sem, *, group):
    half = halo_ref.shape[1]
    chunks = docs_ref.shape[0]
    rest = kv_ref.shape[2]
    copies = [
        pltpu.make_async_copy(ref.at[pl.ds(0, rest)], buf.at[i], sem.at[i])
        for i, ref in enumerate((key_ref, value_ref))
    ]
    for copy in copies:
        copy.start()
    docs = docs_ref[...].astype(F32)
    columns = docs.T
    for c in range(chunks):
        row = docs[c : c + 1]
        count = sum(count_smaller(columns[:, b : b + 1], row) for b in range(c + 1))
        low = count.astype(jnp.int32) + (WINDOW - c * CHUNK)
        low_ref[c : c + 1, :] = jnp.concatenate([low] * group, 1)
    pad = jnp.zeros((PAD - 2, CHUNK), BF16)
    tail = jnp.concatenate([docs[chunks - 2 :].astype(BF16), pad], 0)
    for i in range(2):
        for h in range(half):
            halo_ref[i, h, :WINDOW] = tail_ref[i, sel_ref[1] * half + h]
            halo_ref[i, h, WINDOW:] = tail
    for i in range(2):
        copies[i].wait()
        kv_ref[i] = jnp.transpose(buf[i], (1, 0, 2))


def half_grads(items, get_query, get_keys, get_low, scale, group, put_dq, put_block):
    cols = CHUNK * group
    row = lax.broadcasted_iota(jnp.int32, (CHUNK, cols), 0)
    token = lax.broadcasted_iota(jnp.int32, (CHUNK, cols), 1) & (CHUNK - 1)
    old = row > token
    old_low = old.astype(F32).astype(BF16)
    new_low = 1 - old_low
    position = jnp.where(old, row, row + 2 * CHUNK)
    middle = row + CHUNK
    dqs, sums, state, left = {}, {}, {}, {}
    for c, h, _, _, keys in items:
        for b in range(3 * keys):
            left[h, c + b] = left.get((h, c + b), 0) + 1
    pending = {}
    for c, h, _, query, _ in items:
        pending[c] = pending.get(c, 0) + query

    def scores(item):
        c, h, source, _, _ = item
        q, do = get_query(c, h, source)
        k, v = get_keys(h, c)
        state[item] = (q, do, k, dot(k, q, (1, 1)), dot(v, do, (1, 1)))

    def soft(item):
        q, do, k, s, dp = state[item]
        low = get_low(item[0])
        s = [
            jnp.where(position >= low, jnp.where(old, s[:CHUNK], s[2 * CHUNK :]), -1e30),
            jnp.where(middle >= low, s[CHUNK : 2 * CHUNK], -1e30),
        ]
        dp = [jnp.where(old, dp[:CHUNK], dp[2 * CHUNK :]), dp[CHUNK : 2 * CHUNK]]
        top = functools.reduce(jnp.maximum, [jnp.max(x, axis=0, keepdims=True) for x in s])
        w = [jnp.exp2((x - top) * (scale * LOG2E)) for x in s]
        total = sum(jnp.sum(x, axis=0, keepdims=True) for x in w)
        inverse = 1.0 / total
        p = [x * inverse for x in w]
        delta = sum(jnp.sum(x * y, axis=0, keepdims=True) for x, y in zip(p, dp))
        ds = [(x * (y - delta)).astype(BF16) for x, y in zip(p, dp)]
        p = [x.astype(BF16) for x in p]
        p = jnp.concatenate([p[0] * old_low, p[1], p[0] * new_low], 0) if item[4] else None
        ds = jnp.concatenate([ds[0] * old_low, ds[1], ds[0] * new_low], 0)
        state[item] = (q, do, k, p, ds)

    def grads(item):
        c, h, _, query, keys = item
        q, do, k, p, ds = state.pop(item)
        if keys:
            dv = dot(p, do, (1, 0))
            dk = dot(ds, q, (1, 0))
        for b in range(3 * keys):
            rows = slice(b * CHUNK, (b + 1) * CHUNK)
            key = (h, c + b)
            new = (dk[rows], dv[rows])
            if key in sums:
                new = (sums[key][0] + new[0], sums[key][1] + new[1])
            sums[key] = new
            left[key] -= 1
            if not left[key]:
                put_block(h, c + b, *sums.pop(key))
        if query:
            dqs[c, h] = (dot(k.T, ds, (1, 0)) * scale).T.astype(BF16).reshape(group, CHUNK, -1)
            pending[c] -= 1
            if not pending[c]:
                heads = sorted(i for a, i in dqs if a == c)
                full = jnp.concatenate([dqs.pop((c, i)) for i in heads], 0)
                put_dq(c, jnp.transpose(full, (1, 0, 2)))

    scores(items[0])
    for n, item in enumerate(items):
        if n + 1 < len(items):
            scores(items[n + 1])
        if n:
            grads(items[n - 1])
        soft(item)
    grads(items[-1])


def store_rows(buf, sem, slot, dq_ref, rows, where):
    return pltpu.make_async_copy(buf.at[slot], dq_ref.at[rows, where, :], sem.at[slot])


def run_half(sel, chunks, items, group, half, q_ref, do_ref, get_keys, get_low, scale, put_block, dq_ref, buf, sem):
    rows = half * group
    where = pl.ds(pl.multiple_of(sel * rows, rows), rows)
    held = {}

    def tokens(c):
        return slice(chunks[c] * CHUNK, (chunks[c] + 1) * CHUNK)

    def get_query(c, h, source):
        if c not in held:
            held[c] = [jnp.transpose(ref[tokens(c), where, :], (1, 0, 2)) for ref in (q_ref, do_ref)]
        return [x[h * group : (h + 1) * group].reshape(group * CHUNK, -1) for x in held[c]]

    def put_dq(c, value):
        buf[c] = value
        store_rows(buf, sem, c, dq_ref, tokens(c), where).start()

    half_grads(items, get_query, get_keys, get_low, scale, group, put_dq, put_block)
    for c in range(len(chunks)):
        store_rows(buf, sem, c, dq_ref, tokens(c), where).wait()


def all_items(chunks, half):
    return [(c, h, 0, True, True) for c in range(len(chunks)) for h in range(half)]


def late_kernel(sel_ref, low_ref, q_ref, do_ref, rest_ref, tail_ref, *refs, chunks, group, n):
    dq_ref, part_ref, buf, sem = refs[-4:]
    half = part_ref.shape[1]
    scale = 1.0 / q_ref.shape[-1] ** 0.5
    sel = sel_ref[n]
    rest = rest_ref.shape[2]

    def get_keys(h, c):
        start, stop = (chunks[c] - 2) * CHUNK, (chunks[c] + 1) * CHUNK
        pieces = []
        for i in range(2):
            parts = []
            if start < rest:
                parts.append(rest_ref[i, sel * half + h, start : min(stop, rest)])
            if stop > rest:
                parts.append(tail_ref[i, sel * half + h, max(start - rest, 0) : stop - rest])
            pieces.append(jnp.concatenate(parts, 0))
        return pieces

    def put_block(h, b, dk, dv):
        block = slice((chunks[0] - 2 + b) * CHUNK, (chunks[0] - 1 + b) * CHUNK)
        part_ref[0, h, block] = dk * scale
        part_ref[1, h, block] = dv

    def get_low(c):
        return low_ref[chunks[c] : chunks[c] + 1, :]

    items = all_items(chunks, half)
    run_half(sel, chunks, items, group, half, q_ref, do_ref, get_keys, get_low, scale, put_block, dq_ref, buf, sem)


def early_kernel(sel_ref, docs_ref, low_ref, q_ref, do_ref, rest_ref, halo_ref, *refs, group, n, carry):
    part_ref = refs[0] if carry else None
    dq_ref, own_ref, back_ref, buf, sem = refs[-5:]
    half = own_ref.shape[1]
    scale = 1.0 / q_ref.shape[-1] ** 0.5
    sel = sel_ref[n]
    before = jnp.where(sel_ref[2] == 0, -1.0, halo_ref[0, 0, WINDOW:].astype(F32)).T
    lows = []
    for c in range(2):
        docs = docs_ref[c : c + 1, :].astype(F32)
        count = count_smaller(before[:, :1], docs) + count_smaller(before[:, 1:2], docs)
        count = jnp.concatenate([count] * group, 1)
        lows.append(low_ref[c : c + 1, :] - WINDOW + count.astype(jnp.int32))

    def get_keys(h, c):
        return [
            jnp.concatenate(
                [halo_ref[i, h, c * CHUNK : WINDOW], rest_ref[i, sel * half + h, : (c + 1) * CHUNK]], 0
            )
            for i in range(2)
        ]

    def put_block(h, b, dk, dv):
        dk = dk * scale
        if b < 2:
            block = slice(b * CHUNK, (b + 1) * CHUNK)
            back_ref[0, h, block] = dk.astype(BF16)
            back_ref[1, h, block] = dv.astype(BF16)
        else:
            block = slice((b - 2) * CHUNK, (b - 1) * CHUNK)
            if carry:
                dk, dv = dk + part_ref[0, h, block], dv + part_ref[1, h, block]
            own_ref[0, h, block] = dk.astype(own_ref.dtype)
            own_ref[1, h, block] = dv.astype(own_ref.dtype)

    items = all_items((0, 1), half)
    run_half(
        sel, (0, 1), items, group, half, q_ref, do_ref, get_keys, lambda c: lows[c], scale, put_block, dq_ref, buf, sem
    )


def finish_kernel(early_ref, first_in, part_ref, last_in, back_in, dk_ref, dv_ref):
    tokens = dk_ref.shape[0]
    for i, out in ((0, dk_ref), (1, dv_ref)):
        value = early_ref[i] + part_ref[i, :, :WINDOW] + first_in[i].astype(F32)
        out[:WINDOW] = jnp.transpose(value.astype(BF16), (1, 0, 2))
        late = part_ref[i, :, WINDOW:] + last_in[i].astype(F32)
        value = late[:, tokens - 2 * WINDOW :] + back_in[i].astype(F32)
        if tokens > 2 * WINDOW:
            value = jnp.concatenate([late[:, : tokens - 2 * WINDOW], value], 1)
        out[WINDOW:] = jnp.transpose(value.astype(BF16), (1, 0, 2))


def shift(block, axis, distance):
    devices = range(lax.axis_size(axis))
    return lax.ppermute(block, axis, [(i - distance, i) for i in devices if i - distance in devices])


def swap(block):
    return lax.ppermute(block, "head", [(0, 1), (1, 0)])


def on_device(queries, key_heads, value_heads, out_grad, doc_ids):
    tokens, kv_count, group, size = queries.shape
    half = kv_count // 2
    chunks = tokens // CHUNK
    shape = jax.ShapeDtypeStruct
    dma = pltpu.SemaphoreType.DMA
    head = lax.axis_index("head")
    sel = jnp.stack([1 - head, head, lax.axis_index("ctx")]).astype(jnp.int32)
    rows = queries.reshape(tokens, kv_count * group, size)
    grads = out_grad.reshape(tokens, kv_count * group, size)
    docs = doc_ids.reshape(chunks, CHUNK)
    key_heads = pltpu.with_memory_space_constraint(key_heads, pltpu.HBM)
    value_heads = pltpu.with_memory_space_constraint(value_heads, pltpu.HBM)
    halo_shape = shape((2, half, WINDOW + PAD, size), BF16)
    rest = tokens - WINDOW

    def cost(n):
        work = n * 10 * CHUNK * group * (WINDOW + CHUNK) * size
        return pl.CostEstimate(flops=work * 10, bytes_accessed=n * CHUNK * group * size * 8, transcendentals=0)

    def staging(n):
        return [pltpu.VMEM((n, CHUNK, half * group, size), BF16), dma((n,))]

    def call(body, operands, specs, out_specs, out_shape, scratch, limit, estimate=None, aliases=None):
        return pl.pallas_call(
            body,
            in_specs=specs,
            out_specs=out_specs,
            out_shape=out_shape,
            scratch_shapes=scratch,
            input_output_aliases=aliases or {},
            compiler_params=params(limit),
            cost_estimate=estimate,
        )(*operands)

    tail, halo_other = call(
        tail_kernel,
        (sel, key_heads, value_heads, docs),
        [SMEM, HBM, HBM, VMEM],
        [VMEM, VMEM],
        [shape((2, kv_count, WINDOW, size), BF16), halo_shape],
        [pltpu.VMEM((2, WINDOW, kv_count, size), BF16), dma((2,))],
        16,
    )
    halo_other = shift(halo_other, "ctx", 1)
    kv, halo_mine, low = call(
        functools.partial(rest_kernel, group=group),
        (sel, key_heads, value_heads, docs, tail),
        [SMEM, HBM, HBM, VMEM, VMEM],
        [VMEM] * 3,
        [shape((2, kv_count, rest, size), BF16), halo_shape, shape((chunks, CHUNK * group), jnp.int32)],
        [pltpu.VMEM((2, rest, kv_count, size), BF16), dma((2,))],
        16,
    )
    halo_mine = shift(halo_mine, "ctx", 1)
    late_chunks = tuple(range(2, chunks))
    part_shape = shape((2, half, tokens, size), F32)

    def late(n, query_grad):
        operands = [sel, low, rows, grads, kv, tail]
        specs = [SMEM] + [VMEM] * 5
        if query_grad is not None:
            operands.append(query_grad)
            specs.append(ANY)
        return call(
            functools.partial(late_kernel, chunks=late_chunks, group=group, n=n),
            operands,
            specs,
            [ANY, VMEM],
            [shape(rows.shape, BF16), part_shape],
            staging(len(late_chunks)),
            20,
            cost(half * len(late_chunks)),
            {len(operands) - 1: 0} if query_grad is not None else None,
        )

    def early(n, halo, part, query_grad, emit):
        operands = [sel, docs, low, rows, grads, kv, halo]
        if part is not None:
            operands.append(part)
        return call(
            functools.partial(early_kernel, group=group, n=n, carry=part is not None),
            operands + [query_grad],
            [SMEM] + [VMEM] * (len(operands) - 1) + [ANY],
            [ANY, VMEM, VMEM],
            [
                shape(rows.shape, BF16),
                shape((2, half, WINDOW, size), emit),
                shape((2, half, WINDOW, size), BF16),
            ],
            staging(2),
            20,
            cost(half * 2),
            {len(operands): 0},
        )

    query_grad, part_other = late(0, None)
    query_grad, first_other, back_other = early(0, halo_other, part_other, query_grad, BF16)
    back_other = shift(back_other, "ctx", -1)
    first_other = swap(first_other)
    query_grad, early_mine, back_mine = early(1, halo_mine, None, query_grad, F32)
    back_mine = shift(back_mine, "ctx", -1)
    last_other = part_other[:, :, WINDOW:]
    last_other = last_other.at[:, :, tokens - 2 * WINDOW :].add(back_other.astype(F32)).astype(BF16)
    last_other = swap(last_other)
    query_grad, part_mine = late(1, query_grad)
    out = shape((tokens, half, size), BF16)
    key_grad, value_grad = call(
        finish_kernel,
        (early_mine, first_other, part_mine, last_other, back_mine),
        [VMEM] * 5,
        [VMEM] * 2,
        [out, out],
        [],
        16,
    )
    return query_grad.reshape(queries.shape), key_grad, value_grad


def solution(mesh):
    in_specs = (
        P("ctx", None, "head", None),
        P("ctx", None, None),
        P("ctx", None, None),
        P("ctx", None, "head", None),
        P("ctx"),
    )
    out_specs = (P("ctx", None, "head", None), P("ctx", "head", None), P("ctx", "head", None))

    return jax.shard_map(on_device, mesh=mesh, in_specs=in_specs, out_specs=out_specs, check_vma=False)
```

time: 62.3 us -> 47.8 us (0.77)
  the two profiles are of different devices: /device:TPU:16 before, /device:TPU:1 now
where the time goes in v3:
time: 47.8 us; the launch traced here: 47 us
  Pallas kernels  22.4 us (47%)
  starting transfers between devices  13 us (27%)
  waiting for transfers between devices  9.99 us (21%)
  between operations  0.79 us (2%)
  local copies, waits for them, and re-layouts  0.7 us (1%)
    pallas_call x7, Pallas kernels, call(): pl.pallas_call(body, in_specs=specs, out_specs=out_specs, out_shape=out_s...  22.4 us
    ppermute x4, starting transfers between devices, shift(): lax.ppermute(block, axis, [(i - distance, i) for i in devices if i - dist...  11.4 us
    ppermute x2, waiting for transfers between devices, swap(): return lax.ppermute(block, 'head', [(0, 1), (1, 0)])  5.92 us
    ppermute x4, waiting for transfers between devices, shift(): lax.ppermute(block, axis, [(i - distance, i) for i in devices if i - dist...  4.07 us
    ppermute x2, starting transfers between devices, swap(): return lax.ppermute(block, 'head', [(0, 1), (1, 0)])  1.59 us
  transfers between devices with their start and end apart: 6, of which 3 were waited for; matrix products, arithmetic and copies ran while one was open for 0% of the time, Pallas kernels for 40%

profile of v3, /device:TPU:1, one launch (start us, length us, event | category | flops | bytes accessed | tf_op | source)
XLA Modules:
  0.0 47.0 jit_solution(5204831397484950074)
XLA Ops:
  0.6 0.1 pad_add_fusion.sel_ref
  0.7 0.0 copy-start
  0.7 0.7 %copy-done = s32[512]{0:T(512)S(1)} copy-done((s32[512]{0:T(512)S(1)}, s32[512]{0:T(512)}, u32[]{:S(2)}) %copy-start) | copy-done | bytes 2072
  1.4 0.0 copy-start.3
  1.4 2.1 %shard_map.81 = (bf16[2,8,256,128]{3,2,1,0:T(8,128)(2,1)S(1)}, bf16[2,4,264,128]{3,2,1,0:T(8,128)(2,1)S(1)}) custom-call(s32[3]{0:T(128)S(1)} %pad_add_fusion.sel_ref, bf16[512,8,128]{2,1,0:T(8,128)(2,1)} %key_ref.3, bf16[512,8,128]{2,1,0:T(8,128)(2,1)} %value_ref.3, s32[4,128]{1,0:T(4,128)S(1)} %bitcast.7), custom_call_target="tpu_custom_call" | custom-call | tf_op jit(solution)/shard_map/pallas_call | solution.py:308
  3.5 0.0 copy-start.2
  3.5 4.7 %collective-permute-start.1 = (bf16[2,4,264,128]{3,2,1,0:T(8,128)(2,1)S(1)}, bf16[2,4,264,128]{3,2,1,0:T(8,128)(2,1)S(1)}, u32[]{:S(2)}, u32[]{:S(2)}) collective-permute-start(bf16[2,4,264,128]{3,2,1,0:T(8,128)(2,1)S(1)} %get-tuple-element.44), channel_id=1, source_target_pairs={{0,2},{2,4},{4,6},{6,8},{8,10},{10,12},{12,14},{14,16},{16,18},{18... | collective-permute-start | bytes 1622024 | tf_op jit(solution)/shard_map/ppermute | solution.py:277
  8.2 1.9 %shard_map.82 = (bf16[2,8,256,128]{3,2,1,0:T(8,128)(2,1)S(1)}, bf16[2,4,264,128]{3,2,1,0:T(8,128)(2,1)S(1)}, s32[4,256]{1,0:T(4,128)S(1)}) custom-call(s32[3]{0:T(128)S(1)} %pad_add_fusion.sel_ref, bf16[512,8,128]{2,1,0:T(8,128)(2,1)} %key_ref.3, bf16[512,8,128]{2,1,0:T(8,128)(2,1)} %value_ref.3, s32[4,128]{1,0:T(4,128)S(1)} %bitcast.8, ...), custom_call_target="tpu_custom_call" | custom-call | tf_op jit(solution)/shard_map/pallas_call | solution.py:308
  10.1 1.9 %collective-permute-start = (bf16[2,4,264,128]{3,2,1,0:T(8,128)(2,1)S(1)}, bf16[2,4,264,128]{3,2,1,0:T(8,128)(2,1)S(1)}, u32[]{:S(2)}, u32[]{:S(2)}) collective-permute-start(bf16[2,4,264,128]{3,2,1,0:T(8,128)(2,1)S(1)} %get-tuple-element.43), channel_id=1, source_target_pairs={{0,2},{2,4},{4,6},{6,8},{8,10},{10,12},{12,14},{14,16},{16,18},{18... | collective-permute-start | bytes 1622024 | tf_op jit(solution)/shard_map/ppermute | solution.py:277
  12.0 0.0 copy-done.3
  12.0 0.0 copy-done.2
  12.0 0.0 copy-start.1
  12.1 4.2 %shard_map.83 = (bf16[512,16,128]{2,1,0:T(8,128)(2,1)}, f32[2,4,512,128]{3,2,1,0:T(8,128)S(1)}) custom-call(s32[3]{0:T(128)S(1)} %pad_add_fusion.sel_ref, s32[4,256]{1,0:T(4,128)S(1)} %get-tuple-element.41.low_ref, bf16[512,16,128]{2,1,0:T(8,128)(2,1)S(1)} %bitcast.11, bf16[512,16,128]{2,1,0:T(8,128)(2,1)S(1)} %bitcast.15, ...), custom_call_target="tpu_custom_call" | custom-call | flops 10066329600 | bytes 2097152 | tf_op jit(solution)/shard_map/pallas_call | solution.py:308
  16.2 0.0 collective-permute-done.1.halo_ref
  16.2 0.0 copy-done.1
  16.2 4.3 %shard_map.84 = (bf16[512,16,128]{2,1,0:T(8,128)(2,1)}, bf16[2,4,256,128]{3,2,1,0:T(8,128)(2,1)S(1)}, bf16[2,4,256,128]{3,2,1,0:T(8,128)(2,1)S(1)}) custom-call(s32[3]{0:T(128)S(1)} %pad_add_fusion.sel_ref, s32[4,128]{1,0:T(4,128)S(1)} %bitcast.9, s32[4,256]{1,0:T(4,128)S(1)} %get-tuple-element.41.low_ref, ...), custom_call_target="tpu_custom_call", output_to_operand_aliasing={{0}: (8, {})} | custom-call | flops 10066329600 | bytes 2097152 | tf_op jit(solution)/shard_map/pallas_call | solution.py:308
  20.5 1.3 %collective-permute-start.2 = (bf16[2,4,256,128]{3,2,1,0:T(8,128)(2,1)S(1)}, bf16[2,4,256,128]{3,2,1,0:T(8,128)(2,1)S(1)}, u32[]{:S(2)}, u32[]{:S(2)}) collective-permute-start(bf16[2,4,256,128]{3,2,1,0:T(8,128)(2,1)S(1)} %get-tuple-element.51), channel_id=1, source_target_pairs={{0,1},{1,0},{2,3},{3,2},{4,5},{5,4},{6,7},{7,6},{8,9},{9,8},{10,11... | collective-permute-start | bytes 1572872 | tf_op jit(solution)/shard_map/ppermute | solution.py:281
  21.8 2.7 %collective-permute-start.3 = (bf16[2,4,256,128]{3,2,1,0:T(8,128)(2,1)S(1)}, bf16[2,4,256,128]{3,2,1,0:T(8,128)(2,1)S(1)}, u32[]{:S(2)}, u32[]{:S(2)}) collective-permute-start(bf16[2,4,256,128]{3,2,1,0:T(8,128)(2,1)S(1)} %get-tuple-element.53), channel_id=1, source_target_pairs={{2,0},{4,2},{6,4},{8,6},{10,8},{12,10},{14,12},{16,14},{18,16},{20... | collective-permute-start | bytes 1572872 | tf_op jit(solution)/shard_map/ppermute | solution.py:277
  24.5 0.0 collective-permute-done.halo_ref
  24.6 4.2 %shard_map.85 = (bf16[512,16,128]{2,1,0:T(8,128)(2,1)}, f32[2,4,256,128]{3,2,1,0:T(8,128)S(1)}, bf16[2,4,256,128]{3,2,1,0:T(8,128)(2,1)S(1)}) custom-call(s32[3]{0:T(128)S(1)} %pad_add_fusion.sel_ref, s32[4,128]{1,0:T(4,128)S(1)} %bitcast.10, s32[4,256]{1,0:T(4,128)S(1)} %get-tuple-element.41.low_ref, ...), custom_call_target="tpu_custom_call", output_to_operand_aliasing={{0}: (7, {})} | custom-call | flops 10066329600 | bytes 2097152 | tf_op jit(solution)/shard_map/pallas_call | solution.py:308
  28.8 2.1 %collective-permute-start.5 = (bf16[2,4,256,128]{3,2,1,0:T(8,128)(2,1)S(1)}, bf16[2,4,256,128]{3,2,1,0:T(8,128)(2,1)S(1)}, u32[]{:S(2)}, u32[]{:S(2)}) collective-permute-start(bf16[2,4,256,128]{3,2,1,0:T(8,128)(2,1)S(1)} %get-tuple-element.54), channel_id=1, source_target_pairs={{2,0},{4,2},{6,4},{8,6},{10,8},{12,10},{14,12},{16,14},{18,16},{20... | collective-permute-start | bytes 1572872 | tf_op jit(solution)/shard_map/ppermute | solution.py:277
  30.9 1.9 %collective-permute-done.3 = bf16[2,4,256,128]{3,2,1,0:T(8,128)(2,1)S(1)} collective-permute-done((bf16[2,4,256,128]{3,2,1,0:T(8,128)(2,1)S(1)}, bf16[2,4,256,128]{3,2,1,0:T(8,128)(2,1)S(1)}, u32[]{:S(2)}, u32[]{:S(2)}) %collective-permute-start.3) | collective-permute-done | bytes 524320 | tf_op jit(solution)/shard_map/ppermute | solution.py:277
  32.8 0.1 add_convert_fusion
  32.9 0.3 collective-permute-start.4
  33.2 4.2 %shard_map.86 = (bf16[512,16,128]{2,1,0:T(8,128)(2,1)}, f32[2,4,512,128]{3,2,1,0:T(8,128)S(1)}) custom-call(s32[3]{0:T(128)S(1)} %pad_add_fusion.sel_ref, s32[4,256]{1,0:T(4,128)S(1)} %get-tuple-element.41.low_ref, bf16[512,16,128]{2,1,0:T(8,128)(2,1)S(1)} %bitcast.14, bf16[512,16,128]{2,1,0:T(8,128)(2,1)S(1)} %bitcast.18, ...), custom_call_target="tpu_custom_call", output_to_operand_aliasing={{0}: (6, {})} | custom-call | flops 10066329600 | bytes 2097152 | tf_op jit(solution)/shard_map/pallas_call | solution.py:308
  37.4 0.0 collective-permute-done.2.first_in
  37.4 2.2 %collective-permute-done.5.back_in = bf16[2,4,256,128]{3,2,1,0:T(8,128)(2,1)S(1)} collective-permute-done((bf16[2,4,256,128]{3,2,1,0:T(8,128)(2,1)S(1)}, bf16[2,4,256,128]{3,2,1,0:T(8,128)(2,1)S(1)}, u32[]{:S(2)}, u32[]{:S(2)}) %collective-permute-start.5) | collective-permute-done | bytes 524320 | tf_op jit(solution)/shard_map/ppermute | solution.py:277
  39.6 5.9 %collective-permute-done.4.last_in = bf16[2,4,256,128]{3,2,1,0:T(8,128)(2,1)S(1)} collective-permute-done((bf16[2,4,256,128]{3,2,1,0:T(8,128)(2,1)S(1)}, bf16[2,4,256,128]{3,2,1,0:T(8,128)(2,1)S(1)}, u32[]{:S(2)}, u32[]{:S(2)}) %collective-permute-start.4) | collective-permute-done | bytes 524320 | tf_op jit(solution)/shard_map/ppermute | solution.py:281
  45.5 1.5 %shard_map.87 = (bf16[512,4,128]{2,1,0:T(4,128)(2,1)}, bf16[512,4,128]{2,1,0:T(4,128)(2,1)}) custom-call(f32[2,4,256,128]{3,2,1,0:T(8,128)S(1)} %get-tuple-element.50.early_ref, bf16[2,4,256,128]{3,2,1,0:T(8,128)(2,1)S(1)} %collective-permute-done.2.first_in, f32[2,4,512,128]{3,2,1,0:T(8,128)S(1)} %get-tuple-element.52.part_ref, ...), custom_call_target="tpu_custom_call" | custom-call | tf_op jit(solution)/shard_map/pallas_call | solution.py:308
Async XLA Ops:
  0.7 0.7 %copy-start = (s32[512]{0:T(512)S(1)}, s32[512]{0:T(512)}, u32[]{:S(2)}) copy-start(s32[512]{0:T(512)} %param.13) | copy-start | bytes 6148
  1.4 10.6 %copy-start.3 = (bf16[512,8,2,128]{3,2,1,0:T(2,128)(2,1)S(1)}, bf16[512,8,2,128]{3,2,1,0:T(2,128)(2,1)}, u32[]{:S(2)}) copy-start(bf16[512,8,2,128]{3,2,1,0:T(2,128)(2,1)} %param.12) | copy-start | bytes 6291460
  3.5 8.6 %copy-start.2 = (bf16[512,8,2,128]{3,2,1,0:T(2,128)(2,1)S(1)}, bf16[512,8,2,128]{3,2,1,0:T(2,128)(2,1)}, u32[]{:S(2)}) copy-start(bf16[512,8,2,128]{3,2,1,0:T(2,128)(2,1)} %param.9) | copy-start | bytes 6291460
  3.5 12.7 %collective-permute-start.1 = (bf16[2,4,264,128]{3,2,1,0:T(8,128)(2,1)S(1)}, bf16[2,4,264,128]{3,2,1,0:T(8,128)(2,1)S(1)}, u32[]{:S(2)}, u32[]{:S(2)}) collective-permute-start(bf16[2,4,264,128]{3,2,1,0:T(8,128)(2,1)S(1)} %get-tuple-element.44), channel_id=1, source_target_pairs={{0,2},{2,4},{4,6},{6,8},{8,10},{10,12},{12,14},{14,16},{16,18},{18... | collective-permute-start | bytes 1622024 | tf_op jit(solution)/shard_map/ppermute | solution.py:277
  10.1 14.5 %collective-permute-start = (bf16[2,4,264,128]{3,2,1,0:T(8,128)(2,1)S(1)}, bf16[2,4,264,128]{3,2,1,0:T(8,128)(2,1)S(1)}, u32[]{:S(2)}, u32[]{:S(2)}) collective-permute-start(bf16[2,4,264,128]{3,2,1,0:T(8,128)(2,1)S(1)} %get-tuple-element.43), channel_id=1, source_target_pairs={{0,2},{2,4},{4,6},{6,8},{8,10},{10,12},{12,14},{14,16},{16,18},{18... | collective-permute-start | bytes 1622024 | tf_op jit(solution)/shard_map/ppermute | solution.py:277
  12.0 4.2 %copy-start.1 = (s32[512]{0:T(512)S(1)}, s32[512]{0:T(512)}, u32[]{:S(2)}) copy-start(s32[512]{0:T(512)} %param.13) | copy-start | bytes 6148
  20.5 16.8 %collective-permute-start.2 = (bf16[2,4,256,128]{3,2,1,0:T(8,128)(2,1)S(1)}, bf16[2,4,256,128]{3,2,1,0:T(8,128)(2,1)S(1)}, u32[]{:S(2)}, u32[]{:S(2)}) collective-permute-start(bf16[2,4,256,128]{3,2,1,0:T(8,128)(2,1)S(1)} %get-tuple-element.51), channel_id=1, source_target_pairs={{0,1},{1,0},{2,3},{3,2},{4,5},{5,4},{6,7},{7,6},{8,9},{9,8},{10,11... | collective-permute-start | bytes 1572872 | tf_op jit(solution)/shard_map/ppermute | solution.py:281
  21.8 11.0 %collective-permute-start.3 = (bf16[2,4,256,128]{3,2,1,0:T(8,128)(2,1)S(1)}, bf16[2,4,256,128]{3,2,1,0:T(8,128)(2,1)S(1)}, u32[]{:S(2)}, u32[]{:S(2)}) collective-permute-start(bf16[2,4,256,128]{3,2,1,0:T(8,128)(2,1)S(1)} %get-tuple-element.53), channel_id=1, source_target_pairs={{2,0},{4,2},{6,4},{8,6},{10,8},{12,10},{14,12},{16,14},{18,16},{20... | collective-permute-start | bytes 1572872 | tf_op jit(solution)/shard_map/ppermute | solution.py:277
  28.8 10.8 %collective-permute-start.5 = (bf16[2,4,256,128]{3,2,1,0:T(8,128)(2,1)S(1)}, bf16[2,4,256,128]{3,2,1,0:T(8,128)(2,1)S(1)}, u32[]{:S(2)}, u32[]{:S(2)}) collective-permute-start(bf16[2,4,256,128]{3,2,1,0:T(8,128)(2,1)S(1)} %get-tuple-element.54), channel_id=1, source_target_pairs={{2,0},{4,2},{6,4},{8,6},{10,8},{12,10},{14,12},{16,14},{18,16},{20... | collective-permute-start | bytes 1572872 | tf_op jit(solution)/shard_map/ppermute | solution.py:277
  32.9 12.6 %collective-permute-start.4 = (bf16[2,4,256,128]{3,2,1,0:T(8,128)(2,1)S(1)}, bf16[2,4,256,128]{3,2,1,0:T(8,128)(2,1)S(1)}, u32[]{:S(2)}, u32[]{:S(2)}) collective-permute-start(bf16[2,4,256,128]{3,2,1,0:T(8,128)(2,1)S(1)} %add_convert_fusion), channel_id=1, source_target_pairs={{0,1},{1,0},{2,3},{3,2},{4,5},{5,4},{6,7},{7,6},{8,9},{9,8},{10,11... | collective-permute-start | bytes 1572872 | tf_op jit(solution)/shard_map/ppermute | solution.py:281

commit v4 on v3

--- a/solution.py
+++ b/solution.py
@@ -33,7 +33,7 @@
     return jnp.sum((column < row).astype(F32), axis=0, keepdims=True)
 
 
-def tail_kernel(sel_ref, key_ref, value_ref, docs_ref, kv_ref, halo_ref, buf, sem):
+def tail_kernel(sel_ref, key_ref, value_ref, docs_ref, kv_ref, halo_ref, buf, docs_buf, sem):
     half = halo_ref.shape[1]
     chunks = docs_ref.shape[0]
     first = key_ref.shape[0] - WINDOW
@@ -41,10 +41,12 @@
         pltpu.make_async_copy(ref.at[pl.ds(first, WINDOW)], buf.at[i], sem.at[i])
         for i, ref in enumerate((key_ref, value_ref))
     ]
+    copies.append(pltpu.make_async_copy(docs_ref, docs_buf, sem.at[2]))
     for copy in copies:
         copy.start()
+    copies[2].wait()
     pad = jnp.zeros((PAD - 2, CHUNK), BF16)
-    tail = jnp.concatenate([docs_ref[chunks - 2 :].astype(F32).astype(BF16), pad], 0)
+    tail = jnp.concatenate([docs_buf[chunks - 2 :].astype(F32).astype(BF16), pad], 0)
     for i in range(2):
         copies[i].wait()
         kv_ref[i] = jnp.transpose(buf[i], (1, 0, 2))
@@ -53,16 +55,10 @@
             halo_ref[i, h, WINDOW:] = tail
 
 
-def rest_kernel(sel_ref, key_ref, value_ref, docs_ref, tail_ref, kv_ref, halo_ref, low_ref, buf, sem, *, group):
+def rest_of_block(sel_ref, key_ref, value_ref, docs_ref, tail_ref, kv_ref, halo_ref, low_ref, group):
     half = halo_ref.shape[1]
     chunks = docs_ref.shape[0]
     rest = kv_ref.shape[2]
-    copies = [
-        pltpu.make_async_copy(ref.at[pl.ds(0, rest)], buf.at[i], sem.at[i])
-        for i, ref in enumerate((key_ref, value_ref))
-    ]
-    for copy in copies:
-        copy.start()
     docs = docs_ref[...].astype(F32)
     columns = docs.T
     for c in range(chunks):
@@ -70,15 +66,14 @@
         count = sum(count_smaller(columns[:, b : b + 1], row) for b in range(c + 1))
         low = count.astype(jnp.int32) + (WINDOW - c * CHUNK)
         low_ref[c : c + 1, :] = jnp.concatenate([low] * group, 1)
+    for i, ref in enumerate((key_ref, value_ref)):
+        kv_ref[i] = jnp.transpose(ref[:rest], (1, 0, 2))
     pad = jnp.zeros((PAD - 2, CHUNK), BF16)
     tail = jnp.concatenate([docs[chunks - 2 :].astype(BF16), pad], 0)
     for i in range(2):
         for h in range(half):
             halo_ref[i, h, :WINDOW] = tail_ref[i, sel_ref[1] * half + h]
             halo_ref[i, h, WINDOW:] = tail
-    for i in range(2):
-        copies[i].wait()
-        kv_ref[i] = jnp.transpose(buf[i], (1, 0, 2))
 
 
 def half_grads(items, get_query, get_keys, get_low, scale, group, put_dq, put_block):
@@ -162,7 +157,7 @@
     return pltpu.make_async_copy(buf.at[slot], dq_ref.at[rows, where, :], sem.at[slot])
 
 
-def run_half(sel, chunks, items, group, half, q_ref, do_ref, get_keys, get_low, scale, put_block, dq_ref, buf, sem):
+def run_half(sel, chunks, items, group, half, q_ref, do_ref, get_keys, get_low, scale, put_block, dq_ref, buf, sem, fetch=None):
     rows = half * group
     where = pl.ds(pl.multiple_of(sel * rows, rows), rows)
     held = {}
@@ -172,7 +167,8 @@
 
     def get_query(c, h, source):
         if c not in held:
-            held[c] = [jnp.transpose(ref[tokens(c), where, :], (1, 0, 2)) for ref in (q_ref, do_ref)]
+            read = fetch(c) if fetch else [ref[tokens(c), where, :] for ref in (q_ref, do_ref)]
+            held[c] = [jnp.transpose(x, (1, 0, 2)) for x in read]
         return [x[h * group : (h + 1) * group].reshape(group * CHUNK, -1) for x in held[c]]
 
     def put_dq(c, value):
@@ -188,11 +184,9 @@
     return [(c, h, 0, True, True) for c in range(len(chunks)) for h in range(half)]
 
 
-def late_kernel(sel_ref, low_ref, q_ref, do_ref, rest_ref, tail_ref, *refs, chunks, group, n):
-    dq_ref, part_ref, buf, sem = refs[-4:]
+def run_late(sel, chunks, group, q_ref, do_ref, rest_ref, tail_ref, low_ref, dq_ref, part_ref, buf, sem, fetch=None):
     half = part_ref.shape[1]
     scale = 1.0 / q_ref.shape[-1] ** 0.5
-    sel = sel_ref[n]
     rest = rest_ref.shape[2]
 
     def get_keys(h, c):
@@ -216,7 +210,41 @@
         return low_ref[chunks[c] : chunks[c] + 1, :]
 
     items = all_items(chunks, half)
-    run_half(sel, chunks, items, group, half, q_ref, do_ref, get_keys, get_low, scale, put_block, dq_ref, buf, sem)
+    run_half(
+        sel, chunks, items, group, half, q_ref, do_ref, get_keys, get_low, scale, put_block, dq_ref, buf, sem, fetch
+    )
+
+
+def first_kernel(
+    sel_ref, docs_ref, key_ref, value_ref, tail_ref, q_ref, do_ref, *refs, chunks, group
+):
+    dq_ref, part_ref, kv_ref, halo_ref, low_ref, q_buf, q_sem, buf, sem = refs
+    rows = part_ref.shape[1] * group
+    where = pl.ds(pl.multiple_of(sel_ref[0] * rows, rows), rows)
+
+    def load(c, i):
+        tokens = pl.ds(chunks[c] * CHUNK, CHUNK)
+        return pltpu.make_async_copy(
+            (q_ref, do_ref)[i].at[tokens, where, :], q_buf.at[c, i], q_sem.at[c, i]
+        )
+
+    for c in range(len(chunks)):
+        for i in range(2):
+            load(c, i).start()
+    rest_of_block(sel_ref, key_ref, value_ref, docs_ref, tail_ref, kv_ref, halo_ref, low_ref, group)
+
+    def fetch(c):
+        for i in range(2):
+            load(c, i).wait()
+        return q_buf[c, 0], q_buf[c, 1]
+
+    run_late(
+        sel_ref[0], chunks, group, q_ref, do_ref, kv_ref, tail_ref, low_ref, dq_ref, part_ref, buf, sem, fetch
+    )
+
+
+def late_kernel(sel_ref, low_ref, q_ref, do_ref, rest_ref, tail_ref, dq_in, dq_ref, part_ref, buf, sem, *, chunks, group):
+    run_late(sel_ref[1], chunks, group, q_ref, do_ref, rest_ref, tail_ref, low_ref, dq_ref, part_ref, buf, sem)
 
 
 def early_kernel(sel_ref, docs_ref, low_ref, q_ref, do_ref, rest_ref, halo_ref, *refs, group, n, carry):
@@ -281,6 +309,10 @@
     return lax.ppermute(block, "head", [(0, 1), (1, 0)])
 
 
+def in_hbm(array):
+    return pltpu.with_memory_space_constraint(array, pltpu.HBM)
+
+
 def on_device(queries, key_heads, value_heads, out_grad, doc_ids):
     tokens, kv_count, group, size = queries.shape
     half = kv_count // 2
@@ -292,8 +324,6 @@
     rows = queries.reshape(tokens, kv_count * group, size)
     grads = out_grad.reshape(tokens, kv_count * group, size)
     docs = doc_ids.reshape(chunks, CHUNK)
-    key_heads = pltpu.with_memory_space_constraint(key_heads, pltpu.HBM)
-    value_heads = pltpu.with_memory_space_constraint(value_heads, pltpu.HBM)
     halo_shape = shape((2, half, WINDOW + PAD, size), BF16)
     rest = tokens - WINDOW
 
@@ -318,44 +348,37 @@
 
     tail, halo_other = call(
         tail_kernel,
-        (sel, key_heads, value_heads, docs),
-        [SMEM, HBM, HBM, VMEM],
+        (sel, in_hbm(key_heads), in_hbm(value_heads), in_hbm(docs)),
+        [SMEM, HBM, HBM, HBM],
         [VMEM, VMEM],
         [shape((2, kv_count, WINDOW, size), BF16), halo_shape],
-        [pltpu.VMEM((2, WINDOW, kv_count, size), BF16), dma((2,))],
+        [pltpu.VMEM((2, WINDOW, kv_count, size), BF16), pltpu.VMEM(docs.shape, docs.dtype), dma((3,))],
         16,
     )
     halo_other = shift(halo_other, "ctx", 1)
-    kv, halo_mine, low = call(
-        functools.partial(rest_kernel, group=group),
-        (sel, key_heads, value_heads, docs, tail),
-        [SMEM, HBM, HBM, VMEM, VMEM],
-        [VMEM] * 3,
-        [shape((2, kv_count, rest, size), BF16), halo_shape, shape((chunks, CHUNK * group), jnp.int32)],
-        [pltpu.VMEM((2, rest, kv_count, size), BF16), dma((2,))],
-        16,
-    )
-    halo_mine = shift(halo_mine, "ctx", 1)
     late_chunks = tuple(range(2, chunks))
     part_shape = shape((2, half, tokens, size), F32)
-
-    def late(n, query_grad):
-        operands = [sel, low, rows, grads, kv, tail]
-        specs = [SMEM] + [VMEM] * 5
-        if query_grad is not None:
-            operands.append(query_grad)
-            specs.append(ANY)
-        return call(
-            functools.partial(late_kernel, chunks=late_chunks, group=group, n=n),
-            operands,
-            specs,
-            [ANY, VMEM],
-            [shape(rows.shape, BF16), part_shape],
-            staging(len(late_chunks)),
-            20,
-            cost(half * len(late_chunks)),
-            {len(operands) - 1: 0} if query_grad is not None else None,
-        )
+    query_grad, part_other, kv, halo_mine, low = call(
+        functools.partial(first_kernel, chunks=late_chunks, group=group),
+        (sel, docs, key_heads, value_heads, tail, in_hbm(rows), in_hbm(grads)),
+        [SMEM] + [VMEM] * 4 + [HBM] * 2,
+        [ANY] + [VMEM] * 4,
+        [
+            shape(rows.shape, BF16),
+            part_shape,
+            shape((2, kv_count, rest, size), BF16),
+            halo_shape,
+            shape((chunks, CHUNK * group), jnp.int32),
+        ],
+        [
+            pltpu.VMEM((len(late_chunks), 2, CHUNK, half * group, size), BF16),
+            dma((len(late_chunks), 2)),
+        ]
+        + staging(len(late_chunks)),
+        20,
+        cost(half * len(late_chunks)),
+    )
+    halo_mine = shift(halo_mine, "ctx", 1)
 
     def early(n, halo, part, query_grad, emit):
         operands = [sel, docs, low, rows, grads, kv, halo]
@@ -377,7 +400,6 @@
             {len(operands): 0},
         )
 
-    query_grad, part_other = late(0, None)
     query_grad, first_other, back_other = early(0, halo_other, part_other, query_grad, BF16)
     back_other = shift(back_other, "ctx", -1)
     first_other = swap(first_other)
@@ -386,7 +408,17 @@
     last_other = part_other[:, :, WINDOW:]
     last_other = last_other.at[:, :, tokens - 2 * WINDOW :].add(back_other.astype(F32)).astype(BF16)
     last_other = swap(last_other)
-    query_grad, part_mine = late(1, query_grad)
+    query_grad, part_mine = call(
+        functools.partial(late_kernel, chunks=late_chunks, group=group),
+        (sel, low, rows, grads, kv, tail, query_grad),
+        [SMEM] + [VMEM] * 5 + [ANY],
+        [ANY, VMEM],
+        [shape(rows.shape, BF16), part_shape],
+        staging(len(late_chunks)),
+        20,
+        cost(half * len(late_chunks)),
+        {6: 0},
+    )
     out = shape((tokens, half, size), BF16)
     key_grad, value_grad = call(
         finish_kernel,

time: 47.8 us -> 46.9 us (0.981)
  local copies, waits for them, and re-layouts: 0.7 us -> 0.03 us
    unnamed x8 -> x10, local copies, waits for them, and re-layouts: 0.7 us -> 0.03 us
    pallas_call x7 -> x6, Pallas kernels: 22.4 us -> 22.2 us  [call(): pl.pallas_call(body, in_specs=specs, out_specs=out_specs, out_shape=out_s...]
  transfers between devices with their start and end apart: 6 -> 6, of which waited for: 3 -> 3; matrix products, arithmetic and copies ran while one was open for 0% -> 0% of each run, Pallas kernels for 40% -> 41%
where the time goes in v4:
time: 46.9 us; the launch traced here: 46.1 us
  Pallas kernels  22.2 us (47%)
  starting transfers between devices  12.9 us (28%)
  waiting for transfers between devices  10 us (21%)
  between operations  0.82 us (2%)
    pallas_call x6, Pallas kernels, call(): pl.pallas_call(body, in_specs=specs, out_specs=out_specs, out_shape=out_s...  22.2 us
    ppermute x4, starting transfers between devices, shift(): lax.ppermute(block, axis, [(i - distance, i) for i in devices if i - dist...  11.3 us
    ppermute x2, waiting for transfers between devices, swap(): return lax.ppermute(block, 'head', [(0, 1), (1, 0)])  5.95 us
    ppermute x4, waiting for transfers between devices, shift(): lax.ppermute(block, axis, [(i - distance, i) for i in devices if i - dist...  4.05 us
    ppermute x2, starting transfers between devices, swap(): return lax.ppermute(block, 'head', [(0, 1), (1, 0)])  1.6 us
  transfers between devices with their start and end apart: 6, of which 3 were waited for; matrix products, arithmetic and copies ran while one was open for 0% of the time, Pallas kernels for 41%

profile of v4, /device:TPU:1, one launch (start us, length us, event | category | flops | bytes accessed | tf_op | source)
XLA Modules:
  0.0 46.1 jit_solution(7677372189835479597)
XLA Ops:
  0.6 0.0 copy-start.1
  0.6 0.0 copy-start
  0.7 0.0 copy-start.2
  0.7 0.1 pad_add_fusion.sel_ref
  0.7 2.0 %shard_map.81 = (bf16[2,8,256,128]{3,2,1,0:T(8,128)(2,1)S(1)}, bf16[2,4,264,128]{3,2,1,0:T(8,128)(2,1)S(1)}) custom-call(s32[3]{0:T(128)S(1)} %pad_add_fusion.sel_ref, bf16[512,8,128]{2,1,0:T(8,128)(2,1)} %key_ref.3, bf16[512,8,128]{2,1,0:T(8,128)(2,1)} %value_ref.3, s32[4,128]{1,0:T(4,128)} %bitcast.7), custom_call_target="tpu_custom_call" | custom-call | tf_op jit(solution)/shard_map/pallas_call | solution.py:338
  2.7 4.5 %collective-permute-start.1 = (bf16[2,4,264,128]{3,2,1,0:T(8,128)(2,1)S(1)}, bf16[2,4,264,128]{3,2,1,0:T(8,128)(2,1)S(1)}, u32[]{:S(2)}, u32[]{:S(2)}) collective-permute-start(bf16[2,4,264,128]{3,2,1,0:T(8,128)(2,1)S(1)} %get-tuple-element.44), channel_id=1, source_target_pairs={{0,2},{2,4},{4,6},{6,8},{8,10},{10,12},{12,14},{14,16},{16,18},{18... | collective-permute-start | bytes 1622024 | tf_op jit(solution)/shard_map/ppermute | solution.py:305
  7.3 0.0 copy-done.1
  7.3 0.0 copy-done
  7.3 0.0 copy-done.2
  7.3 0.0 copy-start.3
  7.3 0.0 copy-start.4
  7.3 6.1 %shard_map.82 = (bf16[512,16,128]{2,1,0:T(8,128)(2,1)}, f32[2,4,512,128]{3,2,1,0:T(8,128)S(1)}, bf16[2,8,256,128]{3,2,1,0:T(8,128)(2,1)S(1)}, bf16[2,4,264,128]{3,2,1,0:T(8,128)(2,1)S(1)}, s32[4,256]{1,0:T(4,128)S(1)}) custom-call(s32[3]{0:T(128)S(1)} %pad_add_fusion.sel_ref, s32[4,128]{1,0:T(4,128)S(1)} %bitcast.8, bf16[512,8,128]{2,1,0:T(8,128)(2,1)S(1)} %copy-done, ...), custom_call_target="tpu_custom_call" | custom-call | flops 10066329600 | bytes 2097152 | tf_op jit(solution)/shard_map/pallas_call | solution.py:338
  13.5 1.9 %collective-permute-start = (bf16[2,4,264,128]{3,2,1,0:T(8,128)(2,1)S(1)}, bf16[2,4,264,128]{3,2,1,0:T(8,128)(2,1)S(1)}, u32[]{:S(2)}, u32[]{:S(2)}) collective-permute-start(bf16[2,4,264,128]{3,2,1,0:T(8,128)(2,1)S(1)} %get-tuple-element.43), channel_id=1, source_target_pairs={{0,2},{2,4},{4,6},{6,8},{8,10},{10,12},{12,14},{14,16},{16,18},{18... | collective-permute-start | bytes 1622024 | tf_op jit(solution)/shard_map/ppermute | solution.py:305
  15.4 0.0 collective-permute-done.1.halo_ref
  15.4 0.0 copy-done.3
  15.4 0.0 copy-done.4
  15.4 4.3 %shard_map.83 = (bf16[512,16,128]{2,1,0:T(8,128)(2,1)}, bf16[2,4,256,128]{3,2,1,0:T(8,128)(2,1)S(1)}, bf16[2,4,256,128]{3,2,1,0:T(8,128)(2,1)S(1)}) custom-call(s32[3]{0:T(128)S(1)} %pad_add_fusion.sel_ref, s32[4,128]{1,0:T(4,128)S(1)} %bitcast.9, s32[4,256]{1,0:T(4,128)S(1)} %get-tuple-element.41.low_ref, ...), custom_call_target="tpu_custom_call", output_to_operand_aliasing={{0}: (8, {})} | custom-call | flops 10066329600 | bytes 2097152 | tf_op jit(solution)/shard_map/pallas_call | solution.py:338
  19.7 1.3 %collective-permute-start.2 = (bf16[2,4,256,128]{3,2,1,0:T(8,128)(2,1)S(1)}, bf16[2,4,256,128]{3,2,1,0:T(8,128)(2,1)S(1)}, u32[]{:S(2)}, u32[]{:S(2)}) collective-permute-start(bf16[2,4,256,128]{3,2,1,0:T(8,128)(2,1)S(1)} %get-tuple-element.51), channel_id=1, source_target_pairs={{0,1},{1,0},{2,3},{3,2},{4,5},{5,4},{6,7},{7,6},{8,9},{9,8},{10,11... | collective-permute-start | bytes 1572872 | tf_op jit(solution)/shard_map/ppermute | solution.py:309
  21.0 2.7 %collective-permute-start.3 = (bf16[2,4,256,128]{3,2,1,0:T(8,128)(2,1)S(1)}, bf16[2,4,256,128]{3,2,1,0:T(8,128)(2,1)S(1)}, u32[]{:S(2)}, u32[]{:S(2)}) collective-permute-start(bf16[2,4,256,128]{3,2,1,0:T(8,128)(2,1)S(1)} %get-tuple-element.53), channel_id=1, source_target_pairs={{2,0},{4,2},{6,4},{8,6},{10,8},{12,10},{14,12},{16,14},{18,16},{20... | collective-permute-start | bytes 1572872 | tf_op jit(solution)/shard_map/ppermute | solution.py:305
  23.7 0.0 collective-permute-done.halo_ref
  23.7 4.2 %shard_map.84 = (bf16[512,16,128]{2,1,0:T(8,128)(2,1)}, f32[2,4,256,128]{3,2,1,0:T(8,128)S(1)}, bf16[2,4,256,128]{3,2,1,0:T(8,128)(2,1)S(1)}) custom-call(s32[3]{0:T(128)S(1)} %pad_add_fusion.sel_ref, s32[4,128]{1,0:T(4,128)S(1)} %bitcast.10, s32[4,256]{1,0:T(4,128)S(1)} %get-tuple-element.41.low_ref, ...), custom_call_target="tpu_custom_call", output_to_operand_aliasing={{0}: (7, {})} | custom-call | flops 10066329600 | bytes 2097152 | tf_op jit(solution)/shard_map/pallas_call | solution.py:338
  27.9 2.1 %collective-permute-start.5 = (bf16[2,4,256,128]{3,2,1,0:T(8,128)(2,1)S(1)}, bf16[2,4,256,128]{3,2,1,0:T(8,128)(2,1)S(1)}, u32[]{:S(2)}, u32[]{:S(2)}) collective-permute-start(bf16[2,4,256,128]{3,2,1,0:T(8,128)(2,1)S(1)} %get-tuple-element.54), channel_id=1, source_target_pairs={{2,0},{4,2},{6,4},{8,6},{10,8},{12,10},{14,12},{16,14},{18,16},{20... | collective-permute-start | bytes 1572872 | tf_op jit(solution)/shard_map/ppermute | solution.py:305
  30.0 1.9 %collective-permute-done.3 = bf16[2,4,256,128]{3,2,1,0:T(8,128)(2,1)S(1)} collective-permute-done((bf16[2,4,256,128]{3,2,1,0:T(8,128)(2,1)S(1)}, bf16[2,4,256,128]{3,2,1,0:T(8,128)(2,1)S(1)}, u32[]{:S(2)}, u32[]{:S(2)}) %collective-permute-start.3) | collective-permute-done | bytes 524320 | tf_op jit(solution)/shard_map/ppermute | solution.py:305
  31.9 0.1 add_convert_fusion
  32.1 0.3 collective-permute-start.4
  32.4 4.2 %shard_map.85 = (bf16[512,16,128]{2,1,0:T(8,128)(2,1)}, f32[2,4,512,128]{3,2,1,0:T(8,128)S(1)}) custom-call(s32[3]{0:T(128)S(1)} %pad_add_fusion.sel_ref, s32[4,256]{1,0:T(4,128)S(1)} %get-tuple-element.41.low_ref, bf16[512,16,128]{2,1,0:T(8,128)(2,1)S(1)} %bitcast.14, bf16[512,16,128]{2,1,0:T(8,128)(2,1)S(1)} %bitcast.18, ...), custom_call_target="tpu_custom_call", output_to_operand_aliasing={{0}: (6, {})} | custom-call | flops 10066329600 | bytes 2097152 | tf_op jit(solution)/shard_map/pallas_call | solution.py:338
  36.6 0.0 collective-permute-done.2.first_in
  36.6 2.1 %collective-permute-done.5.back_in = bf16[2,4,256,128]{3,2,1,0:T(8,128)(2,1)S(1)} collective-permute-done((bf16[2,4,256,128]{3,2,1,0:T(8,128)(2,1)S(1)}, bf16[2,4,256,128]{3,2,1,0:T(8,128)(2,1)S(1)}, u32[]{:S(2)}, u32[]{:S(2)}) %collective-permute-start.5) | collective-permute-done | bytes 524320 | tf_op jit(solution)/shard_map/ppermute | solution.py:305
  38.7 5.9 %collective-permute-done.4.last_in = bf16[2,4,256,128]{3,2,1,0:T(8,128)(2,1)S(1)} collective-permute-done((bf16[2,4,256,128]{3,2,1,0:T(8,128)(2,1)S(1)}, bf16[2,4,256,128]{3,2,1,0:T(8,128)(2,1)S(1)}, u32[]{:S(2)}, u32[]{:S(2)}) %collective-permute-start.4) | collective-permute-done | bytes 524320 | tf_op jit(solution)/shard_map/ppermute | solution.py:309
  44.6 1.5 %shard_map.86 = (bf16[512,4,128]{2,1,0:T(4,128)(2,1)}, bf16[512,4,128]{2,1,0:T(4,128)(2,1)}) custom-call(f32[2,4,256,128]{3,2,1,0:T(8,128)S(1)} %get-tuple-element.50.early_ref, bf16[2,4,256,128]{3,2,1,0:T(8,128)(2,1)S(1)} %collective-permute-done.2.first_in, f32[2,4,512,128]{3,2,1,0:T(8,128)S(1)} %get-tuple-element.52.part_ref, ...), custom_call_target="tpu_custom_call" | custom-call | tf_op jit(solution)/shard_map/pallas_call | solution.py:338
Async XLA Ops:
  0.6 6.7 %copy-start.1 = (bf16[512,8,128]{2,1,0:T(8,128)(2,1)S(1)}, bf16[512,8,128]{2,1,0:T(8,128)(2,1)}, u32[]{:S(2)}) copy-start(bf16[512,8,128]{2,1,0:T(8,128)(2,1)} %value_ref.3) | copy-start | bytes 3145732
  0.6 6.7 %copy-start = (bf16[512,8,128]{2,1,0:T(8,128)(2,1)S(1)}, bf16[512,8,128]{2,1,0:T(8,128)(2,1)}, u32[]{:S(2)}) copy-start(bf16[512,8,128]{2,1,0:T(8,128)(2,1)} %key_ref.3) | copy-start | bytes 3145732
  0.7 6.6 %copy-start.2 = (s32[512]{0:T(512)S(1)}, s32[512]{0:T(512)}, u32[]{:S(2)}) copy-start(s32[512]{0:T(512)} %param.13) | copy-start | bytes 6148
  2.7 12.7 %collective-permute-start.1 = (bf16[2,4,264,128]{3,2,1,0:T(8,128)(2,1)S(1)}, bf16[2,4,264,128]{3,2,1,0:T(8,128)(2,1)S(1)}, u32[]{:S(2)}, u32[]{:S(2)}) collective-permute-start(bf16[2,4,264,128]{3,2,1,0:T(8,128)(2,1)S(1)} %get-tuple-element.44), channel_id=1, source_target_pairs={{0,2},{2,4},{4,6},{6,8},{8,10},{10,12},{12,14},{14,16},{16,18},{18... | collective-permute-start | bytes 1622024 | tf_op jit(solution)/shard_map/ppermute | solution.py:305
  7.3 8.1 %copy-start.3 = (bf16[512,8,2,128]{3,2,1,0:T(2,128)(2,1)S(1)}, bf16[512,8,2,128]{3,2,1,0:T(2,128)(2,1)}, u32[]{:S(2)}) copy-start(bf16[512,8,2,128]{3,2,1,0:T(2,128)(2,1)} %param.9) | copy-start | bytes 6291460
  7.3 8.1 %copy-start.4 = (bf16[512,8,2,128]{3,2,1,0:T(2,128)(2,1)S(1)}, bf16[512,8,2,128]{3,2,1,0:T(2,128)(2,1)}, u32[]{:S(2)}) copy-start(bf16[512,8,2,128]{3,2,1,0:T(2,128)(2,1)} %param.12) | copy-start | bytes 6291460
  13.5 10.2 %collective-permute-start = (bf16[2,4,264,128]{3,2,1,0:T(8,128)(2,1)S(1)}, bf16[2,4,264,128]{3,2,1,0:T(8,128)(2,1)S(1)}, u32[]{:S(2)}, u32[]{:S(2)}) collective-permute-start(bf16[2,4,264,128]{3,2,1,0:T(8,128)(2,1)S(1)} %get-tuple-element.43), channel_id=1, source_target_pairs={{0,2},{2,4},{4,6},{6,8},{8,10},{10,12},{12,14},{14,16},{16,18},{18... | collective-permute-start | bytes 1622024 | tf_op jit(solution)/shard_map/ppermute | solution.py:305
  19.7 16.9 %collective-permute-start.2 = (bf16[2,4,256,128]{3,2,1,0:T(8,128)(2,1)S(1)}, bf16[2,4,256,128]{3,2,1,0:T(8,128)(2,1)S(1)}, u32[]{:S(2)}, u32[]{:S(2)}) collective-permute-start(bf16[2,4,256,128]{3,2,1,0:T(8,128)(2,1)S(1)} %get-tuple-element.51), channel_id=1, source_target_pairs={{0,1},{1,0},{2,3},{3,2},{4,5},{5,4},{6,7},{7,6},{8,9},{9,8},{10,11... | collective-permute-start | bytes 1572872 | tf_op jit(solution)/shard_map/ppermute | solution.py:309
  21.0 10.9 %collective-permute-start.3 = (bf16[2,4,256,128]{3,2,1,0:T(8,128)(2,1)S(1)}, bf16[2,4,256,128]{3,2,1,0:T(8,128)(2,1)S(1)}, u32[]{:S(2)}, u32[]{:S(2)}) collective-permute-start(bf16[2,4,256,128]{3,2,1,0:T(8,128)(2,1)S(1)} %get-tuple-element.53), channel_id=1, source_target_pairs={{2,0},{4,2},{6,4},{8,6},{10,8},{12,10},{14,12},{16,14},{18,16},{20... | collective-permute-start | bytes 1572872 | tf_op jit(solution)/shard_map/ppermute | solution.py:305
  27.9 10.8 %collective-permute-start.5 = (bf16[2,4,256,128]{3,2,1,0:T(8,128)(2,1)S(1)}, bf16[2,4,256,128]{3,2,1,0:T(8,128)(2,1)S(1)}, u32[]{:S(2)}, u32[]{:S(2)}) collective-permute-start(bf16[2,4,256,128]{3,2,1,0:T(8,128)(2,1)S(1)} %get-tuple-element.54), channel_id=1, source_target_pairs={{2,0},{4,2},{6,4},{8,6},{10,8},{12,10},{14,12},{16,14},{18,16},{20... | collective-permute-start | bytes 1572872 | tf_op jit(solution)/shard_map/ppermute | solution.py:305
  32.1 12.6 %collective-permute-start.4 = (bf16[2,4,256,128]{3,2,1,0:T(8,128)(2,1)S(1)}, bf16[2,4,256,128]{3,2,1,0:T(8,128)(2,1)S(1)}, u32[]{:S(2)}, u32[]{:S(2)}) collective-permute-start(bf16[2,4,256,128]{3,2,1,0:T(8,128)(2,1)S(1)} %add_convert_fusion), channel_id=1, source_target_pairs={{0,1},{1,0},{2,3},{3,2},{4,5},{5,4},{6,7},{7,6},{8,9},{9,8},{10,11... | collective-permute-start | bytes 1572872 | tf_op jit(solution)/shard_map/ppermute | solution.py:309

commit v5 on v4

--- a/solution.py
+++ b/solution.py
@@ -11,6 +11,7 @@
 WINDOW = 256
 CHUNK = WINDOW // 2
 PAD = 8
+STEP = 32
 LOG2E = 1.4426950408889634
 F32 = jnp.float32
 BF16 = jnp.bfloat16
@@ -31,6 +32,11 @@
 
 def count_smaller(column, row):
     return jnp.sum((column < row).astype(F32), axis=0, keepdims=True)
+
+
+def to_heads(ref, out, i):
+    for r in range(0, out.shape[2], STEP):
+        out[i, :, r : r + STEP] = jnp.transpose(ref[r : r + STEP], (1, 0, 2))
 
 
 def tail_kernel(sel_ref, key_ref, value_ref, docs_ref, kv_ref, halo_ref, buf, docs_buf, sem):
@@ -49,7 +55,7 @@
     tail = jnp.concatenate([docs_buf[chunks - 2 :].astype(F32).astype(BF16), pad], 0)
     for i in range(2):
         copies[i].wait()
-        kv_ref[i] = jnp.transpose(buf[i], (1, 0, 2))
+        to_heads(buf.at[i], kv_ref, i)
         for h in range(half):
             halo_ref[i, h, :WINDOW] = kv_ref[i, sel_ref[0] * half + h]
             halo_ref[i, h, WINDOW:] = tail
@@ -58,7 +64,6 @@
 def rest_of_block(sel_ref, key_ref, value_ref, docs_ref, tail_ref, kv_ref, halo_ref, low_ref, group):
     half = halo_ref.shape[1]
     chunks = docs_ref.shape[0]
-    rest = kv_ref.shape[2]
     docs = docs_ref[...].astype(F32)
     columns = docs.T
     for c in range(chunks):
@@ -67,7 +72,7 @@
         low = count.astype(jnp.int32) + (WINDOW - c * CHUNK)
         low_ref[c : c + 1, :] = jnp.concatenate([low] * group, 1)
     for i, ref in enumerate((key_ref, value_ref)):
-        kv_ref[i] = jnp.transpose(ref[:rest], (1, 0, 2))
+        to_heads(ref, kv_ref, i)
     pad = jnp.zeros((PAD - 2, CHUNK), BF16)
     tail = jnp.concatenate([docs[chunks - 2 :].astype(BF16), pad], 0)
     for i in range(2):
@@ -157,7 +162,20 @@
     return pltpu.make_async_copy(buf.at[slot], dq_ref.at[rows, where, :], sem.at[slot])
 
 
-def run_half(sel, chunks, items, group, half, q_ref, do_ref, get_keys, get_low, scale, put_block, dq_ref, buf, sem, fetch=None):
+def load_rows(q_ref, do_ref, dst, sem, sel, chunks, rows):
+    where = pl.ds(pl.multiple_of(sel * rows, rows), rows)
+    return [
+        [
+            pltpu.make_async_copy(
+                ref.at[pl.ds(chunk * CHUNK, CHUNK), where, :], dst.at[c, i], sem.at[c, i]
+            )
+            for i, ref in enumerate((q_ref, do_ref))
+        ]
+        for c, chunk in enumerate(chunks)
+    ]
+
+
+def run_half(sel, chunks, items, group, half, read, get_keys, get_low, scale, put_block, dq_ref, buf, sem):
     rows = half * group
     where = pl.ds(pl.multiple_of(sel * rows, rows), rows)
     held = {}
@@ -167,8 +185,7 @@
 
     def get_query(c, h, source):
         if c not in held:
-            read = fetch(c) if fetch else [ref[tokens(c), where, :] for ref in (q_ref, do_ref)]
-            held[c] = [jnp.transpose(x, (1, 0, 2)) for x in read]
+            held[c] = [jnp.transpose(x, (1, 0, 2)) for x in read(c)]
         return [x[h * group : (h + 1) * group].reshape(group * CHUNK, -1) for x in held[c]]
 
     def put_dq(c, value):
@@ -184,9 +201,9 @@
     return [(c, h, 0, True, True) for c in range(len(chunks)) for h in range(half)]
 
 
-def run_late(sel, chunks, group, q_ref, do_ref, rest_ref, tail_ref, low_ref, dq_ref, part_ref, buf, sem, fetch=None):
+def run_late(sel, chunks, group, read, rest_ref, tail_ref, low_ref, dq_ref, part_ref, buf, sem):
     half = part_ref.shape[1]
-    scale = 1.0 / q_ref.shape[-1] ** 0.5
+    scale = 1.0 / part_ref.shape[-1] ** 0.5
     rest = rest_ref.shape[2]
 
     def get_keys(h, c):
@@ -210,48 +227,48 @@
         return low_ref[chunks[c] : chunks[c] + 1, :]
 
     items = all_items(chunks, half)
-    run_half(
-        sel, chunks, items, group, half, q_ref, do_ref, get_keys, get_low, scale, put_block, dq_ref, buf, sem, fetch
-    )
-
-
-def first_kernel(
-    sel_ref, docs_ref, key_ref, value_ref, tail_ref, q_ref, do_ref, *refs, chunks, group
+    run_half(sel, chunks, items, group, half, read, get_keys, get_low, scale, put_block, dq_ref, buf, sem)
+
+
+def first_kernel(sel_ref, docs_ref, key_ref, value_ref, tail_ref, q_ref, do_ref, *refs, chunks, group):
+    dq_ref, part_ref, kv_ref, halo_ref, low_ref, next_ref, q_buf, q_sem, next_sem, buf, sem = refs
+    rows = part_ref.shape[1] * group
+    copies = load_rows(q_ref, do_ref, q_buf, q_sem, sel_ref[0], chunks, rows)
+    ahead = load_rows(q_ref, do_ref, next_ref, next_sem, sel_ref[0], (0, 1), rows)
+    for pair in copies + ahead:
+        for copy in pair:
+            copy.start()
+    rest_of_block(sel_ref, key_ref, value_ref, docs_ref, tail_ref, kv_ref, halo_ref, low_ref, group)
+
+    def read(c):
+        for copy in copies[c]:
+            copy.wait()
+        return q_buf[c, 0], q_buf[c, 1]
+
+    run_late(sel_ref[0], chunks, group, read, kv_ref, tail_ref, low_ref, dq_ref, part_ref, buf, sem)
+    for pair in ahead:
+        for copy in pair:
+            copy.wait()
+
+
+def late_kernel(sel_ref, low_ref, rest_ref, tail_ref, qd_ref, dq_in, dq_ref, part_ref, buf, sem, *, chunks, group):
+    def read(c):
+        return qd_ref[c, 0], qd_ref[c, 1]
+
+    run_late(sel_ref[1], chunks, group, read, rest_ref, tail_ref, low_ref, dq_ref, part_ref, buf, sem)
+
+
+def early_kernel(
+    sel_ref, docs_ref, low_ref, q_ref, do_ref, rest_ref, halo_ref, qd_ref, *refs, group, n, carry, ahead
 ):
-    dq_ref, part_ref, kv_ref, halo_ref, low_ref, q_buf, q_sem, buf, sem = refs
-    rows = part_ref.shape[1] * group
-    where = pl.ds(pl.multiple_of(sel_ref[0] * rows, rows), rows)
-
-    def load(c, i):
-        tokens = pl.ds(chunks[c] * CHUNK, CHUNK)
-        return pltpu.make_async_copy(
-            (q_ref, do_ref)[i].at[tokens, where, :], q_buf.at[c, i], q_sem.at[c, i]
-        )
-
-    for c in range(len(chunks)):
-        for i in range(2):
-            load(c, i).start()
-    rest_of_block(sel_ref, key_ref, value_ref, docs_ref, tail_ref, kv_ref, halo_ref, low_ref, group)
-
-    def fetch(c):
-        for i in range(2):
-            load(c, i).wait()
-        return q_buf[c, 0], q_buf[c, 1]
-
-    run_late(
-        sel_ref[0], chunks, group, q_ref, do_ref, kv_ref, tail_ref, low_ref, dq_ref, part_ref, buf, sem, fetch
-    )
-
-
-def late_kernel(sel_ref, low_ref, q_ref, do_ref, rest_ref, tail_ref, dq_in, dq_ref, part_ref, buf, sem, *, chunks, group):
-    run_late(sel_ref[1], chunks, group, q_ref, do_ref, rest_ref, tail_ref, low_ref, dq_ref, part_ref, buf, sem)
-
-
-def early_kernel(sel_ref, docs_ref, low_ref, q_ref, do_ref, rest_ref, halo_ref, *refs, group, n, carry):
     part_ref = refs[0] if carry else None
-    dq_ref, own_ref, back_ref, buf, sem = refs[-5:]
+    dq_ref, own_ref, back_ref, next_ref, next_sem, buf, sem = refs[-7:]
     half = own_ref.shape[1]
-    scale = 1.0 / q_ref.shape[-1] ** 0.5
+    copies = load_rows(q_ref, do_ref, next_ref, next_sem, sel_ref[1], ahead, half * group)
+    for pair in copies:
+        for copy in pair:
+            copy.start()
+    scale = 1.0 / own_ref.shape[-1] ** 0.5
     sel = sel_ref[n]
     before = jnp.where(sel_ref[2] == 0, -1.0, halo_ref[0, 0, WINDOW:].astype(F32)).T
     lows = []
@@ -282,22 +299,47 @@
             own_ref[0, h, block] = dk.astype(own_ref.dtype)
             own_ref[1, h, block] = dv.astype(own_ref.dtype)
 
+    def read(c):
+        return qd_ref[c, 0], qd_ref[c, 1]
+
     items = all_items((0, 1), half)
     run_half(
-        sel, (0, 1), items, group, half, q_ref, do_ref, get_keys, lambda c: lows[c], scale, put_block, dq_ref, buf, sem
-    )
-
-
-def finish_kernel(early_ref, first_in, part_ref, last_in, back_in, dk_ref, dv_ref):
-    tokens = dk_ref.shape[0]
+        sel, (0, 1), items, group, half, read, get_keys, lambda c: lows[c], scale, put_block, dq_ref, buf, sem
+    )
+    for pair in copies:
+        for copy in pair:
+            copy.wait()
+
+
+def out_rows(buf, sem, i, out, rows):
+    return pltpu.make_async_copy(buf.at[i], out.at[rows], sem.at[i])
+
+
+def begin_kernel(early_ref, first_in, part_ref, back_in, dk_ref, dv_ref, late_ref, buf, sem):
+    late = late_ref.shape[2]
     for i, out in ((0, dk_ref), (1, dv_ref)):
-        value = early_ref[i] + part_ref[i, :, :WINDOW] + first_in[i].astype(F32)
-        out[:WINDOW] = jnp.transpose(value.astype(BF16), (1, 0, 2))
-        late = part_ref[i, :, WINDOW:] + last_in[i].astype(F32)
-        value = late[:, tokens - 2 * WINDOW :] + back_in[i].astype(F32)
-        if tokens > 2 * WINDOW:
-            value = jnp.concatenate([late[:, : tokens - 2 * WINDOW], value], 1)
-        out[WINDOW:] = jnp.transpose(value.astype(BF16), (1, 0, 2))
+        for r in range(0, WINDOW, STEP):
+            rows = slice(r, r + STEP)
+            value = early_ref[i, :, rows] + part_ref[i, :, rows] + first_in[i, :, rows].astype(F32)
+            buf[i, rows] = jnp.transpose(value.astype(BF16), (1, 0, 2))
+        out_rows(buf, sem, i, out, pl.ds(0, WINDOW)).start()
+        if late > WINDOW:
+            late_ref[i, :, : late - WINDOW] = part_ref[i, :, WINDOW:late]
+        late_ref[i, :, late - WINDOW :] = part_ref[i, :, late:] + back_in[i].astype(F32)
+    for i, out in ((0, dk_ref), (1, dv_ref)):
+        out_rows(buf, sem, i, out, pl.ds(0, WINDOW)).wait()
+
+
+def finish_kernel(late_ref, last_in, dk_in, dv_in, dk_ref, dv_ref, buf, sem):
+    late = late_ref.shape[2]
+    for i, out in ((0, dk_ref), (1, dv_ref)):
+        for r in range(0, late, STEP):
+            rows = slice(r, r + STEP)
+            value = late_ref[i, :, rows] + last_in[i, :, rows].astype(F32)
+            buf[i, rows] = jnp.transpose(value.astype(BF16), (1, 0, 2))
+        out_rows(buf, sem, i, out, pl.ds(WINDOW, late)).start()
+    for i, out in ((0, dk_ref), (1, dv_ref)):
+        out_rows(buf, sem, i, out, pl.ds(WINDOW, late)).wait()
 
 
 def shift(block, axis, distance):
@@ -358,76 +400,89 @@
     halo_other = shift(halo_other, "ctx", 1)
     late_chunks = tuple(range(2, chunks))
     part_shape = shape((2, half, tokens, size), F32)
-    query_grad, part_other, kv, halo_mine, low = call(
+    q_hbm, do_hbm = in_hbm(rows), in_hbm(grads)
+    qd_shape = shape((2, 2, CHUNK, half * group, size), BF16)
+    late_qd = shape((len(late_chunks),) + qd_shape.shape[1:], BF16)
+    query_grad, part_other, kv, halo_mine, low, qd_other = call(
         functools.partial(first_kernel, chunks=late_chunks, group=group),
-        (sel, docs, key_heads, value_heads, tail, in_hbm(rows), in_hbm(grads)),
+        (sel, docs, key_heads, value_heads, tail, q_hbm, do_hbm),
         [SMEM] + [VMEM] * 4 + [HBM] * 2,
-        [ANY] + [VMEM] * 4,
+        [ANY] + [VMEM] * 5,
         [
             shape(rows.shape, BF16),
             part_shape,
             shape((2, kv_count, rest, size), BF16),
             halo_shape,
             shape((chunks, CHUNK * group), jnp.int32),
+            qd_shape,
         ],
-        [
-            pltpu.VMEM((len(late_chunks), 2, CHUNK, half * group, size), BF16),
-            dma((len(late_chunks), 2)),
-        ]
+        [pltpu.VMEM(late_qd.shape, BF16), dma((len(late_chunks), 2)), dma((2, 2))]
         + staging(len(late_chunks)),
         20,
         cost(half * len(late_chunks)),
     )
     halo_mine = shift(halo_mine, "ctx", 1)
 
-    def early(n, halo, part, query_grad, emit):
-        operands = [sel, docs, low, rows, grads, kv, halo]
+    def early(n, halo, qd, part, query_grad, emit, ahead):
+        operands = [sel, docs, low, q_hbm, do_hbm, kv, halo, qd]
         if part is not None:
             operands.append(part)
         return call(
-            functools.partial(early_kernel, group=group, n=n, carry=part is not None),
+            functools.partial(early_kernel, group=group, n=n, carry=part is not None, ahead=ahead),
             operands + [query_grad],
-            [SMEM] + [VMEM] * (len(operands) - 1) + [ANY],
-            [ANY, VMEM, VMEM],
+            [SMEM, VMEM, VMEM, HBM, HBM] + [VMEM] * (len(operands) - 5) + [ANY],
+            [ANY, VMEM, VMEM, VMEM],
             [
                 shape(rows.shape, BF16),
                 shape((2, half, WINDOW, size), emit),
                 shape((2, half, WINDOW, size), BF16),
+                shape((len(ahead),) + qd_shape.shape[1:], BF16),
             ],
-            staging(2),
+            [dma((len(ahead), 2))] + staging(2),
             20,
             cost(half * 2),
             {len(operands): 0},
         )
 
-    query_grad, first_other, back_other = early(0, halo_other, part_other, query_grad, BF16)
+    query_grad, first_other, back_other, qd_mine = early(0, halo_other, qd_other, part_other, query_grad, BF16, (0, 1))
     back_other = shift(back_other, "ctx", -1)
     first_other = swap(first_other)
-    query_grad, early_mine, back_mine = early(1, halo_mine, None, query_grad, F32)
+    query_grad, early_mine, back_mine, qd_late = early(1, halo_mine, qd_mine, None, query_grad, F32, late_chunks)
     back_mine = shift(back_mine, "ctx", -1)
     last_other = part_other[:, :, WINDOW:]
     last_other = last_other.at[:, :, tokens - 2 * WINDOW :].add(back_other.astype(F32)).astype(BF16)
     last_other = swap(last_other)
     query_grad, part_mine = call(
         functools.partial(late_kernel, chunks=late_chunks, group=group),
-        (sel, low, rows, grads, kv, tail, query_grad),
-        [SMEM] + [VMEM] * 5 + [ANY],
+        (sel, low, kv, tail, qd_late, query_grad),
+        [SMEM] + [VMEM] * 4 + [ANY],
         [ANY, VMEM],
         [shape(rows.shape, BF16), part_shape],
         staging(len(late_chunks)),
         20,
         cost(half * len(late_chunks)),
-        {6: 0},
+        {5: 0},
     )
     out = shape((tokens, half, size), BF16)
+    late_tokens = tokens - WINDOW
+    key_grad, value_grad, late_sum = call(
+        begin_kernel,
+        (early_mine, first_other, part_mine, back_mine),
+        [VMEM] * 4,
+        [ANY, ANY, VMEM],
+        [out, out, shape((2, half, late_tokens, size), F32)],
+        [pltpu.VMEM((2, WINDOW, half, size), BF16), dma((2,))],
+        8,
+    )
     key_grad, value_grad = call(
         finish_kernel,
-        (early_mine, first_other, part_mine, last_other, back_mine),
-        [VMEM] * 5,
-        [VMEM] * 2,
+        (late_sum, last_other, key_grad, value_grad),
+        [VMEM, VMEM, ANY, ANY],
+        [ANY, ANY],
         [out, out],
-        [],
-        16,
+        [pltpu.VMEM((2, late_tokens, half, size), BF16), dma((2,))],
+        8,
+        aliases={2: 0, 3: 1},
     )
     return query_grad.reshape(queries.shape), key_grad, value_grad
 

time: 46.9 us -> 46.8 us (level)
  waiting for transfers between devices: 10 us -> 8.48 us
  Pallas kernels: 22.2 us -> 23.7 us
    ppermute x2, waiting for transfers between devices: 5.95 us -> 4.31 us  [swap(): return lax.ppermute(block, 'head', [(0, 1), (1, 0)])]
    pallas_call x6 -> x7, Pallas kernels: 22.2 us -> 23.7 us  [call(): pl.pallas_call(body, in_specs=specs, out_specs=out_specs, out_shape=out_s...]
  transfers between devices with their start and end apart: 6 -> 6, of which waited for: 3 -> 3; matrix products, arithmetic and copies ran while one was open for 0% -> 0% of each run, Pallas kernels for 41% -> 45%
where the time goes in v5:
time: 46.8 us; the launch traced here: 46.2 us
  Pallas kernels  23.7 us (51%)
  starting transfers between devices  12.8 us (27%)
  waiting for transfers between devices  8.48 us (18%)
  between operations  0.95 us (2%)
    pallas_call x7, Pallas kernels, call(): pl.pallas_call(body, in_specs=specs, out_specs=out_specs, out_shape=out_s...  23.7 us
    ppermute x4, starting transfers between devices, shift(): lax.ppermute(block, axis, [(i - distance, i) for i in devices if i - dist...  11.2 us
    ppermute x2, waiting for transfers between devices, swap(): return lax.ppermute(block, 'head', [(0, 1), (1, 0)])  4.31 us
    ppermute x4, waiting for transfers between devices, shift(): lax.ppermute(block, axis, [(i - distance, i) for i in devices if i - dist...  4.17 us
    ppermute x2, starting transfers between devices, swap(): return lax.ppermute(block, 'head', [(0, 1), (1, 0)])  1.59 us
  transfers between devices with their start and end apart: 6, of which 3 were waited for; matrix products, arithmetic and copies ran while one was open for 0% of the time, Pallas kernels for 45%

profile of v5, /device:TPU:1, one launch (start us, length us, event | category | flops | bytes accessed | tf_op | source)
XLA Modules:
  0.0 46.2 jit_solution(14393011405836900248)
XLA Ops:
  0.6 0.0 copy-start.1
  0.6 0.0 copy-start
  0.7 0.0 copy-start.2
  0.7 0.1 pad_add_fusion.sel_ref
  0.7 1.9 %shard_map.81 = (bf16[2,8,256,128]{3,2,1,0:T(8,128)(2,1)S(1)}, bf16[2,4,264,128]{3,2,1,0:T(8,128)(2,1)S(1)}) custom-call(s32[3]{0:T(128)S(1)} %pad_add_fusion.sel_ref, bf16[512,8,128]{2,1,0:T(8,128)(2,1)} %key_ref.3, bf16[512,8,128]{2,1,0:T(8,128)(2,1)} %value_ref.3, s32[4,128]{1,0:T(4,128)} %bitcast.7), custom_call_target="tpu_custom_call" | custom-call | tf_op jit(solution)/shard_map/pallas_call | solution.py:380
  2.7 4.5 %collective-permute-start.1 = (bf16[2,4,264,128]{3,2,1,0:T(8,128)(2,1)S(1)}, bf16[2,4,264,128]{3,2,1,0:T(8,128)(2,1)S(1)}, u32[]{:S(2)}, u32[]{:S(2)}) collective-permute-start(bf16[2,4,264,128]{3,2,1,0:T(8,128)(2,1)S(1)} %get-tuple-element.50), channel_id=1, source_target_pairs={{0,2},{2,4},{4,6},{6,8},{8,10},{10,12},{12,14},{14,16},{16,18},{18... | collective-permute-start | bytes 1622024 | tf_op jit(solution)/shard_map/ppermute | solution.py:347
  7.2 0.0 copy-done.1
  7.2 0.0 copy-done
  7.2 0.0 copy-done.2
  7.3 6.0 %shard_map.82 = (bf16[512,16,128]{2,1,0:T(8,128)(2,1)}, f32[2,4,512,128]{3,2,1,0:T(8,128)S(1)}, bf16[2,8,256,128]{3,2,1,0:T(8,128)(2,1)S(1)}, bf16[2,4,264,128]{...) custom-call(s32[3]{0:T(128)S(1)} %pad_add_fusion.sel_ref, ...), custom_call_target="tpu_custom_call" | custom-call | flops 10066329600 | bytes 2097152 | tf_op jit(solution)/shard_map/pallas_call | solution.py:380
  13.3 1.9 %collective-permute-start = (bf16[2,4,264,128]{3,2,1,0:T(8,128)(2,1)S(1)}, bf16[2,4,264,128]{3,2,1,0:T(8,128)(2,1)S(1)}, u32[]{:S(2)}, u32[]{:S(2)}) collective-permute-start(bf16[2,4,264,128]{3,2,1,0:T(8,128)(2,1)S(1)} %get-tuple-element.49), channel_id=1, source_target_pairs={{0,2},{2,4},{4,6},{6,8},{8,10},{10,12},{12,14},{14,16},{16,18},{18... | collective-permute-start | bytes 1622024 | tf_op jit(solution)/shard_map/ppermute | solution.py:347
  15.2 0.0 collective-permute-done.1.halo_ref
  15.2 4.8 %shard_map.83 = (bf16[512,16,128]{2,1,0:T(8,128)(2,1)}, bf16[2,4,256,128]{3,2,1,0:T(8,128)(2,1)S(1)}, bf16[2,4,256,128]{3,2,1,0:T(8,128)(2,1)S(1)}, bf16[2,2,128,8,128]{4,3,2,1,0:T(8,128)(2,1)S(1)}) custom-call(s32[3]{0:T(128)S(1)} %pad_add_fusion.sel_ref, s32[4,128]{1,0:T(4,128)S(1)} %bitcast.9, ...), custom_call_target="tpu_custom_call", output_to_operand_aliasing={{0}: (9, {})} | custom-call | flops 10066329600 | bytes 2097152 | tf_op jit(solution)/shard_map/pallas_call | solution.py:380
  20.1 1.3 %collective-permute-start.2 = (bf16[2,4,256,128]{3,2,1,0:T(8,128)(2,1)S(1)}, bf16[2,4,256,128]{3,2,1,0:T(8,128)(2,1)S(1)}, u32[]{:S(2)}, u32[]{:S(2)}) collective-permute-start(bf16[2,4,256,128]{3,2,1,0:T(8,128)(2,1)S(1)} %get-tuple-element.60), channel_id=1, source_target_pairs={{0,1},{1,0},{2,3},{3,2},{4,5},{5,4},{6,7},{7,6},{8,9},{9,8},{10,11... | collective-permute-start | bytes 1572872 | tf_op jit(solution)/shard_map/ppermute | solution.py:351
  21.3 2.7 %collective-permute-start.4 = (bf16[2,4,256,128]{3,2,1,0:T(8,128)(2,1)S(1)}, bf16[2,4,256,128]{3,2,1,0:T(8,128)(2,1)S(1)}, u32[]{:S(2)}, u32[]{:S(2)}) collective-permute-start(bf16[2,4,256,128]{3,2,1,0:T(8,128)(2,1)S(1)} %get-tuple-element.64), channel_id=1, source_target_pairs={{2,0},{4,2},{6,4},{8,6},{10,8},{12,10},{14,12},{16,14},{18,16},{20... | collective-permute-start | bytes 1572872 | tf_op jit(solution)/shard_map/ppermute | solution.py:347
  24.0 0.0 collective-permute-done.halo_ref
  24.0 4.8 %shard_map.84 = (bf16[512,16,128]{2,1,0:T(8,128)(2,1)}, f32[2,4,256,128]{3,2,1,0:T(8,128)S(1)}, bf16[2,4,256,128]{3,2,1,0:T(8,128)(2,1)S(1)}, bf16[2,2,128,8,128]{4,3,2,1,0:T(8,128)(2,1)S(1)}) custom-call(s32[3]{0:T(128)S(1)} %pad_add_fusion.sel_ref, s32[4,128]{1,0:T(4,128)S(1)} %bitcast.10, ...), custom_call_target="tpu_custom_call", output_to_operand_aliasing={{0}: (8, {})} | custom-call | flops 10066329600 | bytes 2097152 | tf_op jit(solution)/shard_map/pallas_call | solution.py:380
  28.8 2.1 %collective-permute-start.3 = (bf16[2,4,256,128]{3,2,1,0:T(8,128)(2,1)S(1)}, bf16[2,4,256,128]{3,2,1,0:T(8,128)(2,1)S(1)}, u32[]{:S(2)}, u32[]{:S(2)}) collective-permute-start(bf16[2,4,256,128]{3,2,1,0:T(8,128)(2,1)S(1)} %get-tuple-element.62), channel_id=1, source_target_pairs={{2,0},{4,2},{6,4},{8,6},{10,8},{12,10},{14,12},{16,14},{18,16},{20... | collective-permute-start | bytes 1572872 | tf_op jit(solution)/shard_map/ppermute | solution.py:347
  30.9 1.4 %collective-permute-done.4 = bf16[2,4,256,128]{3,2,1,0:T(8,128)(2,1)S(1)} collective-permute-done((bf16[2,4,256,128]{3,2,1,0:T(8,128)(2,1)S(1)}, bf16[2,4,256,128]{3,2,1,0:T(8,128)(2,1)S(1)}, u32[]{:S(2)}, u32[]{:S(2)}) %collective-permute-start.4) | collective-permute-done | bytes 524320 | tf_op jit(solution)/shard_map/ppermute | solution.py:347
  32.3 0.1 add_convert_fusion
  32.4 0.3 collective-permute-start.5
  32.7 4.1 %shard_map.85 = (bf16[512,16,128]{2,1,0:T(8,128)(2,1)}, f32[2,4,512,128]{3,2,1,0:T(8,128)S(1)}) custom-call(s32[3]{0:T(128)S(1)} %pad_add_fusion.sel_ref, s32[4,256]{1,0:T(4,128)S(1)} %get-tuple-element.47.low_ref, bf16[2,8,256,128]{3,2,1,0:T(8,128)(2,1)S(1)} %get-tuple-element.48.rest_ref, ...), custom_call_target="tpu_custom_call", output_to_operand_aliasing={{0}: (5, {})} | custom-call | flops 10066329600 | bytes 2097152 | tf_op jit(solution)/shard_map/pallas_call | solution.py:380
  36.8 0.0 collective-permute-done.2.first_in
  36.8 2.8 %collective-permute-done.3.back_in = bf16[2,4,256,128]{3,2,1,0:T(8,128)(2,1)S(1)} collective-permute-done((bf16[2,4,256,128]{3,2,1,0:T(8,128)(2,1)S(1)}, bf16[2,4,256,128]{3,2,1,0:T(8,128)(2,1)S(1)}, u32[]{:S(2)}, u32[]{:S(2)}) %collective-permute-start.3) | collective-permute-done | bytes 524320 | tf_op jit(solution)/shard_map/ppermute | solution.py:347
  39.6 1.1 %shard_map.86 = (bf16[512,4,128]{2,1,0:T(4,128)(2,1)}, bf16[512,4,128]{2,1,0:T(4,128)(2,1)}, f32[2,4,256,128]{3,2,1,0:T(8,128)S(1)}) custom-call(f32[2,4,256,128]{3,2,1,0:T(8,128)S(1)} %get-tuple-element.59.early_ref, bf16[2,4,256,128]{3,2,1,0:T(8,128)(2,1)S(1)} %collective-permute-done.2.first_in, f32[2,4,512,128]{3,2,1,0:T(8,128)S(1)} %get-tuple-element.61.part_ref, ...), custom_call_target="tpu_custom_call" | custom-call | tf_op jit(solution)/shard_map/pallas_call | solution.py:380
  40.7 4.3 %collective-permute-done.5.last_in = bf16[2,4,256,128]{3,2,1,0:T(8,128)(2,1)S(1)} collective-permute-done((bf16[2,4,256,128]{3,2,1,0:T(8,128)(2,1)S(1)}, bf16[2,4,256,128]{3,2,1,0:T(8,128)(2,1)S(1)}, u32[]{:S(2)}, u32[]{:S(2)}) %collective-permute-start.5) | collective-permute-done | bytes 524320 | tf_op jit(solution)/shard_map/ppermute | solution.py:351
  45.0 1.0 %shard_map.87 = (bf16[512,4,128]{2,1,0:T(4,128)(2,1)}, bf16[512,4,128]{2,1,0:T(4,128)(2,1)}) custom-call(f32[2,4,256,128]{3,2,1,0:T(8,128)S(1)} %get-tuple-element.63.late_ref, bf16[2,4,256,128]{3,2,1,0:T(8,128)(2,1)S(1)} %collective-permute-done.5.last_in, ...), custom_call_target="tpu_custom_call", output_to_operand_aliasing={{0}: (2, {}), {1}: (3, {})} | custom-call | tf_op jit(solution)/shard_map/pallas_call | solution.py:380
Async XLA Ops:
  0.6 6.6 %copy-start.1 = (bf16[512,8,128]{2,1,0:T(8,128)(2,1)S(1)}, bf16[512,8,128]{2,1,0:T(8,128)(2,1)}, u32[]{:S(2)}) copy-start(bf16[512,8,128]{2,1,0:T(8,128)(2,1)} %value_ref.3) | copy-start | bytes 3145732
  0.6 6.6 %copy-start = (bf16[512,8,128]{2,1,0:T(8,128)(2,1)S(1)}, bf16[512,8,128]{2,1,0:T(8,128)(2,1)}, u32[]{:S(2)}) copy-start(bf16[512,8,128]{2,1,0:T(8,128)(2,1)} %key_ref.3) | copy-start | bytes 3145732
  0.7 6.6 %copy-start.2 = (s32[512]{0:T(512)S(1)}, s32[512]{0:T(512)}, u32[]{:S(2)}) copy-start(s32[512]{0:T(512)} %param.13) | copy-start | bytes 6148
  2.7 12.5 %collective-permute-start.1 = (bf16[2,4,264,128]{3,2,1,0:T(8,128)(2,1)S(1)}, bf16[2,4,264,128]{3,2,1,0:T(8,128)(2,1)S(1)}, u32[]{:S(2)}, u32[]{:S(2)}) collective-permute-start(bf16[2,4,264,128]{3,2,1,0:T(8,128)(2,1)S(1)} %get-tuple-element.50), channel_id=1, source_target_pairs={{0,2},{2,4},{4,6},{6,8},{8,10},{10,12},{12,14},{14,16},{16,18},{18... | collective-permute-start | bytes 1622024 | tf_op jit(solution)/shard_map/ppermute | solution.py:347
  13.3 10.8 %collective-permute-start = (bf16[2,4,264,128]{3,2,1,0:T(8,128)(2,1)S(1)}, bf16[2,4,264,128]{3,2,1,0:T(8,128)(2,1)S(1)}, u32[]{:S(2)}, u32[]{:S(2)}) collective-permute-start(bf16[2,4,264,128]{3,2,1,0:T(8,128)(2,1)S(1)} %get-tuple-element.49), channel_id=1, source_target_pairs={{0,2},{2,4},{4,6},{6,8},{8,10},{10,12},{12,14},{14,16},{16,18},{18... | collective-permute-start | bytes 1622024 | tf_op jit(solution)/shard_map/ppermute | solution.py:347
  20.1 16.7 %collective-permute-start.2 = (bf16[2,4,256,128]{3,2,1,0:T(8,128)(2,1)S(1)}, bf16[2,4,256,128]{3,2,1,0:T(8,128)(2,1)S(1)}, u32[]{:S(2)}, u32[]{:S(2)}) collective-permute-start(bf16[2,4,256,128]{3,2,1,0:T(8,128)(2,1)S(1)} %get-tuple-element.60), channel_id=1, source_target_pairs={{0,1},{1,0},{2,3},{3,2},{4,5},{5,4},{6,7},{7,6},{8,9},{9,8},{10,11... | collective-permute-start | bytes 1572872 | tf_op jit(solution)/shard_map/ppermute | solution.py:351
  21.3 11.0 %collective-permute-start.4 = (bf16[2,4,256,128]{3,2,1,0:T(8,128)(2,1)S(1)}, bf16[2,4,256,128]{3,2,1,0:T(8,128)(2,1)S(1)}, u32[]{:S(2)}, u32[]{:S(2)}) collective-permute-start(bf16[2,4,256,128]{3,2,1,0:T(8,128)(2,1)S(1)} %get-tuple-element.64), channel_id=1, source_target_pairs={{2,0},{4,2},{6,4},{8,6},{10,8},{12,10},{14,12},{16,14},{18,16},{20... | collective-permute-start | bytes 1572872 | tf_op jit(solution)/shard_map/ppermute | solution.py:347
  28.8 10.8 %collective-permute-start.3 = (bf16[2,4,256,128]{3,2,1,0:T(8,128)(2,1)S(1)}, bf16[2,4,256,128]{3,2,1,0:T(8,128)(2,1)S(1)}, u32[]{:S(2)}, u32[]{:S(2)}) collective-permute-start(bf16[2,4,256,128]{3,2,1,0:T(8,128)(2,1)S(1)} %get-tuple-element.62), channel_id=1, source_target_pairs={{2,0},{4,2},{6,4},{8,6},{10,8},{12,10},{14,12},{16,14},{18,16},{20... | collective-permute-start | bytes 1572872 | tf_op jit(solution)/shard_map/ppermute | solution.py:347
  32.4 12.6 %collective-permute-start.5 = (bf16[2,4,256,128]{3,2,1,0:T(8,128)(2,1)S(1)}, bf16[2,4,256,128]{3,2,1,0:T(8,128)(2,1)S(1)}, u32[]{:S(2)}, u32[]{:S(2)}) collective-permute-start(bf16[2,4,256,128]{3,2,1,0:T(8,128)(2,1)S(1)} %add_convert_fusion), channel_id=1, source_target_pairs={{0,1},{1,0},{2,3},{3,2},{4,5},{5,4},{6,7},{7,6},{8,9},{9,8},{10,11... | collective-permute-start | bytes 1572872 | tf_op jit(solution)/shard_map/ppermute | solution.py:351

commit v6 on v5

v6 whole, which is shorter than its diff:
```python
import functools

import jax
import jax.numpy as jnp
from jax import lax
from jax.experimental import pallas as pl
from jax.experimental.pallas import tpu as pltpu
from jax.sharding import PartitionSpec as P


WINDOW = 256
CHUNK = WINDOW // 2
PAD = 8
STEP = 32
MOVED = 1
LOG2E = 1.4426950408889634
F32 = jnp.float32
BF16 = jnp.bfloat16
VMEM = pl.BlockSpec(memory_space=pltpu.VMEM)
SMEM = pl.BlockSpec(memory_space=pltpu.SMEM)
ANY = pl.BlockSpec(memory_space=pl.ANY)
HBM = pl.BlockSpec(memory_space=pltpu.HBM)
MIB = 1024 * 1024


def dot(a, b, contract):
    return lax.dot_general(a, b, (((contract[0],), (contract[1],)), ((), ())), preferred_element_type=F32)


def params(limit):
    return pltpu.CompilerParams(vmem_limit_bytes=limit * MIB)


def count_smaller(column, row):
    return jnp.sum((column < row).astype(F32), axis=0, keepdims=True)


def to_heads(ref, out, i):
    for r in range(0, out.shape[2], STEP):
        out[i, :, r : r + STEP] = jnp.transpose(ref[r : r + STEP], (1, 0, 2))


def tail_kernel(
    sel_ref, key_ref, value_ref, docs_ref, q_ref, do_ref, kv_ref, halo_ref, raw_ref, lead_ref, buf, docs_buf, sem
):
    half = halo_ref.shape[1]
    chunks = docs_ref.shape[0]
    first = key_ref.shape[0] - WINDOW
    moved = pl.ds(sel_ref[0] * half + half - MOVED, MOVED)
    pairs = [(docs_ref, docs_buf)]
    pairs += [(ref.at[pl.ds(first, WINDOW)], buf.at[i]) for i, ref in enumerate((key_ref, value_ref))]
    pairs += [(ref.at[:, moved], lead_ref.at[i]) for i, ref in enumerate((q_ref, do_ref))]
    pairs += [(ref.at[pl.ds(0, first)], raw_ref.at[i]) for i, ref in enumerate((key_ref, value_ref))]
    copies = [pltpu.make_async_copy(*pair, sem.at[n]) for n, pair in enumerate(pairs)]
    for copy in copies:
        copy.start()
    copies[0].wait()
    pad = jnp.zeros((PAD - 2, CHUNK), BF16)
    tail = jnp.concatenate([docs_buf[chunks - 2 :].astype(F32).astype(BF16), pad], 0)
    for i in range(2):
        copies[1 + i].wait()
        to_heads(buf.at[i], kv_ref, i)
        for h in range(half):
            halo_ref[i, h, :WINDOW] = kv_ref[i, sel_ref[0] * half + h]
            halo_ref[i, h, WINDOW:] = tail
    for copy in copies[3:]:
        copy.wait()


def interleave(rows, group):
    shape = (rows.shape[1], rows.shape[1] * group)
    source = lax.div(lax.broadcasted_iota(jnp.int32, shape, 1), jnp.int32(group))
    pick = (lax.broadcasted_iota(jnp.int32, shape, 0) == source).astype(F32).astype(BF16)
    return dot(rows.astype(BF16), pick, (1, 0))


def rest_of_block(sel_ref, raw_ref, docs_ref, tail_ref, kv_ref, halo_ref, low_ref, group):
    half = halo_ref.shape[1]
    chunks = docs_ref.shape[0]
    docs = docs_ref[...].astype(F32)
    columns = docs.T
    counts = []
    for c in range(chunks):
        row = docs[c : c + 1]
        counts.append(sum(count_smaller(columns[:, b : b + 1], row) for b in range(c + 1)))
    counts = jnp.concatenate(counts, 0)
    coarse = jnp.floor(counts * (1.0 / CHUNK))
    split = interleave(jnp.concatenate([coarse, counts - coarse * CHUNK], 0), group)
    mixed = split[:chunks] * CHUNK + split[chunks:]
    base = WINDOW - CHUNK * lax.broadcasted_iota(jnp.int32, (chunks, CHUNK * group), 0)
    low_ref[0] = jnp.concatenate([counts] * group, 1).astype(jnp.int32) + base
    low_ref[1] = mixed.astype(jnp.int32) + base
    for i in range(2):
        to_heads(raw_ref.at[i], kv_ref, i)
    pad = jnp.zeros((PAD - 2, CHUNK), BF16)
    tail = jnp.concatenate([docs[chunks - 2 :].astype(BF16), pad], 0)
    for i in range(2):
        for h in range(half):
            halo_ref[i, h, :WINDOW] = tail_ref[i, sel_ref[1] * half + h]
            halo_ref[i, h, WINDOW:] = tail


def half_grads(items, get_query, get_keys, get_low, scale, group, put_dq, put_block):
    cols = CHUNK * group
    row = lax.broadcasted_iota(jnp.int32, (CHUNK, cols), 0)
    col = lax.broadcasted_iota(jnp.int32, (CHUNK, cols), 1)
    middle = row + CHUNK
    masks = {}
    for source in sorted({item[2] for item in items}):
        old = row > (lax.div(col, jnp.int32(group)) if source else col & (CHUNK - 1))
        old_low = old.astype(F32).astype(BF16)
        masks[source] = (old, jnp.where(old, row, row + 2 * CHUNK), old_low, 1 - old_low)
    dqs, sums, state, left = {}, {}, {}, {}
    for c, h, _, _, keys in items:
        for b in range(3 * keys):
            left[h, c + b] = left.get((h, c + b), 0) + 1
    pending = {}
    for c, h, _, query, _ in items:
        pending[c] = pending.get(c, 0) + query

    def scores(item):
        c, h, source, _, _ = item
        q, do = get_query(c, h, source)
        k, v = get_keys(h, c)
        state[item] = (q, do, k, dot(k, q, (1, 1)), dot(v, do, (1, 1)))

    def soft(item):
        q, do, k, s, dp = state[item]
        old, position, old_low, new_low = masks[item[2]]
        low = get_low(item[0], item[2])
        s = [
            jnp.where(position >= low, jnp.where(old, s[:CHUNK], s[2 * CHUNK :]), -1e30),
            jnp.where(middle >= low, s[CHUNK : 2 * CHUNK], -1e30),
        ]
        dp = [jnp.where(old, dp[:CHUNK], dp[2 * CHUNK :]), dp[CHUNK : 2 * CHUNK]]
        top = functools.reduce(jnp.maximum, [jnp.max(x, axis=0, keepdims=True) for x in s])
        w = [jnp.exp2((x - top) * (scale * LOG2E)) for x in s]
        total = sum(jnp.sum(x, axis=0, keepdims=True) for x in w)
        inverse = 1.0 / total
        p = [x * inverse for x in w]
        delta = sum(jnp.sum(x * y, axis=0, keepdims=True) for x, y in zip(p, dp))
        ds = [(x * (y - delta)).astype(BF16) for x, y in zip(p, dp)]
        p = [x.astype(BF16) for x in p]
        p = jnp.concatenate([p[0] * old_low, p[1], p[0] * new_low], 0) if item[4] else None
        ds = jnp.concatenate([ds[0] * old_low, ds[1], ds[0] * new_low], 0)
        state[item] = (q, do, k, p, ds)

    def grads(item):
        c, h, _, query, keys = item
        q, do, k, p, ds = state.pop(item)
        if keys:
            dv = dot(p, do, (1, 0))
            dk = dot(ds, q, (1, 0))
        for b in range(3 * keys):
            rows = slice(b * CHUNK, (b + 1) * CHUNK)
            key = (h, c + b)
            new = (dk[rows], dv[rows])
            if key in sums:
                new = (sums[key][0] + new[0], sums[key][1] + new[1])
            sums[key] = new
            left[key] -= 1
            if not left[key]:
                put_block(h, c + b, *sums.pop(key))
        if query:
            dqs[c, h] = (dot(k.T, ds, (1, 0)) * scale).T.astype(BF16).reshape(group, CHUNK, -1)
            pending[c] -= 1
            if not pending[c]:
                heads = sorted(i for a, i in dqs if a == c)
                full = jnp.concatenate([dqs.pop((c, i)) for i in heads], 0)
                put_dq(c, jnp.transpose(full, (1, 0, 2)))

    scores(items[0])
    for n, item in enumerate(items):
        if n + 1 < len(items):
            scores(items[n + 1])
        if n:
            grads(items[n - 1])
        soft(item)
    grads(items[-1])


def store_before(dq_ref, staged_ref, sem, sel, chunks, rows):
    where = pl.ds(pl.multiple_of(sel * rows, rows), rows)
    return [
        pltpu.make_async_copy(staged_ref.at[c], dq_ref.at[pl.ds(chunk * CHUNK, CHUNK), where, :], sem.at[c])
        for c, chunk in enumerate(chunks)
    ]


def run_half(sel, chunks, items, group, half, q_ref, do_ref, lead_ref, get_keys, get_low, put_block, staged_ref):
    rows = half * group
    size = q_ref.shape[-1]
    where = pl.ds(pl.multiple_of(sel * rows, rows), rows)
    held = {}

    def get_query(c, h, source):
        if source:
            columns = slice(chunks[c] * CHUNK * group, (chunks[c] + 1) * CHUNK * group)
            return lead_ref[0, columns], lead_ref[1, columns]
        if c not in held:
            tokens = slice(chunks[c] * CHUNK, (chunks[c] + 1) * CHUNK)
            held[c] = [jnp.transpose(ref[tokens, where, :], (1, 0, 2)) for ref in (q_ref, do_ref)]
        return [x[h * group : (h + 1) * group].reshape(group * CHUNK, size) for x in held[c]]

    def put_dq(c, value):
        staged_ref[c] = value

    half_grads(items, get_query, get_keys, get_low, 1.0 / size**0.5, group, put_dq, put_block)


def partner_items(chunks, half):
    return [(c, h, 0, True, h < half - MOVED) for c in range(len(chunks)) for h in range(half)]


def own_items(chunks, half):
    items = []
    for c in range(len(chunks)):
        items += [(c, h, 0, True, True) for h in range(half)]
        items += [(c, half - MOVED, 1, False, True)]
    return items


def run_late(sel, chunks, items, group, half, q_ref, do_ref, lead_ref, rest_ref, tail_ref, low_ref, staged_ref, part_ref):
    scale = 1.0 / part_ref.shape[-1] ** 0.5
    rest = rest_ref.shape[2]

    def get_keys(h, c):
        start, stop = (chunks[c] - 2) * CHUNK, (chunks[c] + 1) * CHUNK
        pieces = []
        for i in range(2):
            parts = []
            if start < rest:
                parts.append(rest_ref[i, sel * half + h, start : min(stop, rest)])
            if stop > rest:
                parts.append(tail_ref[i, sel * half + h, max(start - rest, 0) : stop - rest])
            pieces.append(jnp.concatenate(parts, 0))
        return pieces

    def put_block(h, b, dk, dv):
        block = slice((chunks[0] - 2 + b) * CHUNK, (chunks[0] - 1 + b) * CHUNK)
        part_ref[0, h, block] = dk * scale
        part_ref[1, h, block] = dv

    def get_low(c, source):
        return low_ref[source, chunks[c] : chunks[c] + 1, :]

    run_half(sel, chunks, items, group, half, q_ref, do_ref, lead_ref, get_keys, get_low, put_block, staged_ref)


def first_kernel(
    sel_ref, docs_ref, raw_ref, tail_ref, q_ref, do_ref, staged_ref, part_ref, kv_ref, halo_ref, low_ref, *, chunks, group
):
    half = halo_ref.shape[1]
    rest_of_block(sel_ref, raw_ref, docs_ref, tail_ref, kv_ref, halo_ref, low_ref, group)
    items = partner_items(chunks, half)
    run_late(
        sel_ref[0], chunks, items, group, half, q_ref, do_ref, None, kv_ref, tail_ref, low_ref, staged_ref, part_ref
    )


def late_kernel(
    sel_ref, low_ref, q_ref, do_ref, lead_ref, rest_ref, tail_ref, before_ref, dq_in, dq_ref, staged_ref, part_ref, sem,
    *, chunks, before, group
):
    half = part_ref.shape[1]
    copies = store_before(dq_ref, before_ref, sem, sel_ref[before[0]], before[1], half * group)
    for copy in copies:
        copy.start()
    items = own_items(chunks, half)
    run_late(
        sel_ref[1], chunks, items, group, half, q_ref, do_ref, lead_ref, rest_ref, tail_ref, low_ref, staged_ref, part_ref
    )
    for copy in copies:
        copy.wait()


def early_kernel(sel_ref, docs_ref, low_ref, q_ref, do_ref, rest_ref, halo_ref, before_ref, *refs, group, n, before):
    extra_ref = refs[0]
    dq_ref, staged_ref, own_ref, back_ref, sem = refs[-5:]
    half = halo_ref.shape[1]
    scale = 1.0 / own_ref.shape[-1] ** 0.5
    sel = sel_ref[n]
    copies = store_before(dq_ref, before_ref, sem, sel_ref[before[0]], before[1], half * group)
    for copy in copies:
        copy.start()
    ahead = jnp.where(sel_ref[2] == 0, -1.0, halo_ref[0, 0, WINDOW:].astype(F32)).T
    counts = []
    for c in range(2):
        docs = docs_ref[c : c + 1, :].astype(F32)
        counts += [count_smaller(ahead[:, b : b + 1], docs) for b in range(2)]
    lows = {}
    if n:
        mixed = interleave(jnp.concatenate(counts, 0), group)
    for c in range(2):
        count = jnp.concatenate([counts[2 * c] + counts[2 * c + 1]] * group, 1)
        lows[c, 0] = low_ref[0, c : c + 1, :] - WINDOW + count.astype(jnp.int32)
        if n:
            count = mixed[2 * c : 2 * c + 1] + mixed[2 * c + 1 : 2 * c + 2]
            lows[c, 1] = low_ref[1, c : c + 1, :] - WINDOW + count.astype(jnp.int32)

    def get_keys(h, c):
        return [
            jnp.concatenate(
                [halo_ref[i, h, c * CHUNK : WINDOW], rest_ref[i, sel * half + h, : (c + 1) * CHUNK]], 0
            )
            for i in range(2)
        ]

    def put_block(h, b, dk, dv):
        dk = dk * scale
        if b < 2:
            block = slice(b * CHUNK, (b + 1) * CHUNK)
            back_ref[0, h, block] = dk.astype(BF16)
            back_ref[1, h, block] = dv.astype(BF16)
        else:
            block = slice((b - 2) * CHUNK, (b - 1) * CHUNK)
            if not n:
                dk, dv = dk + extra_ref[0, h, block], dv + extra_ref[1, h, block]
            own_ref[0, h, block] = dk.astype(own_ref.dtype)
            own_ref[1, h, block] = dv.astype(own_ref.dtype)

    items = own_items((0, 1), half) if n else partner_items((0, 1), half)
    run_half(
        sel, (0, 1), items, group, half, q_ref, do_ref, extra_ref if n else None, get_keys,
        lambda c, source: lows[c, source], put_block, staged_ref
    )
    for copy in copies:
        copy.wait()


def out_rows(buf, sem, i, out, rows):
    return pltpu.make_async_copy(buf.at[i], out.at[rows], sem.at[i])


def begin_kernel(
    sel_ref, early_ref, first_in, part_ref, back_in, before_ref, dq_in, dk_ref, dv_ref, late_ref, dq_ref, buf, sem, dq_sem,
    *, before
):
    late = late_ref.shape[2]
    shared = first_in.shape[1]
    stores = store_before(dq_ref, before_ref, dq_sem, sel_ref[before[0]], before[1], before_ref.shape[2])
    for copy in stores:
        copy.start()
    for i, out in ((0, dk_ref), (1, dv_ref)):
        for r in range(0, WINDOW, STEP):
            rows = slice(r, r + STEP)
            value = early_ref[i, :, rows] + part_ref[i, :, rows]
            value = jnp.concatenate([value[:shared] + first_in[i, :, rows].astype(F32), value[shared:]], 0)
            buf[i, rows] = jnp.transpose(value.astype(BF16), (1, 0, 2))
        out_rows(buf, sem, i, out, pl.ds(0, WINDOW)).start()
        if late > WINDOW:
            late_ref[i, :, : late - WINDOW] = part_ref[i, :, WINDOW:late]
        late_ref[i, :, late - WINDOW :] = part_ref[i, :, late:] + back_in[i].astype(F32)
    for i, out in ((0, dk_ref), (1, dv_ref)):
        out_rows(buf, sem, i, out, pl.ds(0, WINDOW)).wait()
    for copy in stores:
        copy.wait()


def finish_kernel(late_ref, last_in, dk_in, dv_in, dk_ref, dv_ref, buf, sem):
    late = late_ref.shape[2]
    shared = last_in.shape[1]
    for i, out in ((0, dk_ref), (1, dv_ref)):
        for r in range(0, late, STEP):
            rows = slice(r, r + STEP)
            value = late_ref[i, :, rows]
            value = jnp.concatenate([value[:shared] + last_in[i, :, rows].astype(F32), value[shared:]], 0)
            buf[i, rows] = jnp.transpose(value.astype(BF16), (1, 0, 2))
        out_rows(buf, sem, i, out, pl.ds(WINDOW, late)).start()
    for i, out in ((0, dk_ref), (1, dv_ref)):
        out_rows(buf, sem, i, out, pl.ds(WINDOW, late)).wait()


def shift(block, axis, distance):
    devices = range(lax.axis_size(axis))
    return lax.ppermute(block, axis, [(i - distance, i) for i in devices if i - distance in devices])


def swap(block):
    return lax.ppermute(block, "head", [(0, 1), (1, 0)])


def in_hbm(array):
    return pltpu.with_memory_space_constraint(array, pltpu.HBM)


def on_device(queries, key_heads, value_heads, out_grad, doc_ids):
    tokens, kv_count, group, size = queries.shape
    half = kv_count // 2
    shared = half - MOVED
    chunks = tokens // CHUNK
    rest = tokens - WINDOW
    shape = jax.ShapeDtypeStruct
    dma = pltpu.SemaphoreType.DMA
    head = lax.axis_index("head")
    sel = jnp.stack([1 - head, head, lax.axis_index("ctx")]).astype(jnp.int32)
    rows = queries.reshape(tokens, kv_count * group, size)
    grads = out_grad.reshape(tokens, kv_count * group, size)
    docs = doc_ids.reshape(chunks, CHUNK)
    halo_shape = shape((2, half, WINDOW + PAD, size), BF16)
    early_chunks, late_chunks = (0, 1), tuple(range(2, chunks))

    def cost(n):
        work = n * 10 * CHUNK * group * (WINDOW + CHUNK) * size
        return pl.CostEstimate(flops=work * 10, bytes_accessed=n * CHUNK * group * size * 8, transcendentals=0)

    def staged(chunks):
        return shape((len(chunks), CHUNK, half * group, size), BF16)

    def call(body, operands, specs, out_specs, out_shape, scratch, limit, estimate=None, aliases=None):
        return pl.pallas_call(
            body,
            in_specs=specs,
            out_specs=out_specs,
            out_shape=out_shape,
            scratch_shapes=scratch,
            input_output_aliases=aliases or {},
            compiler_params=params(limit),
            cost_estimate=estimate,
        )(*operands)

    tail, halo_other, raw, lead = call(
        tail_kernel,
        (sel, in_hbm(key_heads), in_hbm(value_heads), in_hbm(docs), in_hbm(queries), in_hbm(out_grad)),
        [SMEM] + [HBM] * 5,
        [VMEM] * 4,
        [
            shape((2, kv_count, WINDOW, size), BF16),
            halo_shape,
            shape((2, rest, kv_count, size), BF16),
            shape((2, tokens, MOVED, group, size), BF16),
        ],
        [pltpu.VMEM((2, WINDOW, kv_count, size), BF16), pltpu.VMEM(docs.shape, docs.dtype), dma((7,))],
        16,
    )
    halo_other = shift(halo_other, "ctx", 1)
    lead = swap(lead).reshape(2, tokens * group, size)
    staged_dq, part_other, kv, halo_mine, low = call(
        functools.partial(first_kernel, chunks=late_chunks, group=group),
        (sel, docs, raw, tail, rows, grads),
        [SMEM] + [VMEM] * 5,
        [VMEM] * 5,
        [
            staged(late_chunks),
            shape((2, shared, tokens, size), F32),
            shape((2, kv_count, rest, size), BF16),
            halo_shape,
            shape((2, chunks, CHUNK * group), jnp.int32),
        ],
        [],
        20,
        cost(half * len(late_chunks)),
    )
    halo_mine = shift(halo_mine, "ctx", 1)

    def early(n, halo, extra, heads, staged_dq, query_grad, emit, before):
        operands = [sel, docs, low, rows, grads, kv, halo, staged_dq, extra]
        specs = [SMEM] + [VMEM] * 8
        aliases = {}
        if query_grad is not None:
            aliases = {len(operands): 0}
            operands.append(query_grad)
            specs.append(ANY)
        return call(
            functools.partial(early_kernel, group=group, n=n, before=before),
            operands,
            specs,
            [ANY, VMEM, VMEM, VMEM],
            [
                shape(rows.shape, BF16),
                staged(early_chunks),
                shape((2, heads, WINDOW, size), emit),
                shape((2, heads, WINDOW, size), BF16),
            ],
            [dma((len(before[1]),))],
            20,
            cost(half * 2),
            aliases,
        )

    query_grad, staged_dq, first_other, back_other = early(
        0, halo_other, part_other, shared, staged_dq, None, BF16, (0, late_chunks)
    )
    back_other = shift(back_other, "ctx", -1)
    first_other = swap(first_other)
    query_grad, staged_dq, early_mine, back_mine = early(
        1, halo_mine, lead, half, staged_dq, query_grad, F32, (0, early_chunks)
    )
    back_mine = shift(back_mine, "ctx", -1)
    last_other = part_other[:, :, WINDOW:]
    last_other = last_other.at[:, :, tokens - 2 * WINDOW :].add(back_other.astype(F32)).astype(BF16)
    last_other = swap(last_other)
    query_grad, staged_dq, part_mine = call(
        functools.partial(late_kernel, chunks=late_chunks, before=(1, early_chunks), group=group),
        (sel, low, rows, grads, lead, kv, tail, staged_dq, query_grad),
        [SMEM] + [VMEM] * 7 + [ANY],
        [ANY, VMEM, VMEM],
        [shape(rows.shape, BF16), staged(late_chunks), shape((2, half, tokens, size), F32)],
        [dma((len(early_chunks),))],
        20,
        cost(half * len(late_chunks)),
        {8: 0},
    )
    out = shape((tokens, half, size), BF16)
    key_grad, value_grad, late_sum, query_grad = call(
        functools.partial(begin_kernel, before=(1, late_chunks)),
        (sel, early_mine, first_other, part_mine, back_mine, staged_dq, query_grad),
        [SMEM] + [VMEM] * 5 + [ANY],
        [ANY, ANY, VMEM, ANY],
        [out, out, shape((2, half, rest, size), F32), shape(rows.shape, BF16)],
        [pltpu.VMEM((2, WINDOW, half, size), BF16), dma((2,)), dma((len(late_chunks),))],
        8,
        aliases={6: 3},
    )
    key_grad, value_grad = call(
        finish_kernel,
        (late_sum, last_other, key_grad, value_grad),
        [VMEM, VMEM, ANY, ANY],
        [ANY, ANY],
        [out, out],
        [pltpu.VMEM((2, rest, half, size), BF16), dma((2,))],
        8,
        aliases={2: 0, 3: 1},
    )
    return query_grad.reshape(queries.shape), key_grad, value_grad


def solution(mesh):
    in_specs = (
        P("ctx", None, "head", None),
        P("ctx", None, None),
        P("ctx", None, None),
        P("ctx", None, "head", None),
        P("ctx"),
    )
    out_specs = (P("ctx", None, "head", None), P("ctx", "head", None), P("ctx", "head", None))

    return jax.shard_map(on_device, mesh=mesh, in_specs=in_specs, out_specs=out_specs, check_vma=False)
```

time: 46.8 us -> 42.5 us (0.908)
  the two profiles are of different devices: /device:TPU:1 before, /device:TPU:12 now
where the time goes in v6:
time: 42.5 us; the launch traced here: 42.3 us
  Pallas kernels  20.7 us (49%)
  starting transfers between devices  14.6 us (34%)
  waiting for transfers between devices  5.81 us (14%)
  between operations  0.94 us (2%)
    pallas_call x7, Pallas kernels, call(): pl.pallas_call(body, in_specs=specs, out_specs=out_specs, out_shape=out_s...  20.7 us
    ppermute x4, starting transfers between devices, shift(): lax.ppermute(block, axis, [(i - distance, i) for i in devices if i - dist...  10.9 us
    ppermute x3, starting transfers between devices, swap(): return lax.ppermute(block, 'head', [(0, 1), (1, 0)])  3.7 us
    ppermute x3, waiting for transfers between devices, swap(): return lax.ppermute(block, 'head', [(0, 1), (1, 0)])  3.37 us
    ppermute x4, waiting for transfers between devices, shift(): lax.ppermute(block, axis, [(i - distance, i) for i in devices if i - dist...  2.43 us
  transfers between devices with their start and end apart: 7, of which 3 were waited for; matrix products, arithmetic and copies ran while one was open for 0% of the time, Pallas kernels for 40%

profile of v6, /device:TPU:12, one launch (start us, length us, event | category | flops | bytes accessed | tf_op | source)
XLA Modules:
  0.0 42.3 jit_solution(1522007351606714885)
XLA Ops:
  0.6 0.1 pad_add_fusion.sel_ref
  0.7 0.0 copy-start
  0.7 0.0 copy-start.1
  0.7 0.0 copy-start.2
  0.7 2.6 %shard_map.81 = (bf16[2,8,256,128]{3,2,1,0:T(8,128)(2,1)S(1)}, bf16[2,4,264,128]{3,2,1,0:T(8,128)(2,1)S(1)}, bf16[2,256,8,128]{3,2,1,0:T(8,128)(2,1)S(1)}, bf16[2,512,1,2,128]{4,3,2,1,0:T(2,128)(2,1)S(1)}) custom-call(s32[3]{0:T(128)S(1)} %pad_add_fusion.sel_ref, bf16[512,8,128]{2,1,0:T(8,128)(2,1)} %key_ref.1, bf16[512,8,128]{2,1,0:T(8,128)(2,1)} %value_ref.1, ...), custom_call_target="tpu_custom_call" | custom-call | tf_op jit(solution)/shard_map/pallas_call | solution.py:411
  3.3 1.6 %collective-permute-start.2 = (bf16[2,512,1,2,128]{4,3,2,1,0:T(2,128)(2,1)S(1)}, bf16[2,512,1,2,128]{4,3,2,1,0:T(2,128)(2,1)S(1)}, u32[]{:S(2)}, u32[]{:S(2)}) collective-permute-start(bf16[2,512,1,2,128]{4,3,2,1,0:T(2,128)(2,1)S(1)} %get-tuple-element.58), channel_id=1, source_target_pairs={{0,1},{1,0},{2,3},{3,2},{4,5},{5,4},{6,7},{7,6},{8,9},{9,8},{10,11... | collective-permute-start | bytes 1572872 | tf_op jit(solution)/shard_map/ppermute | solution.py:380
  4.8 1.9 %collective-permute-start.1 = (bf16[2,4,264,128]{3,2,1,0:T(8,128)(2,1)S(1)}, bf16[2,4,264,128]{3,2,1,0:T(8,128)(2,1)S(1)}, u32[]{:S(2)}, u32[]{:S(2)}) collective-permute-start(bf16[2,4,264,128]{3,2,1,0:T(8,128)(2,1)S(1)} %get-tuple-element.54), channel_id=1, source_target_pairs={{0,2},{2,4},{4,6},{6,8},{8,10},{10,12},{12,14},{14,16},{16,18},{18... | collective-permute-start | bytes 1622024 | tf_op jit(solution)/shard_map/ppermute | solution.py:376
  6.8 0.0 copy-done
  6.8 0.0 copy-done.1
  6.8 0.0 copy-done.2
  6.8 3.5 %shard_map.82 = (bf16[2,128,8,128]{3,2,1,0:T(8,128)(2,1)S(1)}, f32[2,3,512,128]{3,2,1,0:T(8,128)S(1)}, bf16[2,8,256,128]{3,2,1,0:T(8,128)(2,1)S(1)}, bf16[2,4,26...) custom-call(s32[3]{0:T(128)S(1)} %pad_add_fusion.sel_ref, s32[4,128]{1,0:T(4,128)S(1)} %bitcast.17, ...), custom_call_target="tpu_custom_call" | custom-call | flops 10066329600 | bytes 2097152 | tf_op jit(solution)/shard_map/pallas_call | solution.py:411
  10.3 3.5 %collective-permute-start = (bf16[2,4,264,128]{3,2,1,0:T(8,128)(2,1)S(1)}, bf16[2,4,264,128]{3,2,1,0:T(8,128)(2,1)S(1)}, u32[]{:S(2)}, u32[]{:S(2)}) collective-permute-start(bf16[2,4,264,128]{3,2,1,0:T(8,128)(2,1)S(1)} %get-tuple-element.53), channel_id=1, source_target_pairs={{0,2},{2,4},{4,6},{6,8},{8,10},{10,12},{12,14},{14,16},{16,18},{18... | collective-permute-start | bytes 1622024 | tf_op jit(solution)/shard_map/ppermute | solution.py:376
  13.9 1.6 %collective-permute-done.1.halo_ref = bf16[2,4,264,128]{3,2,1,0:T(8,128)(2,1)S(1)} collective-permute-done((bf16[2,4,264,128]{3,2,1,0:T(8,128)(2,1)S(1)}, bf16[2,4,264,128]{3,2,1,0:T(8,128)(2,1)S(1)}, u32[]{:S(2)}, u32[]{:S(2)}) %collective-permute-start.1) | collective-permute-done | bytes 540704 | tf_op jit(solution)/shard_map/ppermute | solution.py:376
  15.5 3.9 %shard_map.83 = (bf16[512,16,128]{2,1,0:T(8,128)(2,1)}, bf16[2,128,8,128]{3,2,1,0:T(8,128)(2,1)S(1)}, bf16[2,3,256,128]{3,2,1,0:T(8,128)(2,1)S(1)}, bf16[2,3,256,128]{3,2,1,0:T(8,128)(2,1)S(1)}) custom-call(s32[3]{0:T(128)S(1)} %pad_add_fusion.sel_ref, s32[4,128]{1,0:T(4,128)S(1)} %bitcast.18, s32[2,4,256]{2,1,0:T(4,128)S(1)} %get-tuple-element.51.low_ref, ...), custom_call_target="tpu_custom_call" | custom-call | flops 10066329600 | bytes 2097152 | tf_op jit(solution)/shard_map/pallas_call | solution.py:411
  19.4 0.6 %collective-permute-start.3 = (bf16[2,3,256,128]{3,2,1,0:T(8,128)(2,1)S(1)}, bf16[2,3,256,128]{3,2,1,0:T(8,128)(2,1)S(1)}, u32[]{:S(2)}, u32[]{:S(2)}) collective-permute-start(bf16[2,3,256,128]{3,2,1,0:T(8,128)(2,1)S(1)} %get-tuple-element.61), channel_id=1, source_target_pairs={{0,1},{1,0},{2,3},{3,2},{4,5},{5,4},{6,7},{7,6},{8,9},{9,8},{10,11... | collective-permute-start | bytes 1179656 | tf_op jit(solution)/shard_map/ppermute | solution.py:380
  20.0 1.9 %collective-permute-start.5 = (bf16[2,3,256,128]{3,2,1,0:T(8,128)(2,1)S(1)}, bf16[2,3,256,128]{3,2,1,0:T(8,128)(2,1)S(1)}, u32[]{:S(2)}, u32[]{:S(2)}) collective-permute-start(bf16[2,3,256,128]{3,2,1,0:T(8,128)(2,1)S(1)} %get-tuple-element.70), channel_id=1, source_target_pairs={{2,0},{4,2},{6,4},{8,6},{10,8},{12,10},{14,12},{16,14},{18,16},{20... | collective-permute-start | bytes 1179656 | tf_op jit(solution)/shard_map/ppermute | solution.py:376
  21.9 0.0 collective-permute-done.2
  21.9 0.0 collective-permute-done.halo_ref
  22.0 4.0 %shard_map.84 = (bf16[512,16,128]{2,1,0:T(8,128)(2,1)}, bf16[2,128,8,128]{3,2,1,0:T(8,128)(2,1)S(1)}, f32[2,4,256,128]{3,2,1,0:T(8,128)S(1)}, bf16[2,4,256,128]{3,2,1,0:T(8,128)(2,1)S(1)}) custom-call(s32[3]{0:T(128)S(1)} %pad_add_fusion.sel_ref, s32[4,128]{1,0:T(4,128)S(1)} %bitcast.19, ...), custom_call_target="tpu_custom_call", output_to_operand_aliasing={{0}: (9, {})} | custom-call | flops 10066329600 | bytes 2097152 | tf_op jit(solution)/shard_map/pallas_call | solution.py:411
  26.0 3.6 %collective-permute-start.4 = (bf16[2,4,256,128]{3,2,1,0:T(8,128)(2,1)S(1)}, bf16[2,4,256,128]{3,2,1,0:T(8,128)(2,1)S(1)}, u32[]{:S(2)}, u32[]{:S(2)}) collective-permute-start(bf16[2,4,256,128]{3,2,1,0:T(8,128)(2,1)S(1)} %get-tuple-element.65), channel_id=1, source_target_pairs={{2,0},{4,2},{6,4},{8,6},{10,8},{12,10},{14,12},{16,14},{18,16},{20... | collective-permute-start | bytes 1572872 | tf_op jit(solution)/shard_map/ppermute | solution.py:376
  29.6 0.0 collective-permute-done.5
  29.6 0.1 add_convert_fusion
  29.7 1.5 %collective-permute-start.6 = (bf16[2,3,256,128]{3,2,1,0:T(8,128)(2,1)S(1)}, bf16[2,3,256,128]{3,2,1,0:T(8,128)(2,1)S(1)}, u32[]{:S(2)}, u32[]{:S(2)}) collective-permute-start(bf16[2,3,256,128]{3,2,1,0:T(8,128)(2,1)S(1)} %add_convert_fusion), channel_id=1, source_target_pairs={{0,1},{1,0},{2,3},{3,2},{4,5},{5,4},{6,7},{7,6},{8,9},{9,8},{10,11... | collective-permute-start | bytes 1179656 | tf_op jit(solution)/shard_map/ppermute | solution.py:380
  31.3 4.0 %shard_map.85 = (bf16[512,16,128]{2,1,0:T(8,128)(2,1)}, bf16[2,128,8,128]{3,2,1,0:T(8,128)(2,1)S(1)}, f32[2,4,512,128]{3,2,1,0:T(8,128)S(1)}) custom-call(s32[3]{0:T(128)S(1)} %pad_add_fusion.sel_ref, s32[2,4,256]{2,1,0:T(4,128)S(1)} %get-tuple-element.51.low_ref, bf16[512,16,128]{2,1,0:T(8,128)(2,1)S(1)} %bitcast.11, ...), custom_call_target="tpu_custom_call", output_to_operand_aliasing={{0}: (8, {})} | custom-call | flops 10066329600 | bytes 2097152 | tf_op jit(solution)/shard_map/pallas_call | solution.py:411
  35.3 0.0 collective-permute-done.3.first_in
  35.3 0.8 %collective-permute-done.4.back_in = bf16[2,4,256,128]{3,2,1,0:T(8,128)(2,1)S(1)} collective-permute-done((bf16[2,4,256,128]{3,2,1,0:T(8,128)(2,1)S(1)}, bf16[2,4,256,128]{3,2,1,0:T(8,128)(2,1)S(1)}, u32[]{:S(2)}, u32[]{:S(2)}) %collective-permute-start.4) | collective-permute-done | bytes 524320 | tf_op jit(solution)/shard_map/ppermute | solution.py:376
  36.1 1.6 %shard_map.86 = (bf16[512,4,128]{2,1,0:T(4,128)(2,1)}, bf16[512,4,128]{2,1,0:T(4,128)(2,1)}, f32[2,4,256,128]{3,2,1,0:T(8,128)S(1)}, bf16[512,16,128]{2,1,0:T(8,128)(2,1)}) custom-call(s32[3]{0:T(128)S(1)} %pad_add_fusion.sel_ref, f32[2,4,256,128]{3,2,1,0:T(8,128)S(1)} %get-tuple-element.60.early_ref, ...), custom_call_target="tpu_custom_call", output_to_operand_aliasing={{3}: (6, {})} | custom-call | tf_op jit(solution)/shard_map/pallas_call | solution.py:411
  37.7 3.4 %collective-permute-done.6.last_in = bf16[2,3,256,128]{3,2,1,0:T(8,128)(2,1)S(1)} collective-permute-done((bf16[2,3,256,128]{3,2,1,0:T(8,128)(2,1)S(1)}, bf16[2,3,256,128]{3,2,1,0:T(8,128)(2,1)S(1)}, u32[]{:S(2)}, u32[]{:S(2)}) %collective-permute-start.6) | collective-permute-done | bytes 393248 | tf_op jit(solution)/shard_map/ppermute | solution.py:380
  41.1 1.0 %shard_map.87 = (bf16[512,4,128]{2,1,0:T(4,128)(2,1)}, bf16[512,4,128]{2,1,0:T(4,128)(2,1)}) custom-call(f32[2,4,256,128]{3,2,1,0:T(8,128)S(1)} %get-tuple-element.69.late_ref, bf16[2,3,256,128]{3,2,1,0:T(8,128)(2,1)S(1)} %collective-permute-done.6.last_in, ...), custom_call_target="tpu_custom_call", output_to_operand_aliasing={{0}: (2, {}), {1}: (3, {})} | custom-call | tf_op jit(solution)/shard_map/pallas_call | solution.py:411
Async XLA Ops:
  0.7 6.0 %copy-start = (bf16[512,8,2,128]{3,2,1,0:T(2,128)(2,1)S(1)}, bf16[512,8,2,128]{3,2,1,0:T(2,128)(2,1)}, u32[]{:S(2)}) copy-start(bf16[512,8,2,128]{3,2,1,0:T(2,128)(2,1)} %q_ref.1) | copy-start | bytes 6291460
  0.7 6.1 %copy-start.1 = (bf16[512,8,2,128]{3,2,1,0:T(2,128)(2,1)S(1)}, bf16[512,8,2,128]{3,2,1,0:T(2,128)(2,1)}, u32[]{:S(2)}) copy-start(bf16[512,8,2,128]{3,2,1,0:T(2,128)(2,1)} %do_ref.1) | copy-start | bytes 6291460
  0.7 6.1 %copy-start.2 = (s32[512]{0:T(512)S(1)}, s32[512]{0:T(512)}, u32[]{:S(2)}) copy-start(s32[512]{0:T(512)} %param.13) | copy-start | bytes 6148
  3.3 18.7 %collective-permute-start.2 = (bf16[2,512,1,2,128]{4,3,2,1,0:T(2,128)(2,1)S(1)}, bf16[2,512,1,2,128]{4,3,2,1,0:T(2,128)(2,1)S(1)}, u32[]{:S(2)}, u32[]{:S(2)}) collective-permute-start(bf16[2,512,1,2,128]{4,3,2,1,0:T(2,128)(2,1)S(1)} %get-tuple-element.58), channel_id=1, source_target_pairs={{0,1},{1,0},{2,3},{3,2},{4,5},{5,4},{6,7},{7,6},{8,9},{9,8},{10,11... | collective-permute-start | bytes 1572872 | tf_op jit(solution)/shard_map/ppermute | solution.py:380
  4.8 10.7 %collective-permute-start.1 = (bf16[2,4,264,128]{3,2,1,0:T(8,128)(2,1)S(1)}, bf16[2,4,264,128]{3,2,1,0:T(8,128)(2,1)S(1)}, u32[]{:S(2)}, u32[]{:S(2)}) collective-permute-start(bf16[2,4,264,128]{3,2,1,0:T(8,128)(2,1)S(1)} %get-tuple-element.54), channel_id=1, source_target_pairs={{0,2},{2,4},{4,6},{6,8},{8,10},{10,12},{12,14},{14,16},{16,18},{18... | collective-permute-start | bytes 1622024 | tf_op jit(solution)/shard_map/ppermute | solution.py:376
  10.3 11.6 %collective-permute-start = (bf16[2,4,264,128]{3,2,1,0:T(8,128)(2,1)S(1)}, bf16[2,4,264,128]{3,2,1,0:T(8,128)(2,1)S(1)}, u32[]{:S(2)}, u32[]{:S(2)}) collective-permute-start(bf16[2,4,264,128]{3,2,1,0:T(8,128)(2,1)S(1)} %get-tuple-element.53), channel_id=1, source_target_pairs={{0,2},{2,4},{4,6},{6,8},{8,10},{10,12},{12,14},{14,16},{16,18},{18... | collective-permute-start | bytes 1622024 | tf_op jit(solution)/shard_map/ppermute | solution.py:376
  19.4 15.9 %collective-permute-start.3 = (bf16[2,3,256,128]{3,2,1,0:T(8,128)(2,1)S(1)}, bf16[2,3,256,128]{3,2,1,0:T(8,128)(2,1)S(1)}, u32[]{:S(2)}, u32[]{:S(2)}) collective-permute-start(bf16[2,3,256,128]{3,2,1,0:T(8,128)(2,1)S(1)} %get-tuple-element.61), channel_id=1, source_target_pairs={{0,1},{1,0},{2,3},{3,2},{4,5},{5,4},{6,7},{7,6},{8,9},{9,8},{10,11... | collective-permute-start | bytes 1179656 | tf_op jit(solution)/shard_map/ppermute | solution.py:380
  20.0 9.6 %collective-permute-start.5 = (bf16[2,3,256,128]{3,2,1,0:T(8,128)(2,1)S(1)}, bf16[2,3,256,128]{3,2,1,0:T(8,128)(2,1)S(1)}, u32[]{:S(2)}, u32[]{:S(2)}) collective-permute-start(bf16[2,3,256,128]{3,2,1,0:T(8,128)(2,1)S(1)} %get-tuple-element.70), channel_id=1, source_target_pairs={{2,0},{4,2},{6,4},{8,6},{10,8},{12,10},{14,12},{16,14},{18,16},{20... | collective-permute-start | bytes 1179656 | tf_op jit(solution)/shard_map/ppermute | solution.py:376
  26.0 10.1 %collective-permute-start.4 = (bf16[2,4,256,128]{3,2,1,0:T(8,128)(2,1)S(1)}, bf16[2,4,256,128]{3,2,1,0:T(8,128)(2,1)S(1)}, u32[]{:S(2)}, u32[]{:S(2)}) collective-permute-start(bf16[2,4,256,128]{3,2,1,0:T(8,128)(2,1)S(1)} %get-tuple-element.65), channel_id=1, source_target_pairs={{2,0},{4,2},{6,4},{8,6},{10,8},{12,10},{14,12},{16,14},{18,16},{20... | collective-permute-start | bytes 1572872 | tf_op jit(solution)/shard_map/ppermute | solution.py:376
  29.7 11.4 %collective-permute-start.6 = (bf16[2,3,256,128]{3,2,1,0:T(8,128)(2,1)S(1)}, bf16[2,3,256,128]{3,2,1,0:T(8,128)(2,1)S(1)}, u32[]{:S(2)}, u32[]{:S(2)}) collective-permute-start(bf16[2,3,256,128]{3,2,1,0:T(8,128)(2,1)S(1)} %add_convert_fusion), channel_id=1, source_target_pairs={{0,1},{1,0},{2,3},{3,2},{4,5},{5,4},{6,7},{7,6},{8,9},{9,8},{10,11... | collective-permute-start | bytes 1179656 | tf_op jit(solution)/shard_map/ppermute | solution.py:380

commit v7 on v6

--- a/solution.py
+++ b/solution.py
@@ -41,9 +41,9 @@
 
 
 def tail_kernel(
-    sel_ref, key_ref, value_ref, docs_ref, q_ref, do_ref, kv_ref, halo_ref, raw_ref, lead_ref, buf, docs_buf, sem
+    sel_ref, key_ref, value_ref, docs_ref, q_ref, do_ref, kv_ref, other_ref, mine_ref, raw_ref, lead_ref, buf, docs_buf, sem
 ):
-    half = halo_ref.shape[1]
+    half = key_ref.shape[1] // 2
     chunks = docs_ref.shape[0]
     first = key_ref.shape[0] - WINDOW
     moved = pl.ds(sel_ref[0] * half + half - MOVED, MOVED)
@@ -61,8 +61,11 @@
         copies[1 + i].wait()
         to_heads(buf.at[i], kv_ref, i)
         for h in range(half):
-            halo_ref[i, h, :WINDOW] = kv_ref[i, sel_ref[0] * half + h]
-            halo_ref[i, h, WINDOW:] = tail
+            out, slot = (other_ref, h) if h < half - MOVED else (mine_ref, h + MOVED)
+            out[i, slot, :WINDOW] = kv_ref[i, sel_ref[0] * half + h]
+            out[i, slot, WINDOW:] = tail
+            mine_ref[i, h, :WINDOW] = kv_ref[i, sel_ref[1] * half + h]
+            mine_ref[i, h, WINDOW:] = tail
     for copy in copies[3:]:
         copy.wait()
 
@@ -74,8 +77,7 @@
     return dot(rows.astype(BF16), pick, (1, 0))
 
 
-def rest_of_block(sel_ref, raw_ref, docs_ref, tail_ref, kv_ref, halo_ref, low_ref, group):
-    half = halo_ref.shape[1]
+def rest_of_block(raw_ref, docs_ref, kv_ref, low_ref, group):
     chunks = docs_ref.shape[0]
     docs = docs_ref[...].astype(F32)
     columns = docs.T
@@ -92,12 +94,6 @@
     low_ref[1] = mixed.astype(jnp.int32) + base
     for i in range(2):
         to_heads(raw_ref.at[i], kv_ref, i)
-    pad = jnp.zeros((PAD - 2, CHUNK), BF16)
-    tail = jnp.concatenate([docs[chunks - 2 :].astype(BF16), pad], 0)
-    for i in range(2):
-        for h in range(half):
-            halo_ref[i, h, :WINDOW] = tail_ref[i, sel_ref[1] * half + h]
-            halo_ref[i, h, WINDOW:] = tail
 
 
 def half_grads(items, get_query, get_keys, get_low, scale, group, put_dq, put_block):
@@ -166,8 +162,7 @@
             pending[c] -= 1
             if not pending[c]:
                 heads = sorted(i for a, i in dqs if a == c)
-                full = jnp.concatenate([dqs.pop((c, i)) for i in heads], 0)
-                put_dq(c, jnp.transpose(full, (1, 0, 2)))
+                put_dq(c, jnp.concatenate([dqs.pop((c, i)) for i in heads], 0))
 
     scores(items[0])
     for n, item in enumerate(items):
@@ -179,10 +174,12 @@
     grads(items[-1])
 
 
-def store_before(dq_ref, staged_ref, sem, sel, chunks, rows):
+def store_before(dq_ref, staged_ref, sem, first, sel, chunks, rows):
     where = pl.ds(pl.multiple_of(sel * rows, rows), rows)
     return [
-        pltpu.make_async_copy(staged_ref.at[c], dq_ref.at[pl.ds(chunk * CHUNK, CHUNK), where, :], sem.at[c])
+        pltpu.make_async_copy(
+            staged_ref.at[c], dq_ref.at[pl.ds(chunk * CHUNK, CHUNK), where, :], sem.at[first + c]
+        )
         for c, chunk in enumerate(chunks)
     ]
 
@@ -203,13 +200,13 @@
         return [x[h * group : (h + 1) * group].reshape(group * CHUNK, size) for x in held[c]]
 
     def put_dq(c, value):
-        staged_ref[c] = value
+        staged_ref[c] = jnp.transpose(value, (1, 0, 2)) if value.shape[0] == rows else value
 
     half_grads(items, get_query, get_keys, get_low, 1.0 / size**0.5, group, put_dq, put_block)
 
 
 def partner_items(chunks, half):
-    return [(c, h, 0, True, h < half - MOVED) for c in range(len(chunks)) for h in range(half)]
+    return [(c, h, 0, True, True) for c in range(len(chunks)) for h in range(half - MOVED)]
 
 
 def own_items(chunks, half):
@@ -220,91 +217,138 @@
     return items
 
 
-def run_late(sel, chunks, items, group, half, q_ref, do_ref, lead_ref, rest_ref, tail_ref, low_ref, staged_ref, part_ref):
-    scale = 1.0 / part_ref.shape[-1] ** 0.5
+def block_keys(rest_ref, tail_ref, head, chunk):
     rest = rest_ref.shape[2]
-
-    def get_keys(h, c):
-        start, stop = (chunks[c] - 2) * CHUNK, (chunks[c] + 1) * CHUNK
-        pieces = []
-        for i in range(2):
-            parts = []
-            if start < rest:
-                parts.append(rest_ref[i, sel * half + h, start : min(stop, rest)])
-            if stop > rest:
-                parts.append(tail_ref[i, sel * half + h, max(start - rest, 0) : stop - rest])
-            pieces.append(jnp.concatenate(parts, 0))
-        return pieces
-
-    def put_block(h, b, dk, dv):
-        block = slice((chunks[0] - 2 + b) * CHUNK, (chunks[0] - 1 + b) * CHUNK)
-        part_ref[0, h, block] = dk * scale
-        part_ref[1, h, block] = dv
-
-    def get_low(c, source):
-        return low_ref[source, chunks[c] : chunks[c] + 1, :]
-
-    run_half(sel, chunks, items, group, half, q_ref, do_ref, lead_ref, get_keys, get_low, put_block, staged_ref)
-
-
-def first_kernel(
-    sel_ref, docs_ref, raw_ref, tail_ref, q_ref, do_ref, staged_ref, part_ref, kv_ref, halo_ref, low_ref, *, chunks, group
-):
-    half = halo_ref.shape[1]
-    rest_of_block(sel_ref, raw_ref, docs_ref, tail_ref, kv_ref, halo_ref, low_ref, group)
-    items = partner_items(chunks, half)
-    run_late(
-        sel_ref[0], chunks, items, group, half, q_ref, do_ref, None, kv_ref, tail_ref, low_ref, staged_ref, part_ref
-    )
-
-
-def late_kernel(
-    sel_ref, low_ref, q_ref, do_ref, lead_ref, rest_ref, tail_ref, before_ref, dq_in, dq_ref, staged_ref, part_ref, sem,
-    *, chunks, before, group
-):
-    half = part_ref.shape[1]
-    copies = store_before(dq_ref, before_ref, sem, sel_ref[before[0]], before[1], half * group)
-    for copy in copies:
-        copy.start()
-    items = own_items(chunks, half)
-    run_late(
-        sel_ref[1], chunks, items, group, half, q_ref, do_ref, lead_ref, rest_ref, tail_ref, low_ref, staged_ref, part_ref
-    )
-    for copy in copies:
-        copy.wait()
-
-
-def early_kernel(sel_ref, docs_ref, low_ref, q_ref, do_ref, rest_ref, halo_ref, before_ref, *refs, group, n, before):
-    extra_ref = refs[0]
-    dq_ref, staged_ref, own_ref, back_ref, sem = refs[-5:]
-    half = halo_ref.shape[1]
-    scale = 1.0 / own_ref.shape[-1] ** 0.5
-    sel = sel_ref[n]
-    copies = store_before(dq_ref, before_ref, sem, sel_ref[before[0]], before[1], half * group)
-    for copy in copies:
-        copy.start()
+    start, stop = (chunk - 2) * CHUNK, (chunk + 1) * CHUNK
+    pieces = []
+    for i in range(2):
+        parts = []
+        if start < rest:
+            parts.append(rest_ref[i, head, start : min(stop, rest)])
+        if stop > rest:
+            parts.append(tail_ref[i, head, max(start - rest, 0) : stop - rest])
+        pieces.append(jnp.concatenate(parts, 0))
+    return pieces
+
+
+def halo_keys(halo_ref, rest_ref, slot, head, chunk):
+    return [
+        jnp.concatenate([halo_ref[i, slot, chunk * CHUNK :WINDOW], rest_ref[i, head, : (chunk + 1) * CHUNK]], 0)
+        for i in range(2)
+    ]
+
+
+def early_lows(sel_ref, docs_ref, low_ref, halo_ref, group, mixed):
     ahead = jnp.where(sel_ref[2] == 0, -1.0, halo_ref[0, 0, WINDOW:].astype(F32)).T
     counts = []
     for c in range(2):
         docs = docs_ref[c : c + 1, :].astype(F32)
         counts += [count_smaller(ahead[:, b : b + 1], docs) for b in range(2)]
     lows = {}
-    if n:
-        mixed = interleave(jnp.concatenate(counts, 0), group)
+    if mixed:
+        spread = interleave(jnp.concatenate(counts, 0), group)
     for c in range(2):
         count = jnp.concatenate([counts[2 * c] + counts[2 * c + 1]] * group, 1)
         lows[c, 0] = low_ref[0, c : c + 1, :] - WINDOW + count.astype(jnp.int32)
-        if n:
-            count = mixed[2 * c : 2 * c + 1] + mixed[2 * c + 1 : 2 * c + 2]
+        if mixed:
+            count = spread[2 * c : 2 * c + 1] + spread[2 * c + 1 : 2 * c + 2]
             lows[c, 1] = low_ref[1, c : c + 1, :] - WINDOW + count.astype(jnp.int32)
+    return lows
+
+
+def run_late(sel, chunks, items, group, half, q_ref, do_ref, lead_ref, rest_ref, tail_ref, low_ref, staged_ref, part_ref):
+    scale = 1.0 / part_ref.shape[-1] ** 0.5
 
     def get_keys(h, c):
-        return [
-            jnp.concatenate(
-                [halo_ref[i, h, c * CHUNK : WINDOW], rest_ref[i, sel * half + h, : (c + 1) * CHUNK]], 0
-            )
-            for i in range(2)
-        ]
+        return block_keys(rest_ref, tail_ref, sel * half + h, chunks[c])
+
+    def put_block(h, b, dk, dv):
+        block = slice((chunks[0] - 2 + b) * CHUNK, (chunks[0] - 1 + b) * CHUNK)
+        part_ref[0, h, block] = dk * scale
+        part_ref[1, h, block] = dv
+
+    def get_low(c, source):
+        return low_ref[source, chunks[c] : chunks[c] + 1, :]
+
+    run_half(sel, chunks, items, group, half, q_ref, do_ref, lead_ref, get_keys, get_low, put_block, staged_ref)
+
+
+def first_kernel(
+    sel_ref, docs_ref, raw_ref, tail_ref, q_ref, do_ref, staged_ref, part_ref, kv_ref, low_ref, *, chunks, group
+):
+    half = kv_ref.shape[1] // 2
+    rest_of_block(raw_ref, docs_ref, kv_ref, low_ref, group)
+    items = partner_items(chunks, half)
+    run_late(
+        sel_ref[0], chunks, items, group, half, q_ref, do_ref, None, kv_ref, tail_ref, low_ref, staged_ref, part_ref
+    )
+
+
+def late_kernel(
+    sel_ref, low_ref, q_ref, do_ref, lead_ref, rest_ref, tail_ref, staged_ref, part_ref, *, chunks, group
+):
+    half = part_ref.shape[1]
+    items = own_items(chunks, half)
+    run_late(
+        sel_ref[1], chunks, items, group, half, q_ref, do_ref, lead_ref, rest_ref, tail_ref, low_ref, staged_ref, part_ref
+    )
+
+
+def moved_kernel(
+    sel_ref, docs_ref, low_ref, q_ref, do_ref, rest_ref, tail_ref, halo_ref, own_early_ref, own_late_ref, early_ref, late_ref,
+    dq_ref, buf, sem, *, chunks, group
+):
+    half = halo_ref.shape[1] - MOVED
+    rows = half * group
+    size = q_ref.shape[-1]
+    early = own_early_ref.shape[0]
+    total = early + len(chunks)
+    copies = store_before(dq_ref, own_early_ref, sem, 0, sel_ref[1], range(early), rows)
+    copies += store_before(dq_ref, own_late_ref, sem, early, sel_ref[1], chunks, rows)
+    for copy in copies:
+        copy.start()
+    where = pl.ds(pl.multiple_of(sel_ref[0] * rows, rows), rows)
+    head = sel_ref[0] * half + half - MOVED
+    lows = early_lows(sel_ref, docs_ref, low_ref, halo_ref, group, False)
+
+    def store(c):
+        target = dq_ref.at[pl.ds(c * CHUNK, CHUNK), where, :]
+        return pltpu.make_async_copy(buf.at[c], target, sem.at[total + c])
+
+    def get_query(c, h, source):
+        tokens = slice(c * CHUNK, (c + 1) * CHUNK)
+        both = [jnp.transpose(ref[tokens, where, :], (1, 0, 2)) for ref in (q_ref, do_ref)]
+        return [x[rows - MOVED * group :].reshape(group * CHUNK, size) for x in both]
+
+    def get_keys(h, c):
+        return halo_keys(halo_ref, rest_ref, half, head, c) if c < early else block_keys(rest_ref, tail_ref, head, c)
+
+    def get_low(c, source):
+        return lows[c, 0] if c < early else low_ref[0, c : c + 1, :]
+
+    def put_dq(c, value):
+        others = early_ref[c] if c < early else late_ref[c - early]
+        buf[c] = jnp.transpose(jnp.concatenate([others, value], 0), (1, 0, 2))
+        store(c).start()
+
+    items = [(c, 0, 0, True, False) for c in range(total)]
+    half_grads(items, get_query, get_keys, get_low, 1.0 / size**0.5, group, put_dq, None)
+    for copy in copies:
+        copy.wait()
+    for c in range(total):
+        store(c).wait()
+
+
+def early_kernel(
+    sel_ref, docs_ref, low_ref, q_ref, do_ref, rest_ref, halo_ref, extra_ref, staged_ref, own_ref, back_ref, *, group, n
+):
+    half = rest_ref.shape[1] // 2
+    scale = 1.0 / own_ref.shape[-1] ** 0.5
+    sel = sel_ref[n]
+    lows = early_lows(sel_ref, docs_ref, low_ref, halo_ref, group, n > 0)
+
+    def get_keys(h, c):
+        return halo_keys(halo_ref, rest_ref, h, sel * half + h, c)
 
     def put_block(h, b, dk, dv):
         dk = dk * scale
@@ -324,23 +368,14 @@
         sel, (0, 1), items, group, half, q_ref, do_ref, extra_ref if n else None, get_keys,
         lambda c, source: lows[c, source], put_block, staged_ref
     )
-    for copy in copies:
-        copy.wait()
 
 
 def out_rows(buf, sem, i, out, rows):
     return pltpu.make_async_copy(buf.at[i], out.at[rows], sem.at[i])
 
 
-def begin_kernel(
-    sel_ref, early_ref, first_in, part_ref, back_in, before_ref, dq_in, dk_ref, dv_ref, late_ref, dq_ref, buf, sem, dq_sem,
-    *, before
-):
-    late = late_ref.shape[2]
+def begin_kernel(early_ref, first_in, part_ref, dk_ref, dv_ref, buf, sem):
     shared = first_in.shape[1]
-    stores = store_before(dq_ref, before_ref, dq_sem, sel_ref[before[0]], before[1], before_ref.shape[2])
-    for copy in stores:
-        copy.start()
     for i, out in ((0, dk_ref), (1, dv_ref)):
         for r in range(0, WINDOW, STEP):
             rows = slice(r, r + STEP)
@@ -348,22 +383,20 @@
             value = jnp.concatenate([value[:shared] + first_in[i, :, rows].astype(F32), value[shared:]], 0)
             buf[i, rows] = jnp.transpose(value.astype(BF16), (1, 0, 2))
         out_rows(buf, sem, i, out, pl.ds(0, WINDOW)).start()
-        if late > WINDOW:
-            late_ref[i, :, : late - WINDOW] = part_ref[i, :, WINDOW:late]
-        late_ref[i, :, late - WINDOW :] = part_ref[i, :, late:] + back_in[i].astype(F32)
     for i, out in ((0, dk_ref), (1, dv_ref)):
         out_rows(buf, sem, i, out, pl.ds(0, WINDOW)).wait()
-    for copy in stores:
-        copy.wait()
-
-
-def finish_kernel(late_ref, last_in, dk_in, dv_in, dk_ref, dv_ref, buf, sem):
-    late = late_ref.shape[2]
+
+
+def finish_kernel(part_ref, last_in, back_in, dk_in, dv_in, dk_ref, dv_ref, buf, sem):
+    late = part_ref.shape[2] - WINDOW
     shared = last_in.shape[1]
     for i, out in ((0, dk_ref), (1, dv_ref)):
         for r in range(0, late, STEP):
             rows = slice(r, r + STEP)
-            value = late_ref[i, :, rows]
+            value = part_ref[i, :, WINDOW + r : WINDOW + r + STEP]
+            skip = late - WINDOW
+            if r >= skip:
+                value = value + back_in[i, :, r - skip : r - skip + STEP].astype(F32)
             value = jnp.concatenate([value[:shared] + last_in[i, :, rows].astype(F32), value[shared:]], 0)
             buf[i, rows] = jnp.transpose(value.astype(BF16), (1, 0, 2))
         out_rows(buf, sem, i, out, pl.ds(WINDOW, late)).start()
@@ -397,7 +430,10 @@
     rows = queries.reshape(tokens, kv_count * group, size)
     grads = out_grad.reshape(tokens, kv_count * group, size)
     docs = doc_ids.reshape(chunks, CHUNK)
-    halo_shape = shape((2, half, WINDOW + PAD, size), BF16)
+
+    def halo_shape(heads):
+        return shape((2, heads, WINDOW + PAD, size), BF16)
+
     early_chunks, late_chunks = (0, 1), tuple(range(2, chunks))
 
     def cost(n):
@@ -406,6 +442,9 @@
 
     def staged(chunks):
         return shape((len(chunks), CHUNK, half * group, size), BF16)
+
+    def by_head(chunks):
+        return shape((len(chunks), shared * group, CHUNK, size), BF16)
 
     def call(body, operands, specs, out_specs, out_shape, scratch, limit, estimate=None, aliases=None):
         return pl.pallas_call(
@@ -419,14 +458,15 @@
             cost_estimate=estimate,
         )(*operands)
 
-    tail, halo_other, raw, lead = call(
+    tail, halo_other, halo_mine, raw, lead = call(
         tail_kernel,
         (sel, in_hbm(key_heads), in_hbm(value_heads), in_hbm(docs), in_hbm(queries), in_hbm(out_grad)),
         [SMEM] + [HBM] * 5,
-        [VMEM] * 4,
+        [VMEM] * 5,
         [
             shape((2, kv_count, WINDOW, size), BF16),
-            halo_shape,
+            halo_shape(shared),
+            halo_shape(half + MOVED),
             shape((2, rest, kv_count, size), BF16),
             shape((2, tokens, MOVED, group, size), BF16),
         ],
@@ -434,93 +474,83 @@
         16,
     )
     halo_other = shift(halo_other, "ctx", 1)
+    halo_mine = shift(halo_mine, "ctx", 1)
     lead = swap(lead).reshape(2, tokens * group, size)
-    staged_dq, part_other, kv, halo_mine, low = call(
+    late_dq, part_other, kv, low = call(
         functools.partial(first_kernel, chunks=late_chunks, group=group),
         (sel, docs, raw, tail, rows, grads),
         [SMEM] + [VMEM] * 5,
-        [VMEM] * 5,
+        [VMEM] * 4,
         [
-            staged(late_chunks),
+            by_head(late_chunks),
             shape((2, shared, tokens, size), F32),
             shape((2, kv_count, rest, size), BF16),
-            halo_shape,
             shape((2, chunks, CHUNK * group), jnp.int32),
         ],
         [],
         20,
         cost(half * len(late_chunks)),
     )
-    halo_mine = shift(halo_mine, "ctx", 1)
-
-    def early(n, halo, extra, heads, staged_dq, query_grad, emit, before):
-        operands = [sel, docs, low, rows, grads, kv, halo, staged_dq, extra]
-        specs = [SMEM] + [VMEM] * 8
-        aliases = {}
-        if query_grad is not None:
-            aliases = {len(operands): 0}
-            operands.append(query_grad)
-            specs.append(ANY)
+
+    def early(n, halo, extra, heads, staged_dq, emit):
         return call(
-            functools.partial(early_kernel, group=group, n=n, before=before),
-            operands,
-            specs,
-            [ANY, VMEM, VMEM, VMEM],
-            [
-                shape(rows.shape, BF16),
-                staged(early_chunks),
-                shape((2, heads, WINDOW, size), emit),
-                shape((2, heads, WINDOW, size), BF16),
-            ],
-            [dma((len(before[1]),))],
+            functools.partial(early_kernel, group=group, n=n),
+            (sel, docs, low, rows, grads, kv, halo, extra),
+            [SMEM] + [VMEM] * 7,
+            [VMEM] * 3,
+            [staged_dq, shape((2, heads, WINDOW, size), emit), shape((2, heads, WINDOW, size), BF16)],
+            [],
             20,
             cost(half * 2),
-            aliases,
         )
 
-    query_grad, staged_dq, first_other, back_other = early(
-        0, halo_other, part_other, shared, staged_dq, None, BF16, (0, late_chunks)
-    )
+    early_dq, first_other, back_other = early(0, halo_other, part_other, shared, by_head(early_chunks), BF16)
     back_other = shift(back_other, "ctx", -1)
     first_other = swap(first_other)
-    query_grad, staged_dq, early_mine, back_mine = early(
-        1, halo_mine, lead, half, staged_dq, query_grad, F32, (0, early_chunks)
-    )
+    own_late_dq, part_mine = call(
+        functools.partial(late_kernel, chunks=late_chunks, group=group),
+        (sel, low, rows, grads, lead, kv, tail),
+        [SMEM] + [VMEM] * 6,
+        [VMEM] * 2,
+        [staged(late_chunks), shape((2, half, tokens, size), F32)],
+        [],
+        20,
+        cost(half * len(late_chunks)),
+    )
+    own_early_dq, early_mine, back_mine = early(1, halo_mine, lead, half, staged(early_chunks), F32)
     back_mine = shift(back_mine, "ctx", -1)
     last_other = part_other[:, :, WINDOW:]
     last_other = last_other.at[:, :, tokens - 2 * WINDOW :].add(back_other.astype(F32)).astype(BF16)
     last_other = swap(last_other)
-    query_grad, staged_dq, part_mine = call(
-        functools.partial(late_kernel, chunks=late_chunks, before=(1, early_chunks), group=group),
-        (sel, low, rows, grads, lead, kv, tail, staged_dq, query_grad),
-        [SMEM] + [VMEM] * 7 + [ANY],
-        [ANY, VMEM, VMEM],
-        [shape(rows.shape, BF16), staged(late_chunks), shape((2, half, tokens, size), F32)],
-        [dma((len(early_chunks),))],
+    query_grad = call(
+        functools.partial(moved_kernel, chunks=late_chunks, group=group),
+        (sel, docs, low, rows, grads, kv, tail, halo_mine, own_early_dq, own_late_dq, early_dq, late_dq),
+        [SMEM] + [VMEM] * 11,
+        ANY,
+        shape(rows.shape, BF16),
+        [pltpu.VMEM((chunks, CHUNK, half * group, size), BF16), dma((2 * chunks,))],
         20,
-        cost(half * len(late_chunks)),
-        {8: 0},
+        cost(chunks),
     )
     out = shape((tokens, half, size), BF16)
-    key_grad, value_grad, late_sum, query_grad = call(
-        functools.partial(begin_kernel, before=(1, late_chunks)),
-        (sel, early_mine, first_other, part_mine, back_mine, staged_dq, query_grad),
-        [SMEM] + [VMEM] * 5 + [ANY],
-        [ANY, ANY, VMEM, ANY],
-        [out, out, shape((2, half, rest, size), F32), shape(rows.shape, BF16)],
-        [pltpu.VMEM((2, WINDOW, half, size), BF16), dma((2,)), dma((len(late_chunks),))],
+    key_grad, value_grad = call(
+        begin_kernel,
+        (early_mine, first_other, part_mine),
+        [VMEM] * 3,
+        [ANY, ANY],
+        [out, out],
+        [pltpu.VMEM((2, WINDOW, half, size), BF16), dma((2,))],
         8,
-        aliases={6: 3},
     )
     key_grad, value_grad = call(
         finish_kernel,
-        (late_sum, last_other, key_grad, value_grad),
-        [VMEM, VMEM, ANY, ANY],
+        (part_mine, last_other, back_mine, key_grad, value_grad),
+        [VMEM] * 3 + [ANY] * 2,
         [ANY, ANY],
         [out, out],
         [pltpu.VMEM((2, rest, half, size), BF16), dma((2,))],
         8,
-        aliases={2: 0, 3: 1},
+        aliases={3: 0, 4: 1},
     )
     return query_grad.reshape(queries.shape), key_grad, value_grad
 

time: 42.5 us -> 42.6 us (level)
  the two profiles are of different devices: /device:TPU:12 before, /device:TPU:10 now
where the time goes in v7:
time: 42.6 us; the launch traced here: 42.4 us
  Pallas kernels  21.3 us (50%)
  starting transfers between devices  12.9 us (30%)
  waiting for transfers between devices  7.09 us (17%)
  between operations  0.93 us (2%)
    pallas_call x8, Pallas kernels, call(): pl.pallas_call(body, in_specs=specs, out_specs=out_specs, out_shape=out_s...  21.3 us
    ppermute x4, starting transfers between devices, shift(): lax.ppermute(block, axis, [(i - distance, i) for i in devices if i - dist...  10.2 us
    ppermute x3, waiting for transfers between devices, swap(): return lax.ppermute(block, 'head', [(0, 1), (1, 0)])  5.92 us
    ppermute x3, starting transfers between devices, swap(): return lax.ppermute(block, 'head', [(0, 1), (1, 0)])  2.78 us
    ppermute x4, waiting for transfers between devices, shift(): lax.ppermute(block, axis, [(i - distance, i) for i in devices if i - dist...  1.17 us
  transfers between devices with their start and end apart: 7, of which 2 were waited for; matrix products, arithmetic and copies ran while one was open for 0% of the time, Pallas kernels for 42%

profile of v7, /device:TPU:10, one launch (start us, length us, event | category | flops | bytes accessed | tf_op | source)
XLA Modules:
  0.0 42.4 jit_solution(11393735666298548436)
XLA Ops:
  0.6 0.1 pad_add_fusion.sel_ref
  0.7 0.0 copy-start
  0.7 0.0 copy-start.1
  0.7 0.0 copy-start.2
  0.7 2.6 %shard_map.81 = (bf16[2,8,256,128]{3,2,1,0:T(8,128)(2,1)S(1)}, bf16[2,3,264,128]{3,2,1,0:T(8,128)(2,1)S(1)}, bf16[2,5,264,128]{3,2,1,0:T(8,128)(2,1)S(1)}, bf16[...) custom-call(s32[3]{0:T(128)S(1)} %pad_add_fusion.sel_ref, bf16[512,8,128]{2,1,0:T(8,128)(2,1)} %key_ref.1, ...), custom_call_target="tpu_custom_call" | custom-call | tf_op jit(solution)/shard_map/pallas_call | solution.py:450
  3.3 1.9 %collective-permute-start.2 = (bf16[2,3,264,128]{3,2,1,0:T(8,128)(2,1)S(1)}, bf16[2,3,264,128]{3,2,1,0:T(8,128)(2,1)S(1)}, u32[]{:S(2)}, u32[]{:S(2)}) collective-permute-start(bf16[2,3,264,128]{3,2,1,0:T(8,128)(2,1)S(1)} %get-tuple-element.52), channel_id=1, source_target_pairs={{0,2},{2,4},{4,6},{6,8},{8,10},{10,12},{12,14},{14,16},{16,18},{18... | collective-permute-start | bytes 1216520 | tf_op jit(solution)/shard_map/ppermute | solution.py:409
  5.2 0.6 %collective-permute-start.1 = (bf16[2,512,1,2,128]{4,3,2,1,0:T(2,128)(2,1)S(1)}, bf16[2,512,1,2,128]{4,3,2,1,0:T(2,128)(2,1)S(1)}, u32[]{:S(2)}, u32[]{:S(2)}) collective-permute-start(bf16[2,512,1,2,128]{4,3,2,1,0:T(2,128)(2,1)S(1)} %get-tuple-element.49), channel_id=1, source_target_pairs={{0,1},{1,0},{2,3},{3,2},{4,5},{5,4},{6,7},{7,6},{8,9},{9,8},{10,11... | collective-permute-start | bytes 1572872 | tf_op jit(solution)/shard_map/ppermute | solution.py:413
  5.8 3.2 %collective-permute-start = (bf16[2,5,264,128]{3,2,1,0:T(8,128)(2,1)S(1)}, bf16[2,5,264,128]{3,2,1,0:T(8,128)(2,1)S(1)}, u32[]{:S(2)}, u32[]{:S(2)}) collective-permute-start(bf16[2,5,264,128]{3,2,1,0:T(8,128)(2,1)S(1)} %get-tuple-element.48), channel_id=1, source_target_pairs={{0,2},{2,4},{4,6},{6,8},{8,10},{10,12},{12,14},{14,16},{16,18},{18... | collective-permute-start | bytes 2027528 | tf_op jit(solution)/shard_map/ppermute | solution.py:409
  9.1 0.0 copy-done
  9.1 0.0 copy-done.1
  9.1 0.0 copy-done.2
  9.1 3.2 %shard_map.82 = (bf16[2,6,128,128]{3,2,1,0:T(8,128)(2,1)S(1)}, f32[2,3,512,128]{3,2,1,0:T(8,128)S(1)}, bf16[2,8,256,128]{3,2,1,0:T(8,128)(2,1)S(1)}, s32[2,4,256]{2,1,0:T(4,128)S(1)}) custom-call(s32[3]{0:T(128)S(1)} %pad_add_fusion.sel_ref, s32[4,128]{1,0:T(4,128)S(1)} %bitcast.19, bf16[2,256,8,128]{3,2,1,0:T(8,128)(2,1)S(1)} %get-tuple-element.44.raw_ref, ...), custom_call_target="tpu_custom_call" | custom-call | flops 10066329600 | bytes 2097152 | tf_op jit(solution)/shard_map/pallas_call | solution.py:450
  12.2 1.2 %collective-permute-done.2.halo_ref = bf16[2,3,264,128]{3,2,1,0:T(8,128)(2,1)S(1)} collective-permute-done((bf16[2,3,264,128]{3,2,1,0:T(8,128)(2,1)S(1)}, bf16[2,3,264,128]{3,2,1,0:T(8,128)(2,1)S(1)}, u32[]{:S(2)}, u32[]{:S(2)}) %collective-permute-start.2) | collective-permute-done | bytes 405536 | tf_op jit(solution)/shard_map/ppermute | solution.py:409
  13.4 2.8 %shard_map.85 = (bf16[2,6,128,128]{3,2,1,0:T(8,128)(2,1)S(1)}, bf16[2,3,256,128]{3,2,1,0:T(8,128)(2,1)S(1)}, bf16[2,3,256,128]{3,2,1,0:T(8,128)(2,1)S(1)}) custom-call(s32[3]{0:T(128)S(1)} %pad_add_fusion.sel_ref, s32[4,128]{1,0:T(4,128)S(1)} %bitcast.20, s32[2,4,256]{2,1,0:T(4,128)S(1)} %get-tuple-element.46.low_ref, bf16[512,16,128]{2,1,0:T(8,128)(2,1)S(1)} %bitcast.9, ...), custom_call_target="tpu_custom_call" | custom-call | flops 10066329600 | bytes 2097152 | tf_op jit(solution)/shard_map/pallas_call | solution.py:450
  16.2 2.2 %collective-permute-start.3 = (bf16[2,3,256,128]{3,2,1,0:T(8,128)(2,1)S(1)}, bf16[2,3,256,128]{3,2,1,0:T(8,128)(2,1)S(1)}, u32[]{:S(2)}, u32[]{:S(2)}) collective-permute-start(bf16[2,3,256,128]{3,2,1,0:T(8,128)(2,1)S(1)} %get-tuple-element.57), channel_id=1, source_target_pairs={{2,0},{4,2},{6,4},{8,6},{10,8},{12,10},{14,12},{16,14},{18,16},{20... | collective-permute-start | bytes 1179656 | tf_op jit(solution)/shard_map/ppermute | solution.py:409
  18.5 1.6 %collective-permute-start.6 = (bf16[2,3,256,128]{3,2,1,0:T(8,128)(2,1)S(1)}, bf16[2,3,256,128]{3,2,1,0:T(8,128)(2,1)S(1)}, u32[]{:S(2)}, u32[]{:S(2)}) collective-permute-start(bf16[2,3,256,128]{3,2,1,0:T(8,128)(2,1)S(1)} %get-tuple-element.60), channel_id=1, source_target_pairs={{0,1},{1,0},{2,3},{3,2},{4,5},{5,4},{6,7},{7,6},{8,9},{9,8},{10,11... | collective-permute-start | bytes 1179656 | tf_op jit(solution)/shard_map/ppermute | solution.py:413
  20.1 0.0 collective-permute-done.1
  20.1 3.7 %shard_map.84 = (bf16[2,128,8,128]{3,2,1,0:T(8,128)(2,1)S(1)}, f32[2,4,512,128]{3,2,1,0:T(8,128)S(1)}) custom-call(s32[3]{0:T(128)S(1)} %pad_add_fusion.sel_ref, s32[2,4,256]{2,1,0:T(4,128)S(1)} %get-tuple-element.46.low_ref, bf16[512,16,128]{2,1,0:T(8,128)(2,1)S(1)} %bitcast.10, bf16[512,16,128]{2,1,0:T(8,128)(2,1)S(1)} %bitcast.15, ...), custom_call_target="tpu_custom_call" | custom-call | flops 10066329600 | bytes 2097152 | tf_op jit(solution)/shard_map/pallas_call | solution.py:450
  23.8 0.0 collective-permute-done.halo_ref
  23.8 3.8 %shard_map.83 = (bf16[2,128,8,128]{3,2,1,0:T(8,128)(2,1)S(1)}, f32[2,4,256,128]{3,2,1,0:T(8,128)S(1)}, bf16[2,4,256,128]{3,2,1,0:T(8,128)(2,1)S(1)}) custom-call(s32[3]{0:T(128)S(1)} %pad_add_fusion.sel_ref, s32[4,128]{1,0:T(4,128)S(1)} %bitcast.21, s32[2,4,256]{2,1,0:T(4,128)S(1)} %get-tuple-element.46.low_ref, bf16[512,16,128]{2,1,0:T(8,128)(2,1)S(1)} %bitcast.11, ...), custom_call_target="tpu_custom_call" | custom-call | flops 10066329600 | bytes 2097152 | tf_op jit(solution)/shard_map/pallas_call | solution.py:450
  27.6 2.8 %collective-permute-start.5 = (bf16[2,4,256,128]{3,2,1,0:T(8,128)(2,1)S(1)}, bf16[2,4,256,128]{3,2,1,0:T(8,128)(2,1)S(1)}, u32[]{:S(2)}, u32[]{:S(2)}) collective-permute-start(bf16[2,4,256,128]{3,2,1,0:T(8,128)(2,1)S(1)} %get-tuple-element.58), channel_id=1, source_target_pairs={{2,0},{4,2},{6,4},{8,6},{10,8},{12,10},{14,12},{16,14},{18,16},{20... | collective-permute-start | bytes 1572872 | tf_op jit(solution)/shard_map/ppermute | solution.py:409
  30.3 0.0 collective-permute-done.3
  30.3 0.1 add_convert_fusion
  30.5 0.6 %collective-permute-start.4 = (bf16[2,3,256,128]{3,2,1,0:T(8,128)(2,1)S(1)}, bf16[2,3,256,128]{3,2,1,0:T(8,128)(2,1)S(1)}, u32[]{:S(2)}, u32[]{:S(2)}) collective-permute-start(bf16[2,3,256,128]{3,2,1,0:T(8,128)(2,1)S(1)} %add_convert_fusion), channel_id=1, source_target_pairs={{0,1},{1,0},{2,3},{3,2},{4,5},{5,4},{6,7},{7,6},{8,9},{9,8},{10,11... | collective-permute-start | bytes 1179656 | tf_op jit(solution)/shard_map/ppermute | solution.py:413
  31.1 3.1 %shard_map.86 = bf16[512,16,128]{2,1,0:T(8,128)(2,1)} custom-call(s32[3]{0:T(128)S(1)} %pad_add_fusion.sel_ref, s32[4,128]{1,0:T(4,128)S(1)} %bitcast.22, s32[2,4,256]{2,1,0:T(4,128)S(1)} %get-tuple-element.46.low_ref, bf16[512,16,128]{2,1,0:T(8,128)(2,1)S(1)} %bitcast.12, bf16[512,16,128]{2,1,0:T(8,128)(2,1)S(1)} %bitcast.17, ...), custom_call_target="tpu_custom_call" | custom-call | flops 5033164800 | bytes 1048576 | tf_op jit(solution)/shard_map/pallas_call | solution.py:450
  34.2 0.0 collective-permute-done.6.first_in
  34.2 1.1 %shard_map.87 = (bf16[512,4,128]{2,1,0:T(4,128)(2,1)}, bf16[512,4,128]{2,1,0:T(4,128)(2,1)}) custom-call(f32[2,4,256,128]{3,2,1,0:T(8,128)S(1)} %get-tuple-element.59.early_ref, bf16[2,3,256,128]{3,2,1,0:T(8,128)(2,1)S(1)} %collective-permute-done.6.first_in, f32[2,4,512,128]{3,2,1,0:T(8,128)S(1)} %get-tuple-element.56.part_ref), custom_call_target="tpu_custom_call" | custom-call | tf_op jit(solution)/shard_map/pallas_call | solution.py:450
  35.3 5.9 %collective-permute-done.4.last_in = bf16[2,3,256,128]{3,2,1,0:T(8,128)(2,1)S(1)} collective-permute-done((bf16[2,3,256,128]{3,2,1,0:T(8,128)(2,1)S(1)}, bf16[2,3,256,128]{3,2,1,0:T(8,128)(2,1)S(1)}, u32[]{:S(2)}, u32[]{:S(2)}) %collective-permute-start.4) | collective-permute-done | bytes 393248 | tf_op jit(solution)/shard_map/ppermute | solution.py:413
  41.2 0.0 collective-permute-done.5.back_in
  41.2 1.1 %shard_map.88 = (bf16[512,4,128]{2,1,0:T(4,128)(2,1)}, bf16[512,4,128]{2,1,0:T(4,128)(2,1)}) custom-call(f32[2,4,512,128]{3,2,1,0:T(8,128)S(1)} %get-tuple-element.56.part_ref, bf16[2,3,256,128]{3,2,1,0:T(8,128)(2,1)S(1)} %collective-permute-done.4.last_in, ...), custom_call_target="tpu_custom_call", output_to_operand_aliasing={{0}: (3, {}), {1}: (4, {})} | custom-call | tf_op jit(solution)/shard_map/pallas_call | solution.py:450
Async XLA Ops:
  0.7 8.3 %copy-start = (bf16[512,8,2,128]{3,2,1,0:T(2,128)(2,1)S(1)}, bf16[512,8,2,128]{3,2,1,0:T(2,128)(2,1)}, u32[]{:S(2)}) copy-start(bf16[512,8,2,128]{3,2,1,0:T(2,128)(2,1)} %q_ref.1) | copy-start | bytes 6291460
  0.7 8.4 %copy-start.1 = (bf16[512,8,2,128]{3,2,1,0:T(2,128)(2,1)S(1)}, bf16[512,8,2,128]{3,2,1,0:T(2,128)(2,1)}, u32[]{:S(2)}) copy-start(bf16[512,8,2,128]{3,2,1,0:T(2,128)(2,1)} %do_ref.1) | copy-start | bytes 6291460
  0.7 8.4 %copy-start.2 = (s32[512]{0:T(512)S(1)}, s32[512]{0:T(512)}, u32[]{:S(2)}) copy-start(s32[512]{0:T(512)} %param.13) | copy-start | bytes 6148
  3.3 10.1 %collective-permute-start.2 = (bf16[2,3,264,128]{3,2,1,0:T(8,128)(2,1)S(1)}, bf16[2,3,264,128]{3,2,1,0:T(8,128)(2,1)S(1)}, u32[]{:S(2)}, u32[]{:S(2)}) collective-permute-start(bf16[2,3,264,128]{3,2,1,0:T(8,128)(2,1)S(1)} %get-tuple-element.52), channel_id=1, source_target_pairs={{0,2},{2,4},{4,6},{6,8},{8,10},{10,12},{12,14},{14,16},{16,18},{18... | collective-permute-start | bytes 1216520 | tf_op jit(solution)/shard_map/ppermute | solution.py:409
  5.2 14.8 %collective-permute-start.1 = (bf16[2,512,1,2,128]{4,3,2,1,0:T(2,128)(2,1)S(1)}, bf16[2,512,1,2,128]{4,3,2,1,0:T(2,128)(2,1)S(1)}, u32[]{:S(2)}, u32[]{:S(2)}) collective-permute-start(bf16[2,512,1,2,128]{4,3,2,1,0:T(2,128)(2,1)S(1)} %get-tuple-element.49), channel_id=1, source_target_pairs={{0,1},{1,0},{2,3},{3,2},{4,5},{5,4},{6,7},{7,6},{8,9},{9,8},{10,11... | collective-permute-start | bytes 1572872 | tf_op jit(solution)/shard_map/ppermute | solution.py:413
  5.8 17.9 %collective-permute-start = (bf16[2,5,264,128]{3,2,1,0:T(8,128)(2,1)S(1)}, bf16[2,5,264,128]{3,2,1,0:T(8,128)(2,1)S(1)}, u32[]{:S(2)}, u32[]{:S(2)}) collective-permute-start(bf16[2,5,264,128]{3,2,1,0:T(8,128)(2,1)S(1)} %get-tuple-element.48), channel_id=1, source_target_pairs={{0,2},{2,4},{4,6},{6,8},{8,10},{10,12},{12,14},{14,16},{16,18},{18... | collective-permute-start | bytes 2027528 | tf_op jit(solution)/shard_map/ppermute | solution.py:409
  16.2 14.1 %collective-permute-start.3 = (bf16[2,3,256,128]{3,2,1,0:T(8,128)(2,1)S(1)}, bf16[2,3,256,128]{3,2,1,0:T(8,128)(2,1)S(1)}, u32[]{:S(2)}, u32[]{:S(2)}) collective-permute-start(bf16[2,3,256,128]{3,2,1,0:T(8,128)(2,1)S(1)} %get-tuple-element.57), channel_id=1, source_target_pairs={{2,0},{4,2},{6,4},{8,6},{10,8},{12,10},{14,12},{16,14},{18,16},{20... | collective-permute-start | bytes 1179656 | tf_op jit(solution)/shard_map/ppermute | solution.py:409
  18.5 15.7 %collective-permute-start.6 = (bf16[2,3,256,128]{3,2,1,0:T(8,128)(2,1)S(1)}, bf16[2,3,256,128]{3,2,1,0:T(8,128)(2,1)S(1)}, u32[]{:S(2)}, u32[]{:S(2)}) collective-permute-start(bf16[2,3,256,128]{3,2,1,0:T(8,128)(2,1)S(1)} %get-tuple-element.60), channel_id=1, source_target_pairs={{0,1},{1,0},{2,3},{3,2},{4,5},{5,4},{6,7},{7,6},{8,9},{9,8},{10,11... | collective-permute-start | bytes 1179656 | tf_op jit(solution)/shard_map/ppermute | solution.py:413
  27.6 13.6 %collective-permute-start.5 = (bf16[2,4,256,128]{3,2,1,0:T(8,128)(2,1)S(1)}, bf16[2,4,256,128]{3,2,1,0:T(8,128)(2,1)S(1)}, u32[]{:S(2)}, u32[]{:S(2)}) collective-permute-start(bf16[2,4,256,128]{3,2,1,0:T(8,128)(2,1)S(1)} %get-tuple-element.58), channel_id=1, source_target_pairs={{2,0},{4,2},{6,4},{8,6},{10,8},{12,10},{14,12},{16,14},{18,16},{20... | collective-permute-start | bytes 1572872 | tf_op jit(solution)/shard_map/ppermute | solution.py:409
  30.5 10.8 %collective-permute-start.4 = (bf16[2,3,256,128]{3,2,1,0:T(8,128)(2,1)S(1)}, bf16[2,3,256,128]{3,2,1,0:T(8,128)(2,1)S(1)}, u32[]{:S(2)}, u32[]{:S(2)}) collective-permute-start(bf16[2,3,256,128]{3,2,1,0:T(8,128)(2,1)S(1)} %add_convert_fusion), channel_id=1, source_target_pairs={{0,1},{1,0},{2,3},{3,2},{4,5},{5,4},{6,7},{7,6},{8,9},{9,8},{10,11... | collective-permute-start | bytes 1179656 | tf_op jit(solution)/shard_map/ppermute | solution.py:413

commit v8 on v7

--- a/solution.py
+++ b/solution.py
@@ -57,15 +57,15 @@
     copies[0].wait()
     pad = jnp.zeros((PAD - 2, CHUNK), BF16)
     tail = jnp.concatenate([docs_buf[chunks - 2 :].astype(F32).astype(BF16), pad], 0)
+    for out in (other_ref, mine_ref):
+        out[out.shape[0] - PAD :] = tail
     for i in range(2):
         copies[1 + i].wait()
         to_heads(buf.at[i], kv_ref, i)
         for h in range(half):
             out, slot = (other_ref, h) if h < half - MOVED else (mine_ref, h + MOVED)
-            out[i, slot, :WINDOW] = kv_ref[i, sel_ref[0] * half + h]
-            out[i, slot, WINDOW:] = tail
-            mine_ref[i, h, :WINDOW] = kv_ref[i, sel_ref[1] * half + h]
-            mine_ref[i, h, WINDOW:] = tail
+            out[halo_rows(out, i, slot)] = kv_ref[i, sel_ref[0] * half + h]
+            mine_ref[halo_rows(mine_ref, i, h)] = kv_ref[i, sel_ref[1] * half + h]
     for copy in copies[3:]:
         copy.wait()
 
@@ -231,15 +231,20 @@
     return pieces
 
 
+def halo_rows(ref, i, slot):
+    heads = (ref.shape[0] - PAD) // (2 * WINDOW)
+    return slice((i * heads + slot) * WINDOW, (i * heads + slot + 1) * WINDOW)
+
+
 def halo_keys(halo_ref, rest_ref, slot, head, chunk):
     return [
-        jnp.concatenate([halo_ref[i, slot, chunk * CHUNK :WINDOW], rest_ref[i, head, : (chunk + 1) * CHUNK]], 0)
+        jnp.concatenate([halo_ref[halo_rows(halo_ref, i, slot)][chunk * CHUNK :], rest_ref[i, head, : (chunk + 1) * CHUNK]], 0)
         for i in range(2)
     ]
 
 
 def early_lows(sel_ref, docs_ref, low_ref, halo_ref, group, mixed):
-    ahead = jnp.where(sel_ref[2] == 0, -1.0, halo_ref[0, 0, WINDOW:].astype(F32)).T
+    ahead = jnp.where(sel_ref[2] == 0, -1.0, halo_ref[halo_ref.shape[0] - PAD :].astype(F32)).T
     counts = []
     for c in range(2):
         docs = docs_ref[c : c + 1, :].astype(F32)
@@ -298,7 +303,7 @@
     sel_ref, docs_ref, low_ref, q_ref, do_ref, rest_ref, tail_ref, halo_ref, own_early_ref, own_late_ref, early_ref, late_ref,
     dq_ref, buf, sem, *, chunks, group
 ):
-    half = halo_ref.shape[1] - MOVED
+    half = rest_ref.shape[1] // 2
     rows = half * group
     size = q_ref.shape[-1]
     early = own_early_ref.shape[0]
@@ -432,7 +437,7 @@
     docs = doc_ids.reshape(chunks, CHUNK)
 
     def halo_shape(heads):
-        return shape((2, heads, WINDOW + PAD, size), BF16)
+        return shape((2 * heads * WINDOW + PAD, size), BF16)
 
     early_chunks, late_chunks = (0, 1), tuple(range(2, chunks))
 

time: 42.6 us -> 42.6 us (level)
  the two profiles are of different devices: /device:TPU:10 before, /device:TPU:8 now
where the time goes in v8:
time: 42.6 us; the launch traced here: 42.4 us
  Pallas kernels  21.3 us (50%)
  starting transfers between devices  14.9 us (35%)
  waiting for transfers between devices  5.06 us (12%)
  between operations  0.93 us (2%)
    pallas_call x8, Pallas kernels, call(): pl.pallas_call(body, in_specs=specs, out_specs=out_specs, out_shape=out_s...  21.3 us
    ppermute x4, starting transfers between devices, shift(): lax.ppermute(block, axis, [(i - distance, i) for i in devices if i - dist...  11.2 us
    ppermute x3, waiting for transfers between devices, swap(): return lax.ppermute(block, 'head', [(0, 1), (1, 0)])  4.96 us
    ppermute x3, starting transfers between devices, swap(): return lax.ppermute(block, 'head', [(0, 1), (1, 0)])  3.71 us
  transfers between devices with their start and end apart: 7, of which 2 were waited for; matrix products, arithmetic and copies ran while one was open for 0% of the time, Pallas kernels for 42%

profile of v8, /device:TPU:8, one launch (start us, length us, event | category | flops | bytes accessed | tf_op | source)
XLA Modules:
  0.0 42.4 jit_solution(12172538780873007609)
XLA Ops:
  0.6 0.1 pad_add_fusion.sel_ref
  0.7 0.0 copy-start
  0.7 0.0 copy-start.1
  0.7 0.0 copy-start.2
  0.7 2.6 %shard_map.81 = (bf16[2,8,256,128]{3,2,1,0:T(8,128)(2,1)S(1)}, bf16[1544,128]{1,0:T(8,128)(2,1)S(1)}, bf16[2568,128]{1,0:T(8,128)(2,1)S(1)}, bf16[2,256,8,128]{3...) custom-call(s32[3]{0:T(128)S(1)} %pad_add_fusion.sel_ref, bf16[512,8,128]{2,1,0:T(8,128)(2,1)} %key_ref.1, ...), custom_call_target="tpu_custom_call" | custom-call | tf_op jit(solution)/shard_map/pallas_call | solution.py:455
  3.3 1.9 %collective-permute-start.2 = (bf16[1544,128]{1,0:T(8,128)(2,1)S(1)}, bf16[1544,128]{1,0:T(8,128)(2,1)S(1)}, u32[]{:S(2)}, u32[]{:S(2)}) collective-permute-start(bf16[1544,128]{1,0:T(8,128)(2,1)S(1)} %get-tuple-element.52), channel_id=1, source_target_pairs={{0,2},{2,4},{4,6},{6,8},{8,10},{10,12},{12,14},{14,16},{16,18},{18... | collective-permute-start | bytes 1185800 | tf_op jit(solution)/shard_map/ppermute | solution.py:414
  5.2 1.6 %collective-permute-start.1 = (bf16[2,512,1,2,128]{4,3,2,1,0:T(2,128)(2,1)S(1)}, bf16[2,512,1,2,128]{4,3,2,1,0:T(2,128)(2,1)S(1)}, u32[]{:S(2)}, u32[]{:S(2)}) collective-permute-start(bf16[2,512,1,2,128]{4,3,2,1,0:T(2,128)(2,1)S(1)} %get-tuple-element.49), channel_id=1, source_target_pairs={{0,1},{1,0},{2,3},{3,2},{4,5},{5,4},{6,7},{7,6},{8,9},{9,8},{10,11... | collective-permute-start | bytes 1572872 | tf_op jit(solution)/shard_map/ppermute | solution.py:418
  6.8 3.2 %collective-permute-start = (bf16[2568,128]{1,0:T(8,128)(2,1)S(1)}, bf16[2568,128]{1,0:T(8,128)(2,1)S(1)}, u32[]{:S(2)}, u32[]{:S(2)}) collective-permute-start(bf16[2568,128]{1,0:T(8,128)(2,1)S(1)} %get-tuple-element.48), channel_id=1, source_target_pairs={{0,2},{2,4},{4,6},{6,8},{8,10},{10,12},{12,14},{14,16},{16,18},{18... | collective-permute-start | bytes 1972232 | tf_op jit(solution)/shard_map/ppermute | solution.py:414
  10.0 0.0 copy-done
  10.0 0.0 copy-done.1
  10.0 0.0 copy-done.2
  10.0 3.2 %shard_map.82 = (bf16[2,6,128,128]{3,2,1,0:T(8,128)(2,1)S(1)}, f32[2,3,512,128]{3,2,1,0:T(8,128)S(1)}, bf16[2,8,256,128]{3,2,1,0:T(8,128)(2,1)S(1)}, s32[2,4,256]{2,1,0:T(4,128)S(1)}) custom-call(s32[3]{0:T(128)S(1)} %pad_add_fusion.sel_ref, s32[4,128]{1,0:T(4,128)S(1)} %bitcast.19, bf16[2,256,8,128]{3,2,1,0:T(8,128)(2,1)S(1)} %get-tuple-element.44.raw_ref, ...), custom_call_target="tpu_custom_call" | custom-call | flops 10066329600 | bytes 2097152 | tf_op jit(solution)/shard_map/pallas_call | solution.py:455
  13.2 0.1 collective-permute-done.2.halo_ref
  13.3 2.8 %shard_map.85 = (bf16[2,6,128,128]{3,2,1,0:T(8,128)(2,1)S(1)}, bf16[2,3,256,128]{3,2,1,0:T(8,128)(2,1)S(1)}, bf16[2,3,256,128]{3,2,1,0:T(8,128)(2,1)S(1)}) custom-call(s32[3]{0:T(128)S(1)} %pad_add_fusion.sel_ref, s32[4,128]{1,0:T(4,128)S(1)} %bitcast.20, s32[2,4,256]{2,1,0:T(4,128)S(1)} %get-tuple-element.46.low_ref, bf16[512,16,128]{2,1,0:T(8,128)(2,1)S(1)} %bitcast.9, ...), custom_call_target="tpu_custom_call" | custom-call | flops 10066329600 | bytes 2097152 | tf_op jit(solution)/shard_map/pallas_call | solution.py:455
  16.1 3.3 %collective-permute-start.3 = (bf16[2,3,256,128]{3,2,1,0:T(8,128)(2,1)S(1)}, bf16[2,3,256,128]{3,2,1,0:T(8,128)(2,1)S(1)}, u32[]{:S(2)}, u32[]{:S(2)}) collective-permute-start(bf16[2,3,256,128]{3,2,1,0:T(8,128)(2,1)S(1)} %get-tuple-element.57), channel_id=1, source_target_pairs={{2,0},{4,2},{6,4},{8,6},{10,8},{12,10},{14,12},{16,14},{18,16},{20... | collective-permute-start | bytes 1179656 | tf_op jit(solution)/shard_map/ppermute | solution.py:414
  19.4 0.6 %collective-permute-start.6 = (bf16[2,3,256,128]{3,2,1,0:T(8,128)(2,1)S(1)}, bf16[2,3,256,128]{3,2,1,0:T(8,128)(2,1)S(1)}, u32[]{:S(2)}, u32[]{:S(2)}) collective-permute-start(bf16[2,3,256,128]{3,2,1,0:T(8,128)(2,1)S(1)} %get-tuple-element.60), channel_id=1, source_target_pairs={{0,1},{1,0},{2,3},{3,2},{4,5},{5,4},{6,7},{7,6},{8,9},{9,8},{10,11... | collective-permute-start | bytes 1179656 | tf_op jit(solution)/shard_map/ppermute | solution.py:418
  20.1 0.0 collective-permute-done.1
  20.1 3.7 %shard_map.84 = (bf16[2,128,8,128]{3,2,1,0:T(8,128)(2,1)S(1)}, f32[2,4,512,128]{3,2,1,0:T(8,128)S(1)}) custom-call(s32[3]{0:T(128)S(1)} %pad_add_fusion.sel_ref, s32[2,4,256]{2,1,0:T(4,128)S(1)} %get-tuple-element.46.low_ref, bf16[512,16,128]{2,1,0:T(8,128)(2,1)S(1)} %bitcast.10, bf16[512,16,128]{2,1,0:T(8,128)(2,1)S(1)} %bitcast.15, ...), custom_call_target="tpu_custom_call" | custom-call | flops 10066329600 | bytes 2097152 | tf_op jit(solution)/shard_map/pallas_call | solution.py:455
  23.7 0.0 collective-permute-done.halo_ref
  23.8 3.8 %shard_map.83 = (bf16[2,128,8,128]{3,2,1,0:T(8,128)(2,1)S(1)}, f32[2,4,256,128]{3,2,1,0:T(8,128)S(1)}, bf16[2,4,256,128]{3,2,1,0:T(8,128)(2,1)S(1)}) custom-call(s32[3]{0:T(128)S(1)} %pad_add_fusion.sel_ref, s32[4,128]{1,0:T(4,128)S(1)} %bitcast.21, s32[2,4,256]{2,1,0:T(4,128)S(1)} %get-tuple-element.46.low_ref, bf16[512,16,128]{2,1,0:T(8,128)(2,1)S(1)} %bitcast.11, ...), custom_call_target="tpu_custom_call" | custom-call | flops 10066329600 | bytes 2097152 | tf_op jit(solution)/shard_map/pallas_call | solution.py:455
  27.6 2.8 %collective-permute-start.5 = (bf16[2,4,256,128]{3,2,1,0:T(8,128)(2,1)S(1)}, bf16[2,4,256,128]{3,2,1,0:T(8,128)(2,1)S(1)}, u32[]{:S(2)}, u32[]{:S(2)}) collective-permute-start(bf16[2,4,256,128]{3,2,1,0:T(8,128)(2,1)S(1)} %get-tuple-element.58), channel_id=1, source_target_pairs={{2,0},{4,2},{6,4},{8,6},{10,8},{12,10},{14,12},{16,14},{18,16},{20... | collective-permute-start | bytes 1572872 | tf_op jit(solution)/shard_map/ppermute | solution.py:414
  30.3 0.0 collective-permute-done.3
  30.3 0.1 add_convert_fusion
  30.4 1.6 %collective-permute-start.4 = (bf16[2,3,256,128]{3,2,1,0:T(8,128)(2,1)S(1)}, bf16[2,3,256,128]{3,2,1,0:T(8,128)(2,1)S(1)}, u32[]{:S(2)}, u32[]{:S(2)}) collective-permute-start(bf16[2,3,256,128]{3,2,1,0:T(8,128)(2,1)S(1)} %add_convert_fusion), channel_id=1, source_target_pairs={{0,1},{1,0},{2,3},{3,2},{4,5},{5,4},{6,7},{7,6},{8,9},{9,8},{10,11... | collective-permute-start | bytes 1179656 | tf_op jit(solution)/shard_map/ppermute | solution.py:418
  32.0 3.1 %shard_map.86 = bf16[512,16,128]{2,1,0:T(8,128)(2,1)} custom-call(s32[3]{0:T(128)S(1)} %pad_add_fusion.sel_ref, s32[4,128]{1,0:T(4,128)S(1)} %bitcast.22, s32[2,4,256]{2,1,0:T(4,128)S(1)} %get-tuple-element.46.low_ref, bf16[512,16,128]{2,1,0:T(8,128)(2,1)S(1)} %bitcast.12, bf16[512,16,128]{2,1,0:T(8,128)(2,1)S(1)} %bitcast.17, ...), custom_call_target="tpu_custom_call" | custom-call | flops 5033164800 | bytes 1048576 | tf_op jit(solution)/shard_map/pallas_call | solution.py:455
  35.1 0.0 collective-permute-done.6.first_in
  35.1 1.1 %shard_map.87 = (bf16[512,4,128]{2,1,0:T(4,128)(2,1)}, bf16[512,4,128]{2,1,0:T(4,128)(2,1)}) custom-call(f32[2,4,256,128]{3,2,1,0:T(8,128)S(1)} %get-tuple-element.59.early_ref, bf16[2,3,256,128]{3,2,1,0:T(8,128)(2,1)S(1)} %collective-permute-done.6.first_in, f32[2,4,512,128]{3,2,1,0:T(8,128)S(1)} %get-tuple-element.56.part_ref), custom_call_target="tpu_custom_call" | custom-call | tf_op jit(solution)/shard_map/pallas_call | solution.py:455
  36.2 5.0 %collective-permute-done.4.last_in = bf16[2,3,256,128]{3,2,1,0:T(8,128)(2,1)S(1)} collective-permute-done((bf16[2,3,256,128]{3,2,1,0:T(8,128)(2,1)S(1)}, bf16[2,3,256,128]{3,2,1,0:T(8,128)(2,1)S(1)}, u32[]{:S(2)}, u32[]{:S(2)}) %collective-permute-start.4) | collective-permute-done | bytes 393248 | tf_op jit(solution)/shard_map/ppermute | solution.py:418
  41.2 0.0 collective-permute-done.5.back_in
  41.2 1.1 %shard_map.88 = (bf16[512,4,128]{2,1,0:T(4,128)(2,1)}, bf16[512,4,128]{2,1,0:T(4,128)(2,1)}) custom-call(f32[2,4,512,128]{3,2,1,0:T(8,128)S(1)} %get-tuple-element.56.part_ref, bf16[2,3,256,128]{3,2,1,0:T(8,128)(2,1)S(1)} %collective-permute-done.4.last_in, ...), custom_call_target="tpu_custom_call", output_to_operand_aliasing={{0}: (3, {}), {1}: (4, {})} | custom-call | tf_op jit(solution)/shard_map/pallas_call | solution.py:455
Async XLA Ops:
  0.7 9.3 %copy-start = (bf16[512,8,2,128]{3,2,1,0:T(2,128)(2,1)S(1)}, bf16[512,8,2,128]{3,2,1,0:T(2,128)(2,1)}, u32[]{:S(2)}) copy-start(bf16[512,8,2,128]{3,2,1,0:T(2,128)(2,1)} %q_ref.1) | copy-start | bytes 6291460
  0.7 9.3 %copy-start.1 = (bf16[512,8,2,128]{3,2,1,0:T(2,128)(2,1)S(1)}, bf16[512,8,2,128]{3,2,1,0:T(2,128)(2,1)}, u32[]{:S(2)}) copy-start(bf16[512,8,2,128]{3,2,1,0:T(2,128)(2,1)} %do_ref.1) | copy-start | bytes 6291460
  0.7 9.3 %copy-start.2 = (s32[512]{0:T(512)S(1)}, s32[512]{0:T(512)}, u32[]{:S(2)}) copy-start(s32[512]{0:T(512)} %param.13) | copy-start | bytes 6148
  3.3 10.0 %collective-permute-start.2 = (bf16[1544,128]{1,0:T(8,128)(2,1)S(1)}, bf16[1544,128]{1,0:T(8,128)(2,1)S(1)}, u32[]{:S(2)}, u32[]{:S(2)}) collective-permute-start(bf16[1544,128]{1,0:T(8,128)(2,1)S(1)} %get-tuple-element.52), channel_id=1, source_target_pairs={{0,2},{2,4},{4,6},{6,8},{8,10},{10,12},{12,14},{14,16},{16,18},{18... | collective-permute-start | bytes 1185800 | tf_op jit(solution)/shard_map/ppermute | solution.py:414
  5.2 14.8 %collective-permute-start.1 = (bf16[2,512,1,2,128]{4,3,2,1,0:T(2,128)(2,1)S(1)}, bf16[2,512,1,2,128]{4,3,2,1,0:T(2,128)(2,1)S(1)}, u32[]{:S(2)}, u32[]{:S(2)}) collective-permute-start(bf16[2,512,1,2,128]{4,3,2,1,0:T(2,128)(2,1)S(1)} %get-tuple-element.49), channel_id=1, source_target_pairs={{0,1},{1,0},{2,3},{3,2},{4,5},{5,4},{6,7},{7,6},{8,9},{9,8},{10,11... | collective-permute-start | bytes 1572872 | tf_op jit(solution)/shard_map/ppermute | solution.py:418
  6.8 17.0 %collective-permute-start = (bf16[2568,128]{1,0:T(8,128)(2,1)S(1)}, bf16[2568,128]{1,0:T(8,128)(2,1)S(1)}, u32[]{:S(2)}, u32[]{:S(2)}) collective-permute-start(bf16[2568,128]{1,0:T(8,128)(2,1)S(1)} %get-tuple-element.48), channel_id=1, source_target_pairs={{0,2},{2,4},{4,6},{6,8},{8,10},{10,12},{12,14},{14,16},{16,18},{18... | collective-permute-start | bytes 1972232 | tf_op jit(solution)/shard_map/ppermute | solution.py:414
  16.1 14.2 %collective-permute-start.3 = (bf16[2,3,256,128]{3,2,1,0:T(8,128)(2,1)S(1)}, bf16[2,3,256,128]{3,2,1,0:T(8,128)(2,1)S(1)}, u32[]{:S(2)}, u32[]{:S(2)}) collective-permute-start(bf16[2,3,256,128]{3,2,1,0:T(8,128)(2,1)S(1)} %get-tuple-element.57), channel_id=1, source_target_pairs={{2,0},{4,2},{6,4},{8,6},{10,8},{12,10},{14,12},{16,14},{18,16},{20... | collective-permute-start | bytes 1179656 | tf_op jit(solution)/shard_map/ppermute | solution.py:414
  19.4 15.7 %collective-permute-start.6 = (bf16[2,3,256,128]{3,2,1,0:T(8,128)(2,1)S(1)}, bf16[2,3,256,128]{3,2,1,0:T(8,128)(2,1)S(1)}, u32[]{:S(2)}, u32[]{:S(2)}) collective-permute-start(bf16[2,3,256,128]{3,2,1,0:T(8,128)(2,1)S(1)} %get-tuple-element.60), channel_id=1, source_target_pairs={{0,1},{1,0},{2,3},{3,2},{4,5},{5,4},{6,7},{7,6},{8,9},{9,8},{10,11... | collective-permute-start | bytes 1179656 | tf_op jit(solution)/shard_map/ppermute | solution.py:418
  27.6 13.6 %collective-permute-start.5 = (bf16[2,4,256,128]{3,2,1,0:T(8,128)(2,1)S(1)}, bf16[2,4,256,128]{3,2,1,0:T(8,128)(2,1)S(1)}, u32[]{:S(2)}, u32[]{:S(2)}) collective-permute-start(bf16[2,4,256,128]{3,2,1,0:T(8,128)(2,1)S(1)} %get-tuple-element.58), channel_id=1, source_target_pairs={{2,0},{4,2},{6,4},{8,6},{10,8},{12,10},{14,12},{16,14},{18,16},{20... | collective-permute-start | bytes 1572872 | tf_op jit(solution)/shard_map/ppermute | solution.py:414
  30.4 10.7 %collective-permute-start.4 = (bf16[2,3,256,128]{3,2,1,0:T(8,128)(2,1)S(1)}, bf16[2,3,256,128]{3,2,1,0:T(8,128)(2,1)S(1)}, u32[]{:S(2)}, u32[]{:S(2)}) collective-permute-start(bf16[2,3,256,128]{3,2,1,0:T(8,128)(2,1)S(1)} %add_convert_fusion), channel_id=1, source_target_pairs={{0,1},{1,0},{2,3},{3,2},{4,5},{5,4},{6,7},{7,6},{8,9},{9,8},{10,11... | collective-permute-start | bytes 1179656 | tf_op jit(solution)/shard_map/ppermute | solution.py:418

commit v9 on v8

--- a/solution.py
+++ b/solution.py
@@ -395,6 +395,11 @@
 def finish_kernel(part_ref, last_in, back_in, dk_in, dv_in, dk_ref, dv_ref, buf, sem):
     late = part_ref.shape[2] - WINDOW
     shared = last_in.shape[1]
+
+    def piece(i, out, n):
+        rows = pl.ds(n * CHUNK, CHUNK)
+        return pltpu.make_async_copy(buf.at[i, rows], out.at[pl.ds(WINDOW + n * CHUNK, CHUNK)], sem.at[i, n])
+
     for i, out in ((0, dk_ref), (1, dv_ref)):
         for r in range(0, late, STEP):
             rows = slice(r, r + STEP)
@@ -404,9 +409,11 @@
                 value = value + back_in[i, :, r - skip : r - skip + STEP].astype(F32)
             value = jnp.concatenate([value[:shared] + last_in[i, :, rows].astype(F32), value[shared:]], 0)
             buf[i, rows] = jnp.transpose(value.astype(BF16), (1, 0, 2))
-        out_rows(buf, sem, i, out, pl.ds(WINDOW, late)).start()
+            if (r + STEP) % CHUNK == 0:
+                piece(i, out, r // CHUNK).start()
     for i, out in ((0, dk_ref), (1, dv_ref)):
-        out_rows(buf, sem, i, out, pl.ds(WINDOW, late)).wait()
+        for n in range(late // CHUNK):
+            piece(i, out, n).wait()
 
 
 def shift(block, axis, distance):
@@ -553,7 +560,7 @@
         [VMEM] * 3 + [ANY] * 2,
         [ANY, ANY],
         [out, out],
-        [pltpu.VMEM((2, rest, half, size), BF16), dma((2,))],
+        [pltpu.VMEM((2, rest, half, size), BF16), dma((2, rest // CHUNK))],
         8,
         aliases={3: 0, 4: 1},
     )

time: 42.6 us -> 42.6 us (level)
  no operation moved by 1% of the time
where the time goes in v9:
time: 42.6 us; the launch traced here: 42.4 us
  Pallas kernels  21.3 us (50%)
  starting transfers between devices  14.9 us (35%)
  waiting for transfers between devices  5.06 us (12%)
  between operations  0.93 us (2%)
    pallas_call x8, Pallas kernels, call(): pl.pallas_call(body, in_specs=specs, out_specs=out_specs, out_shape=out_s...  21.3 us
    ppermute x4, starting transfers between devices, shift(): lax.ppermute(block, axis, [(i - distance, i) for i in devices if i - dist...  11.2 us
    ppermute x3, waiting for transfers between devices, swap(): return lax.ppermute(block, 'head', [(0, 1), (1, 0)])  4.96 us
    ppermute x3, starting transfers between devices, swap(): return lax.ppermute(block, 'head', [(0, 1), (1, 0)])  3.71 us
  transfers between devices with their start and end apart: 7, of which 2 were waited for; matrix products, arithmetic and copies ran while one was open for 0% of the time, Pallas kernels for 42%

profile of v9, /device:TPU:8, one launch (start us, length us, event | category | flops | bytes accessed | tf_op | source)
XLA Modules:
  0.0 42.4 jit_solution(6285345490050743659)
XLA Ops:
  0.6 0.1 pad_add_fusion.sel_ref
  0.7 0.0 copy-start
  0.7 0.0 copy-start.1
  0.7 0.0 copy-start.2
  0.7 2.6 %shard_map.81 = (bf16[2,8,256,128]{3,2,1,0:T(8,128)(2,1)S(1)}, bf16[1544,128]{1,0:T(8,128)(2,1)S(1)}, bf16[2568,128]{1,0:T(8,128)(2,1)S(1)}, bf16[2,256,8,128]{3...) custom-call(s32[3]{0:T(128)S(1)} %pad_add_fusion.sel_ref, bf16[512,8,128]{2,1,0:T(8,128)(2,1)} %key_ref.1, ...), custom_call_target="tpu_custom_call" | custom-call | tf_op jit(solution)/shard_map/pallas_call | solution.py:462
  3.3 1.9 %collective-permute-start.2 = (bf16[1544,128]{1,0:T(8,128)(2,1)S(1)}, bf16[1544,128]{1,0:T(8,128)(2,1)S(1)}, u32[]{:S(2)}, u32[]{:S(2)}) collective-permute-start(bf16[1544,128]{1,0:T(8,128)(2,1)S(1)} %get-tuple-element.52), channel_id=1, source_target_pairs={{0,2},{2,4},{4,6},{6,8},{8,10},{10,12},{12,14},{14,16},{16,18},{18... | collective-permute-start | bytes 1185800 | tf_op jit(solution)/shard_map/ppermute | solution.py:421
  5.2 1.6 %collective-permute-start.1 = (bf16[2,512,1,2,128]{4,3,2,1,0:T(2,128)(2,1)S(1)}, bf16[2,512,1,2,128]{4,3,2,1,0:T(2,128)(2,1)S(1)}, u32[]{:S(2)}, u32[]{:S(2)}) collective-permute-start(bf16[2,512,1,2,128]{4,3,2,1,0:T(2,128)(2,1)S(1)} %get-tuple-element.49), channel_id=1, source_target_pairs={{0,1},{1,0},{2,3},{3,2},{4,5},{5,4},{6,7},{7,6},{8,9},{9,8},{10,11... | collective-permute-start | bytes 1572872 | tf_op jit(solution)/shard_map/ppermute | solution.py:425
  6.8 3.2 %collective-permute-start = (bf16[2568,128]{1,0:T(8,128)(2,1)S(1)}, bf16[2568,128]{1,0:T(8,128)(2,1)S(1)}, u32[]{:S(2)}, u32[]{:S(2)}) collective-permute-start(bf16[2568,128]{1,0:T(8,128)(2,1)S(1)} %get-tuple-element.48), channel_id=1, source_target_pairs={{0,2},{2,4},{4,6},{6,8},{8,10},{10,12},{12,14},{14,16},{16,18},{18... | collective-permute-start | bytes 1972232 | tf_op jit(solution)/shard_map/ppermute | solution.py:421
  10.0 0.0 copy-done
  10.0 0.0 copy-done.1
  10.0 0.0 copy-done.2
  10.0 3.2 %shard_map.82 = (bf16[2,6,128,128]{3,2,1,0:T(8,128)(2,1)S(1)}, f32[2,3,512,128]{3,2,1,0:T(8,128)S(1)}, bf16[2,8,256,128]{3,2,1,0:T(8,128)(2,1)S(1)}, s32[2,4,256]{2,1,0:T(4,128)S(1)}) custom-call(s32[3]{0:T(128)S(1)} %pad_add_fusion.sel_ref, s32[4,128]{1,0:T(4,128)S(1)} %bitcast.19, bf16[2,256,8,128]{3,2,1,0:T(8,128)(2,1)S(1)} %get-tuple-element.44.raw_ref, ...), custom_call_target="tpu_custom_call" | custom-call | flops 10066329600 | bytes 2097152 | tf_op jit(solution)/shard_map/pallas_call | solution.py:462
  13.2 0.1 collective-permute-done.2.halo_ref
  13.3 2.8 %shard_map.85 = (bf16[2,6,128,128]{3,2,1,0:T(8,128)(2,1)S(1)}, bf16[2,3,256,128]{3,2,1,0:T(8,128)(2,1)S(1)}, bf16[2,3,256,128]{3,2,1,0:T(8,128)(2,1)S(1)}) custom-call(s32[3]{0:T(128)S(1)} %pad_add_fusion.sel_ref, s32[4,128]{1,0:T(4,128)S(1)} %bitcast.20, s32[2,4,256]{2,1,0:T(4,128)S(1)} %get-tuple-element.46.low_ref, bf16[512,16,128]{2,1,0:T(8,128)(2,1)S(1)} %bitcast.9, ...), custom_call_target="tpu_custom_call" | custom-call | flops 10066329600 | bytes 2097152 | tf_op jit(solution)/shard_map/pallas_call | solution.py:462
  16.1 3.3 %collective-permute-start.3 = (bf16[2,3,256,128]{3,2,1,0:T(8,128)(2,1)S(1)}, bf16[2,3,256,128]{3,2,1,0:T(8,128)(2,1)S(1)}, u32[]{:S(2)}, u32[]{:S(2)}) collective-permute-start(bf16[2,3,256,128]{3,2,1,0:T(8,128)(2,1)S(1)} %get-tuple-element.57), channel_id=1, source_target_pairs={{2,0},{4,2},{6,4},{8,6},{10,8},{12,10},{14,12},{16,14},{18,16},{20... | collective-permute-start | bytes 1179656 | tf_op jit(solution)/shard_map/ppermute | solution.py:421
  19.4 0.6 %collective-permute-start.6 = (bf16[2,3,256,128]{3,2,1,0:T(8,128)(2,1)S(1)}, bf16[2,3,256,128]{3,2,1,0:T(8,128)(2,1)S(1)}, u32[]{:S(2)}, u32[]{:S(2)}) collective-permute-start(bf16[2,3,256,128]{3,2,1,0:T(8,128)(2,1)S(1)} %get-tuple-element.60), channel_id=1, source_target_pairs={{0,1},{1,0},{2,3},{3,2},{4,5},{5,4},{6,7},{7,6},{8,9},{9,8},{10,11... | collective-permute-start | bytes 1179656 | tf_op jit(solution)/shard_map/ppermute | solution.py:425
  20.1 0.0 collective-permute-done.1
  20.1 3.7 %shard_map.84 = (bf16[2,128,8,128]{3,2,1,0:T(8,128)(2,1)S(1)}, f32[2,4,512,128]{3,2,1,0:T(8,128)S(1)}) custom-call(s32[3]{0:T(128)S(1)} %pad_add_fusion.sel_ref, s32[2,4,256]{2,1,0:T(4,128)S(1)} %get-tuple-element.46.low_ref, bf16[512,16,128]{2,1,0:T(8,128)(2,1)S(1)} %bitcast.10, bf16[512,16,128]{2,1,0:T(8,128)(2,1)S(1)} %bitcast.15, ...), custom_call_target="tpu_custom_call" | custom-call | flops 10066329600 | bytes 2097152 | tf_op jit(solution)/shard_map/pallas_call | solution.py:462
  23.7 0.0 collective-permute-done.halo_ref
  23.8 3.8 %shard_map.83 = (bf16[2,128,8,128]{3,2,1,0:T(8,128)(2,1)S(1)}, f32[2,4,256,128]{3,2,1,0:T(8,128)S(1)}, bf16[2,4,256,128]{3,2,1,0:T(8,128)(2,1)S(1)}) custom-call(s32[3]{0:T(128)S(1)} %pad_add_fusion.sel_ref, s32[4,128]{1,0:T(4,128)S(1)} %bitcast.21, s32[2,4,256]{2,1,0:T(4,128)S(1)} %get-tuple-element.46.low_ref, bf16[512,16,128]{2,1,0:T(8,128)(2,1)S(1)} %bitcast.11, ...), custom_call_target="tpu_custom_call" | custom-call | flops 10066329600 | bytes 2097152 | tf_op jit(solution)/shard_map/pallas_call | solution.py:462
  27.6 2.8 %collective-permute-start.5 = (bf16[2,4,256,128]{3,2,1,0:T(8,128)(2,1)S(1)}, bf16[2,4,256,128]{3,2,1,0:T(8,128)(2,1)S(1)}, u32[]{:S(2)}, u32[]{:S(2)}) collective-permute-start(bf16[2,4,256,128]{3,2,1,0:T(8,128)(2,1)S(1)} %get-tuple-element.58), channel_id=1, source_target_pairs={{2,0},{4,2},{6,4},{8,6},{10,8},{12,10},{14,12},{16,14},{18,16},{20... | collective-permute-start | bytes 1572872 | tf_op jit(solution)/shard_map/ppermute | solution.py:421
  30.3 0.0 collective-permute-done.3
  30.3 0.1 add_convert_fusion
  30.4 1.6 %collective-permute-start.4 = (bf16[2,3,256,128]{3,2,1,0:T(8,128)(2,1)S(1)}, bf16[2,3,256,128]{3,2,1,0:T(8,128)(2,1)S(1)}, u32[]{:S(2)}, u32[]{:S(2)}) collective-permute-start(bf16[2,3,256,128]{3,2,1,0:T(8,128)(2,1)S(1)} %add_convert_fusion), channel_id=1, source_target_pairs={{0,1},{1,0},{2,3},{3,2},{4,5},{5,4},{6,7},{7,6},{8,9},{9,8},{10,11... | collective-permute-start | bytes 1179656 | tf_op jit(solution)/shard_map/ppermute | solution.py:425
  32.0 3.1 %shard_map.86 = bf16[512,16,128]{2,1,0:T(8,128)(2,1)} custom-call(s32[3]{0:T(128)S(1)} %pad_add_fusion.sel_ref, s32[4,128]{1,0:T(4,128)S(1)} %bitcast.22, s32[2,4,256]{2,1,0:T(4,128)S(1)} %get-tuple-element.46.low_ref, bf16[512,16,128]{2,1,0:T(8,128)(2,1)S(1)} %bitcast.12, bf16[512,16,128]{2,1,0:T(8,128)(2,1)S(1)} %bitcast.17, ...), custom_call_target="tpu_custom_call" | custom-call | flops 5033164800 | bytes 1048576 | tf_op jit(solution)/shard_map/pallas_call | solution.py:462
  35.1 0.0 collective-permute-done.6.first_in
  35.1 1.1 %shard_map.87 = (bf16[512,4,128]{2,1,0:T(4,128)(2,1)}, bf16[512,4,128]{2,1,0:T(4,128)(2,1)}) custom-call(f32[2,4,256,128]{3,2,1,0:T(8,128)S(1)} %get-tuple-element.59.early_ref, bf16[2,3,256,128]{3,2,1,0:T(8,128)(2,1)S(1)} %collective-permute-done.6.first_in, f32[2,4,512,128]{3,2,1,0:T(8,128)S(1)} %get-tuple-element.56.part_ref), custom_call_target="tpu_custom_call" | custom-call | tf_op jit(solution)/shard_map/pallas_call | solution.py:462
  36.2 5.0 %collective-permute-done.4.last_in = bf16[2,3,256,128]{3,2,1,0:T(8,128)(2,1)S(1)} collective-permute-done((bf16[2,3,256,128]{3,2,1,0:T(8,128)(2,1)S(1)}, bf16[2,3,256,128]{3,2,1,0:T(8,128)(2,1)S(1)}, u32[]{:S(2)}, u32[]{:S(2)}) %collective-permute-start.4) | collective-permute-done | bytes 393248 | tf_op jit(solution)/shard_map/ppermute | solution.py:425
  41.2 0.0 collective-permute-done.5.back_in
  41.2 1.0 %shard_map.88 = (bf16[512,4,128]{2,1,0:T(4,128)(2,1)}, bf16[512,4,128]{2,1,0:T(4,128)(2,1)}) custom-call(f32[2,4,512,128]{3,2,1,0:T(8,128)S(1)} %get-tuple-element.56.part_ref, bf16[2,3,256,128]{3,2,1,0:T(8,128)(2,1)S(1)} %collective-permute-done.4.last_in, ...), custom_call_target="tpu_custom_call", output_to_operand_aliasing={{0}: (3, {}), {1}: (4, {})} | custom-call | tf_op jit(solution)/shard_map/pallas_call | solution.py:462
Async XLA Ops:
  0.7 9.3 %copy-start = (bf16[512,8,2,128]{3,2,1,0:T(2,128)(2,1)S(1)}, bf16[512,8,2,128]{3,2,1,0:T(2,128)(2,1)}, u32[]{:S(2)}) copy-start(bf16[512,8,2,128]{3,2,1,0:T(2,128)(2,1)} %q_ref.1) | copy-start | bytes 6291460
  0.7 9.3 %copy-start.1 = (bf16[512,8,2,128]{3,2,1,0:T(2,128)(2,1)S(1)}, bf16[512,8,2,128]{3,2,1,0:T(2,128)(2,1)}, u32[]{:S(2)}) copy-start(bf16[512,8,2,128]{3,2,1,0:T(2,128)(2,1)} %do_ref.1) | copy-start | bytes 6291460
  0.7 9.3 %copy-start.2 = (s32[512]{0:T(512)S(1)}, s32[512]{0:T(512)}, u32[]{:S(2)}) copy-start(s32[512]{0:T(512)} %param.13) | copy-start | bytes 6148
  3.3 10.0 %collective-permute-start.2 = (bf16[1544,128]{1,0:T(8,128)(2,1)S(1)}, bf16[1544,128]{1,0:T(8,128)(2,1)S(1)}, u32[]{:S(2)}, u32[]{:S(2)}) collective-permute-start(bf16[1544,128]{1,0:T(8,128)(2,1)S(1)} %get-tuple-element.52), channel_id=1, source_target_pairs={{0,2},{2,4},{4,6},{6,8},{8,10},{10,12},{12,14},{14,16},{16,18},{18... | collective-permute-start | bytes 1185800 | tf_op jit(solution)/shard_map/ppermute | solution.py:421
  5.2 14.8 %collective-permute-start.1 = (bf16[2,512,1,2,128]{4,3,2,1,0:T(2,128)(2,1)S(1)}, bf16[2,512,1,2,128]{4,3,2,1,0:T(2,128)(2,1)S(1)}, u32[]{:S(2)}, u32[]{:S(2)}) collective-permute-start(bf16[2,512,1,2,128]{4,3,2,1,0:T(2,128)(2,1)S(1)} %get-tuple-element.49), channel_id=1, source_target_pairs={{0,1},{1,0},{2,3},{3,2},{4,5},{5,4},{6,7},{7,6},{8,9},{9,8},{10,11... | collective-permute-start | bytes 1572872 | tf_op jit(solution)/shard_map/ppermute | solution.py:425
  6.8 17.0 %collective-permute-start = (bf16[2568,128]{1,0:T(8,128)(2,1)S(1)}, bf16[2568,128]{1,0:T(8,128)(2,1)S(1)}, u32[]{:S(2)}, u32[]{:S(2)}) collective-permute-start(bf16[2568,128]{1,0:T(8,128)(2,1)S(1)} %get-tuple-element.48), channel_id=1, source_target_pairs={{0,2},{2,4},{4,6},{6,8},{8,10},{10,12},{12,14},{14,16},{16,18},{18... | collective-permute-start | bytes 1972232 | tf_op jit(solution)/shard_map/ppermute | solution.py:421
  16.1 14.2 %collective-permute-start.3 = (bf16[2,3,256,128]{3,2,1,0:T(8,128)(2,1)S(1)}, bf16[2,3,256,128]{3,2,1,0:T(8,128)(2,1)S(1)}, u32[]{:S(2)}, u32[]{:S(2)}) collective-permute-start(bf16[2,3,256,128]{3,2,1,0:T(8,128)(2,1)S(1)} %get-tuple-element.57), channel_id=1, source_target_pairs={{2,0},{4,2},{6,4},{8,6},{10,8},{12,10},{14,12},{16,14},{18,16},{20... | collective-permute-start | bytes 1179656 | tf_op jit(solution)/shard_map/ppermute | solution.py:421
  19.4 15.7 %collective-permute-start.6 = (bf16[2,3,256,128]{3,2,1,0:T(8,128)(2,1)S(1)}, bf16[2,3,256,128]{3,2,1,0:T(8,128)(2,1)S(1)}, u32[]{:S(2)}, u32[]{:S(2)}) collective-permute-start(bf16[2,3,256,128]{3,2,1,0:T(8,128)(2,1)S(1)} %get-tuple-element.60), channel_id=1, source_target_pairs={{0,1},{1,0},{2,3},{3,2},{4,5},{5,4},{6,7},{7,6},{8,9},{9,8},{10,11... | collective-permute-start | bytes 1179656 | tf_op jit(solution)/shard_map/ppermute | solution.py:425
  27.6 13.6 %collective-permute-start.5 = (bf16[2,4,256,128]{3,2,1,0:T(8,128)(2,1)S(1)}, bf16[2,4,256,128]{3,2,1,0:T(8,128)(2,1)S(1)}, u32[]{:S(2)}, u32[]{:S(2)}) collective-permute-start(bf16[2,4,256,128]{3,2,1,0:T(8,128)(2,1)S(1)} %get-tuple-element.58), channel_id=1, source_target_pairs={{2,0},{4,2},{6,4},{8,6},{10,8},{12,10},{14,12},{16,14},{18,16},{20... | collective-permute-start | bytes 1572872 | tf_op jit(solution)/shard_map/ppermute | solution.py:421
  30.4 10.7 %collective-permute-start.4 = (bf16[2,3,256,128]{3,2,1,0:T(8,128)(2,1)S(1)}, bf16[2,3,256,128]{3,2,1,0:T(8,128)(2,1)S(1)}, u32[]{:S(2)}, u32[]{:S(2)}) collective-permute-start(bf16[2,3,256,128]{3,2,1,0:T(8,128)(2,1)S(1)} %add_convert_fusion), channel_id=1, source_target_pairs={{0,1},{1,0},{2,3},{3,2},{4,5},{5,4},{6,7},{7,6},{8,9},{9,8},{10,11... | collective-permute-start | bytes 1179656 | tf_op jit(solution)/shard_map/ppermute | solution.py:425
